TPU v7x, 32 devices: a whole 2x2x4 slice. The times are simulated.
32 devices in a mesh: dp: 8 (over z, y), tensor: 4 (over x, core).
Axes of the slice: x: 2, y: 2, z: 4, core: 2. Of those that a mesh axis runs over, the one named last changes fastest.
Arguments:
- block_input: bfloat16 [20480, 1024], P(('dp', 'tensor')), may hold values from -6 to 6
- norm_gains: float32 [2, 1024], P(None, 'dp'), may hold values from 0.1 to 1.9
- qkv_weight: float32 [3, 1024, 1024], P(None, 'dp', 'tensor'), may hold values from -0.1875 to 0.1875
- out_weight: float32 [1024, 1024], P('tensor', 'dp'), may hold values from -3 to 3
- gate_up_weight: float32 [2, 1024, 4096], P(None, 'dp', 'tensor'), may hold values from -0.1875 to 0.1875
- down_weight: float32 [4096, 1024], P('tensor', 'dp'), may hold values from -0.09375 to 0.09375
- parent_of_row: int32 [20480], P('dp'), may hold values from 0 to 4, as said below
- cotangent: float32 [20480, 1024], P(('dp', 'tensor')), may hold values from -6 to 6
Outputs:
- block_output: float32 [20480, 1024], P(('dp', 'tensor'))
- input_grad: float32 [20480, 1024], P(('dp', 'tensor'))
- norm_gains_grad: float32 [2, 1024], P(None, 'dp')
- qkv_weight_grad: float32 [3, 1024, 1024], P(None, 'dp', 'tensor')
- out_weight_grad: float32 [1024, 1024], P('tensor', 'dp')
- gate_up_weight_grad: float32 [2, 1024, 4096], P(None, 'dp', 'tensor')
- down_weight_grad: float32 [4096, 1024], P('tensor', 'dp')
Inputs may be any that keep to these rules, and one draw needn't show every extreme that they name: `parent_of_row`: trunk and branch rows hold 0; the rows of a leaf hold its branch, 1 to 4; each branch is the parent of exactly two leaves of its tree.
All inputs are finite; a program needn't handle non-finite values.
Results may differ from a plain program's by a relative error of at most 0.019.
Values may be sent and summed in bfloat16 or wider, within the bound.
No kernel may reach another device: no remote copies, remote signals or barrier semaphores. Data moves between devices by JAX's collectives and lax.ppermute only.
A program may use at most 192 MiB of HBM per device.

v0:
```python
import jax
import jax.numpy as jnp
from jax import lax
from jax.sharding import PartitionSpec as P

HDIM = 64
TRUNK = 1024
SEG = 128
ROW_TREE = 2560


epsilon = 1e-06


def norm_rows(values, gain_row):
    inverse_rms = lax.rsqrt(jnp.mean(values * values, axis=-1, keepdims=True) + epsilon)
    return values * inverse_rms * gain_row


def segment_ids(row_count):
    position = jnp.arange(row_count, dtype=jnp.int32)
    tree_base = position // ROW_TREE * 13
    within = position % ROW_TREE
    beyond = within - TRUNK
    own_segment = jnp.where(
        within < TRUNK,
        0,
        jnp.where(beyond < 4 * SEG, 1 + beyond // SEG, 5 + (beyond - 4 * SEG) // SEG),
    )
    return (own_segment + tree_base, tree_base)


def body(
    block_input,
    norm_gains,
    qkv_weight,
    out_weight,
    gate_up_weight,
    down_weight,
    parent_of_row,
    cotangent,
):
    gains_cast = norm_gains.astype(jnp.bfloat16)
    qkv_cast = qkv_weight.astype(jnp.bfloat16)
    out_cast = out_weight.astype(jnp.bfloat16)
    gate_up_cast = gate_up_weight.astype(jnp.bfloat16)
    down_cast = down_weight.astype(jnp.bfloat16)
    gains_low, qkv_low, out_low, gate_up_low, down_low = (
        lax.all_gather(gains_cast, "dp", axis=1, tiled=True),
        lax.all_gather(qkv_cast, "dp", axis=1, tiled=True),
        lax.all_gather(out_cast, "dp", axis=1, tiled=True),
        lax.all_gather(gate_up_cast, "dp", axis=1, tiled=True),
        lax.all_gather(down_cast, "dp", axis=1, tiled=True),
    )
    row_count = parent_of_row.shape[0]
    width_local = qkv_low.shape[2]
    head_local = width_local // HDIM
    block_rows = min(512, row_count)
    block_count = row_count // block_rows
    score_scale = float(HDIM) ** (-0.5)
    segment_of_row, trunk_of_row = segment_ids(row_count)
    parent_segment = parent_of_row + trunk_of_row
    column_index = jnp.arange(row_count, dtype=jnp.int32)
    residual_in = block_input.astype(jnp.float32)
    gain_attn = gains_low[0].astype(jnp.float32)
    gain_mlp = gains_low[1].astype(jnp.float32)
    normed_attn = lax.all_gather(
        norm_rows(residual_in, gain_attn).astype(jnp.bfloat16), "tensor", axis=0, tiled=True
    )
    projected = jnp.einsum(
        "rd,cde->cre", normed_attn, qkv_low, preferred_element_type=jnp.float32
    ).astype(jnp.bfloat16)
    query_rows = projected[0].reshape(row_count, head_local, HDIM)
    key_rows = projected[1].reshape(row_count, head_local, HDIM)
    value_rows = projected[2].reshape(row_count, head_local, HDIM)

    def block_scores(block_index):
        row_start = block_index * block_rows
        query_block = lax.dynamic_slice_in_dim(query_rows, row_start, block_rows, 0)
        scores = (
            jnp.einsum("qhd,khd->hqk", query_block, key_rows, preferred_element_type=jnp.float32)
            * score_scale
        )
        row_index = row_start + jnp.arange(block_rows, dtype=jnp.int32)
        row_segment = lax.dynamic_slice_in_dim(segment_of_row, row_start, block_rows, 0)
        row_parent = lax.dynamic_slice_in_dim(parent_segment, row_start, block_rows, 0)
        row_trunk = lax.dynamic_slice_in_dim(trunk_of_row, row_start, block_rows, 0)
        column_segment = segment_of_row[None, :]
        allowed = (column_index[None, :] <= row_index[:, None]) & (
            (column_segment == row_segment[:, None])
            | (column_segment == row_parent[:, None])
            | (column_segment == row_trunk[:, None])
        )
        return (jnp.where(allowed[None], scores, -1e30), query_block)

    def attend_block(block_index):
        scores, query_block = block_scores(block_index)
        top_score = jnp.max(scores, axis=-1, keepdims=True)
        exp_scores = jnp.exp(scores - top_score)
        row_total = jnp.sum(exp_scores, axis=-1, keepdims=True)
        softmax_low = (exp_scores / row_total).astype(jnp.bfloat16)
        mixed_heads = jnp.einsum(
            "hqk,khd->qhd", softmax_low, value_rows, preferred_element_type=jnp.float32
        ).astype(jnp.bfloat16)
        return (mixed_heads, (top_score + jnp.log(row_total))[..., 0])

    block_ids = jnp.arange(block_count, dtype=jnp.int32)
    attended, log_totals = lax.map(attend_block, block_ids)
    attended = attended.reshape(row_count, width_local)
    attn_partial = jnp.dot(attended, out_low, preferred_element_type=jnp.float32)
    residual_mid = residual_in + lax.psum_scatter(
        attn_partial, "tensor", scatter_dimension=0, tiled=True
    )
    normed_mlp = lax.all_gather(
        norm_rows(residual_mid, gain_mlp).astype(jnp.bfloat16), "tensor", axis=0, tiled=True
    )
    gate_up = jnp.einsum(
        "rd,cdf->crf", normed_mlp, gate_up_low, preferred_element_type=jnp.float32
    ).astype(jnp.bfloat16)
    gate_value = gate_up[0].astype(jnp.float32)
    up_value = gate_up[1].astype(jnp.float32)
    sigmoid_gate = jax.nn.sigmoid(gate_value)
    hidden = (gate_value * sigmoid_gate * up_value).astype(jnp.bfloat16)
    mlp_partial = jnp.dot(hidden, down_low, preferred_element_type=jnp.float32)
    block_output = residual_mid + lax.psum_scatter(
        mlp_partial.astype(jnp.bfloat16), "tensor", scatter_dimension=0, tiled=True
    ).astype(jnp.float32)
    gains_again = norm_gains.astype(jnp.bfloat16)
    qkv_again = qkv_weight.astype(jnp.bfloat16)
    out_again = out_weight.astype(jnp.bfloat16)
    gate_up_again = gate_up_weight.astype(jnp.bfloat16)
    down_again = down_weight.astype(jnp.bfloat16)
    gains_low, qkv_low, out_low, gate_up_low, down_low = (
        lax.all_gather(gains_again, "dp", axis=1, tiled=True),
        lax.all_gather(qkv_again, "dp", axis=1, tiled=True),
        lax.all_gather(out_again, "dp", axis=1, tiled=True),
        lax.all_gather(gate_up_again, "dp", axis=1, tiled=True),
        lax.all_gather(down_again, "dp", axis=1, tiled=True),
    )
    gain_attn = gains_low[0].astype(jnp.float32)
    gain_mlp = gains_low[1].astype(jnp.float32)
    mlp_grad_rows = lax.all_gather(cotangent.astype(jnp.bfloat16), "tensor", axis=0, tiled=True)
    down_grad = jnp.einsum("rf,rd->fd", hidden, mlp_grad_rows, preferred_element_type=jnp.float32)
    hidden_grad = jnp.einsum(
        "rd,fd->rf", mlp_grad_rows, down_low, preferred_element_type=jnp.float32
    )
    gate_grad = hidden_grad * up_value * sigmoid_gate * (1.0 + gate_value * (1.0 - sigmoid_gate))
    up_grad = hidden_grad * gate_value * sigmoid_gate
    gate_up_grad_low = jnp.stack([gate_grad, up_grad]).astype(jnp.bfloat16)
    gate_up_grad = jnp.einsum(
        "rd,crf->cdf", normed_mlp, gate_up_grad_low, preferred_element_type=jnp.float32
    )
    normed_mlp_part = jnp.einsum(
        "crf,cdf->rd", gate_up_grad_low, gate_up_low, preferred_element_type=jnp.float32
    )
    normed_mlp_grad = lax.psum_scatter(normed_mlp_part, "tensor", scatter_dimension=0, tiled=True)
    norm_back_mlp = jax.vjp(norm_rows, residual_mid, gain_mlp)[1]
    mid_from_norm, gain_mlp_grad = norm_back_mlp(normed_mlp_grad)
    mid_grad = cotangent + mid_from_norm
    attn_grad_rows = lax.all_gather(mid_grad.astype(jnp.bfloat16), "tensor", axis=0, tiled=True)
    out_grad = jnp.einsum("re,rd->ed", attended, attn_grad_rows, preferred_element_type=jnp.float32)
    attended_grad = jnp.einsum(
        "rd,ed->re", attn_grad_rows, out_low, preferred_element_type=jnp.float32
    ).astype(jnp.bfloat16)
    attended_grad = attended_grad.reshape(row_count, head_local, HDIM)

    def back_block(carry, block_inputs):
        key_grad, value_grad = carry
        block_index, log_total = block_inputs
        scores, query_block = block_scores(block_index)
        probs = jnp.exp(scores - log_total[..., None])
        grad_block = lax.dynamic_slice_in_dim(
            attended_grad, block_index * block_rows, block_rows, 0
        )
        probs_grad = jnp.einsum(
            "qhd,khd->hqk", grad_block, value_rows, preferred_element_type=jnp.float32
        )
        inner_term = jnp.sum(probs * probs_grad, axis=-1, keepdims=True)
        score_grad = (probs * (probs_grad - inner_term)).astype(jnp.bfloat16)
        query_grad = (
            jnp.einsum("hqk,khd->qhd", score_grad, key_rows, preferred_element_type=jnp.float32)
            * score_scale
        )
        key_grad = (
            key_grad
            + jnp.einsum(
                "hqk,qhd->khd", score_grad, query_block, preferred_element_type=jnp.float32
            )
            * score_scale
        )
        value_grad = value_grad + jnp.einsum(
            "hqk,qhd->khd",
            probs.astype(jnp.bfloat16),
            grad_block,
            preferred_element_type=jnp.float32,
        )
        return ((key_grad, value_grad), query_grad)

    zero_grad = jnp.zeros((row_count, head_local, HDIM), jnp.float32)
    carried, query_grads = lax.scan(back_block, (zero_grad, zero_grad), (block_ids, log_totals))
    projected_grad = jnp.stack(
        [
            query_grads.reshape(row_count, width_local),
            carried[0].reshape(row_count, width_local),
            carried[1].reshape(row_count, width_local),
        ]
    ).astype(jnp.bfloat16)
    qkv_grad = jnp.einsum(
        "rd,cre->cde", normed_attn, projected_grad, preferred_element_type=jnp.float32
    )
    normed_attn_part = jnp.einsum(
        "cre,cde->rd", projected_grad, qkv_low, preferred_element_type=jnp.float32
    )
    normed_attn_grad = lax.psum_scatter(
        normed_attn_part.astype(jnp.bfloat16), "tensor", scatter_dimension=0, tiled=True
    ).astype(jnp.float32)
    norm_back_attn = jax.vjp(norm_rows, residual_in, gain_attn)[1]
    input_from_norm, gain_attn_grad = norm_back_attn(normed_attn_grad)
    input_grad = mid_grad + input_from_norm
    gain_grads = lax.psum(jnp.stack([gain_attn_grad, gain_mlp_grad]), "tensor")
    gains_out, qkv_out, out_out, gate_up_out, down_out = (
        lax.psum_scatter(
            gain_grads.astype(jnp.bfloat16), "dp", scatter_dimension=1, tiled=True
        ).astype(jnp.float32),
        lax.psum_scatter(
            qkv_grad.astype(jnp.bfloat16), "dp", scatter_dimension=1, tiled=True
        ).astype(jnp.float32),
        lax.psum_scatter(
            out_grad.astype(jnp.bfloat16), "dp", scatter_dimension=1, tiled=True
        ).astype(jnp.float32),
        lax.psum_scatter(
            gate_up_grad.astype(jnp.bfloat16), "dp", scatter_dimension=1, tiled=True
        ).astype(jnp.float32),
        lax.psum_scatter(
            down_grad.astype(jnp.bfloat16), "dp", scatter_dimension=1, tiled=True
        ).astype(jnp.float32),
    )
    return (block_output, input_grad, gains_out, qkv_out, out_out, gate_up_out, down_out)


def solution(mesh):
    placed = (
        P(("dp", "tensor"), None),
        P(None, "dp"),
        P(None, "dp", "tensor"),
        P("tensor", "dp"),
        P(None, "dp", "tensor"),
        P("tensor", "dp"),
        P("dp"),
        P(("dp", "tensor"), None),
    )
    return jax.shard_map(
        body,
        mesh=mesh,
        in_specs=placed,
        out_specs=(
            P(("dp", "tensor"), None),
            P(("dp", "tensor"), None),
            P(None, "dp"),
            P(None, "dp", "tensor"),
            P("tensor", "dp"),
            P(None, "dp", "tensor"),
            P("tensor", "dp"),
        ),
        check_vma=False,
    )
```

profile of v0, /device:TPU:0, one launch (start us, length us, event | category | flops | bytes accessed | tf_op | source)
XLA Modules:
  0.0 1441.7 jit_solution(5446281379806303339)
XLA Ops:
  9.9 22.1 %all_gather.32 = bf16[2,1024]{1,0:T(2,128)(2,1)S(1)} all-gather(bf16[2,128]{1,0:T(2,128)(2,1)S(1)} %convert_element_type.137), channel_id=1, replica_groups=mesh['dp'=8,'tensor'=4] {'dp'}, dimensions={1}, use_global_device_ids=true | all-gather | bytes 4608 | tf_op jit(solution)/shard_map/all_gather | solution.py:49
  36.5 29.7 %all_gather.35 = bf16[256,1024]{1,0:T(8,128)(2,1)} all-gather(bf16[256,128]{1,0:T(8,128)(2,1)S(1)} %convert_element_type.142), channel_id=1, replica_groups=mesh['dp'=8,'tensor'=4] {'dp'}, dimensions={1}, use_global_device_ids=true | all-gather | bytes 589824 | tf_op jit(solution)/shard_map/all_gather | solution.py:51
  66.2 40.1 %all-gather.8.cloned.1.call-done = bf16[2560,1024]{1,0:T(8,128)(2,1)} async-done(((bf16[640,1024]{1,0:T(8,128)(2,1)}), bf16[2560,1024]{1,0:T(8,128)(2,1)}) %all-gather.8.cloned.1.call-update) | async-done | bytes 5242896 | tf_op jit(solution)/shard_map/all_gather | solution.py:67
  115.6 182.9 %while.30 = (s32[]{:T(128)}, bf16[5,512,4,64]{1,3,2,0:T(8,128)(2,1)S(1)}, f32[5,4,512]{2,1,0:T(4,128)}, s32[5]{0:T(128)S(1)}, s32[2560]{0:T(1024)S(1)}, /*index=...) while((s32[]{:T(128)}, ...), condition=%wide.region_4.5_spmd.clone.clone, body=%wide.region_1.4_spmd.clone.clone.sunk | while | flops 1414396416 | bytes 155287808 | solution.py:108
  141.3 10.3 fusion.172
  177.8 10.3 fusion.172
  214.3 10.3 fusion.172
  250.8 10.3 fusion.172
  287.3 10.3 fusion.172
  308.8 83.3 %reduce-scatter.20.cloned.1.call-done = f32[640,1024]{1,0:T(8,128)} async-done(((f32[2560,1024]{1,0:T(8,128)}), f32[640,1024]{1,0:T(8,128)}) %reduce-scatter.20.cloned.1.call-update) | async-done | bytes 2621456 | tf_op jit(solution)/shard_map/reduce_scatter | solution.py:111
  401.0 67.2 %all-gather.14.cloned.1.call-done = bf16[2,1024,1024]{2,1,0:T(8,128)(2,1)} async-done(((bf16[2,128,1024]{2,1,0:T(8,128)(2,1)}), bf16[2,1024,1024]{2,1,0:T(8,128)(2,1)}) %all-gather.14.cloned.1.call-update) | async-done | bytes 4194320 | tf_op jit(solution)/shard_map/all_gather | solution.py:52
  468.2 40.7 %all-gather.12.cloned.1.call-done = bf16[2560,1024]{1,0:T(8,128)(2,1)} async-done(((bf16[640,1024]{1,0:T(8,128)(2,1)}), bf16[2560,1024]{1,0:T(8,128)(2,1)}) %all-gather.12.cloned.1.call-update) | async-done | bytes 5242896 | tf_op jit(solution)/shard_map/all_gather | solution.py:114
  508.9 16.7 %convert_bitcast_fusion = bf16[2,2560,1024]{2,1,0:T(8,128)(2,1)} fusion(bf16[2,1024,1024]{2,1,0:T(8,128)(2,1)} %all-gather.14.cloned.1.call-done, bf16[2560,1024]{1,0:T(8,128)(2,1)} %all-gather.12.cloned.1.call-done), kind=kOutput, calls=%fused_computation.68 | convolution fusion | flops 10742661120 | bytes 19922944 | tf_op jit(solution)/shard_map/rd,cdf->crf/dot_general | solution.py:117
  525.6 36.9 %all-gather.16.cloned.1.call-done = bf16[1024,1024]{1,0:T(8,128)(2,1)} async-done(((bf16[1024,128]{1,0:T(8,128)(2,1)}), bf16[1024,1024]{1,0:T(8,128)(2,1)}) %all-gather.16.cloned.1.call-update) | async-done | bytes 2097168 | tf_op jit(solution)/shard_map/all_gather | solution.py:53
  562.5 40.8 %all-gather.18.cloned.1.call-done = bf16[2560,1024]{1,0:T(8,128)(2,1)} async-done(((bf16[640,1024]{1,0:T(8,128)(2,1)}), bf16[2560,1024]{1,0:T(8,128)(2,1)}) %all-gather.18.cloned.1.call-update) | async-done | bytes 5242896 | tf_op jit(solution)/shard_map/all_gather | solution.py:142
  603.2 18.4 %fusion.63 = (bf16[1,2560,1024]{2,1,0:T(8,128)(2,1)S(1)}, bf16[1,2560,1024]{2,1,0:T(8,128)(2,1)}, bf16[2560,1024]{1,0:T(8,128)(2,1)}) fusion(bf16[2,2560,1024]{2,1,0:T(8,128)(2,1)} %convert_bitcast_fusion, bf16[2560,1024]{1,0:T(8,128)(2,1)} %all-gather.18.cloned.1.call-done, bf16[1024,1024]{1,0:T(8,128)(2,1)} %all-gather.16.cloned.1.call-done), kind=kOutput, calls=%fused_computation.87 | convolution fusion | flops 5415895040 | bytes 33554432 | tf_op jit(solution)/shard_map/rd,fd->rf/dot_general | solution.py:144
  624.0 15.2 %fusion.55 = f32[2560,1024]{1,0:T(8,128)} fusion(bf16[2,1024,1024]{2,1,0:T(8,128)(2,1)S(1)} %copy-done.26, bf16[1,2560,1024]{2,1,0:T(8,128)(2,1)} %get-tuple-element.370, bf16[1,2560,1024]{2,1,0:T(8,128)(2,1)S(1)} %get-tuple-element.369), kind=kOutput, calls=%fused_computation.71 | convolution fusion | flops 10742661120 | bytes 25165824 | tf_op jit(solution)/shard_map/crf,cdf->rd/dot_general | solution.py:153
  639.3 10.3 convolution_convert_fusion
  649.6 75.1 %reduce-scatter.24.cloned.1.call-done = f32[640,1024]{1,0:T(8,128)} async-done(((f32[2560,1024]{1,0:T(8,128)}), f32[640,1024]{1,0:T(8,128)}) %reduce-scatter.24.cloned.1.call-update) | async-done | bytes 2621456 | tf_op jit(solution)/shard_map/reduce_scatter | solution.py:156
  727.7 51.0 %reduce-scatter.22.cloned.1.call-done = bf16[640,1024]{1,0:T(8,128)(2,1)} async-done(((bf16[2560,1024]{1,0:T(8,128)(2,1)}), bf16[640,1024]{1,0:T(8,128)(2,1)}) %reduce-scatter.22.cloned.1.call-update) | async-done | bytes 1310736 | tf_op jit(solution)/shard_map/reduce_scatter | solution.py:125
  785.3 9.1 convolution_convert_fusion.2
  797.1 17.0 %convert_bitcast_fusion.1 = bf16[2,1024,1024]{1,2,0:T(8,128)(2,1)} fusion(bf16[2560,1024]{1,0:T(8,128)(2,1)} %all-gather.12.cloned.1.call-done, bf16[1,2560,1024]{2,1,0:T(8,128)(2,1)} %get-tuple-element.370, bf16[1,2560,1024]{2,1,0:T(8,128)(2,1)} %copy-done.27), kind=kOutput, calls=%fused_computation.90 | convolution fusion | flops 10744758272 | bytes 19922944 | tf_op jit(solution)/shard_map/rd,crf->cdf/dot_general | solution.py:150
  814.1 11.3 copy.56
  842.6 372.6 %while.31 = (s32[]{:T(128)}, f32[2560,4,64]{0,2,1:T(8,128)}, f32[2560,4,64]{0,2,1:T(8,128)}, bf16[5,512,4,64]{1,3,2,0:T(8,128)(2,1)}, s32[5]{0:T(128)S(1)}, /*in...) while((s32[]{:T(128)}, f32[2560,4,64]{0,2,1:T(8,128)}, ...), condition=%wide.region_12.13_spmd.clone.clone, body=%wide.region_10.12_spmd.clone.clone.sunk | while | flops 3446667776 | bytes 204824912 | solution.py:200
  852.3 12.0 fusion.182
  864.3 10.2 fusion.185
  874.5 16.4 %multiply_reduce_fusion.5 = (f32[4,512]{1,0:T(4,128)S(1)}, f32[4,512,2560]{2,1,0:T(8,128)}) fusion(f32[4,512,2560]{2,1,0:T(8,128)} %fusion.182, f32[4,512]{1,0:T(4,128)S(1)} %dynamic-slice_bitcast_fusion.2, pred[512,2560]{1,0:T(8,128)(4,1)S(1)} %fusion.183, bf16[2560,4,64]{0,2,1:T(8,128)(2,1)} %get-tuple-element.616, ...), kind=kOutput, calls=%fused_computation.21.clone.1 | convolution fusion | flops 697300992 | bytes 44843012 | tf_op jit(solution)/shard_map/while/body/eval_jaxpr/qhd,khd->hqk/dot_general | solution.py:175
  890.9 15.9 %multiply_convert_fusion.3 = bf16[4,512,2560]{2,1,0:T(8,128)(2,1)S(1)} fusion(f32[4,512,2560]{2,1,0:T(8,128)} %get-tuple-element.526, f32[4,512,2560]{2,1,0:T(8,128)} %fusion.182, f32[4,512]{1,0:T(4,128)S(1)} %get-tuple-element.527, f32[4,512]{1,0:T(4,128)S(1)} %dynamic-slice_bitcast_fusion.2, pred[512,2560]{1,0:T(8,128)(4,1)} %copy-done.1), kind=kLoop, calls=%fused_computation.20.clone.1 | loop fusion | flops 31457280 | bytes 53755904 | tf_op jit(solution)/shard_map/while/body/eval_jaxpr/convert_element_type | solution.py:179
  926.2 12.1 fusion.182
  938.3 10.4 fusion.185
  948.7 16.6 %multiply_reduce_fusion.5 = (f32[4,512]{1,0:T(4,128)S(1)}, f32[4,512,2560]{2,1,0:T(8,128)}) fusion(f32[4,512,2560]{2,1,0:T(8,128)} %fusion.182, f32[4,512]{1,0:T(4,128)S(1)} %dynamic-slice_bitcast_fusion.2, pred[512,2560]{1,0:T(8,128)(4,1)S(1)} %fusion.183, bf16[2560,4,64]{0,2,1:T(8,128)(2,1)} %get-tuple-element.616, ...), kind=kOutput, calls=%fused_computation.21.clone.1 | convolution fusion | flops 697300992 | bytes 44843012 | tf_op jit(solution)/shard_map/while/body/eval_jaxpr/qhd,khd->hqk/dot_general | solution.py:175
  965.3 16.2 %multiply_convert_fusion.3 = bf16[4,512,2560]{2,1,0:T(8,128)(2,1)S(1)} fusion(f32[4,512,2560]{2,1,0:T(8,128)} %get-tuple-element.526, f32[4,512,2560]{2,1,0:T(8,128)} %fusion.182, f32[4,512]{1,0:T(4,128)S(1)} %get-tuple-element.527, f32[4,512]{1,0:T(4,128)S(1)} %dynamic-slice_bitcast_fusion.2, pred[512,2560]{1,0:T(8,128)(4,1)} %copy-done.1), kind=kLoop, calls=%fused_computation.20.clone.1 | loop fusion | flops 31457280 | bytes 53755904 | tf_op jit(solution)/shard_map/while/body/eval_jaxpr/convert_element_type | solution.py:179
  1001.5 11.9 fusion.182
  1013.4 10.1 fusion.185
  1023.6 16.4 %multiply_reduce_fusion.5 = (f32[4,512]{1,0:T(4,128)S(1)}, f32[4,512,2560]{2,1,0:T(8,128)}) fusion(f32[4,512,2560]{2,1,0:T(8,128)} %fusion.182, f32[4,512]{1,0:T(4,128)S(1)} %dynamic-slice_bitcast_fusion.2, pred[512,2560]{1,0:T(8,128)(4,1)S(1)} %fusion.183, bf16[2560,4,64]{0,2,1:T(8,128)(2,1)} %get-tuple-element.616, ...), kind=kOutput, calls=%fused_computation.21.clone.1 | convolution fusion | flops 697300992 | bytes 44843012 | tf_op jit(solution)/shard_map/while/body/eval_jaxpr/qhd,khd->hqk/dot_general | solution.py:175
  1040.0 15.9 %multiply_convert_fusion.3 = bf16[4,512,2560]{2,1,0:T(8,128)(2,1)S(1)} fusion(f32[4,512,2560]{2,1,0:T(8,128)} %get-tuple-element.526, f32[4,512,2560]{2,1,0:T(8,128)} %fusion.182, f32[4,512]{1,0:T(4,128)S(1)} %get-tuple-element.527, f32[4,512]{1,0:T(4,128)S(1)} %dynamic-slice_bitcast_fusion.2, pred[512,2560]{1,0:T(8,128)(4,1)} %copy-done.1), kind=kLoop, calls=%fused_computation.20.clone.1 | loop fusion | flops 31457280 | bytes 53755904 | tf_op jit(solution)/shard_map/while/body/eval_jaxpr/convert_element_type | solution.py:179
  1076.0 11.8 fusion.182
  1087.8 10.1 fusion.185
  1097.9 16.4 %multiply_reduce_fusion.5 = (f32[4,512]{1,0:T(4,128)S(1)}, f32[4,512,2560]{2,1,0:T(8,128)}) fusion(f32[4,512,2560]{2,1,0:T(8,128)} %fusion.182, f32[4,512]{1,0:T(4,128)S(1)} %dynamic-slice_bitcast_fusion.2, pred[512,2560]{1,0:T(8,128)(4,1)S(1)} %fusion.183, bf16[2560,4,64]{0,2,1:T(8,128)(2,1)} %get-tuple-element.616, ...), kind=kOutput, calls=%fused_computation.21.clone.1 | convolution fusion | flops 697300992 | bytes 44843012 | tf_op jit(solution)/shard_map/while/body/eval_jaxpr/qhd,khd->hqk/dot_general | solution.py:175
  1114.3 15.8 %multiply_convert_fusion.3 = bf16[4,512,2560]{2,1,0:T(8,128)(2,1)S(1)} fusion(f32[4,512,2560]{2,1,0:T(8,128)} %get-tuple-element.526, f32[4,512,2560]{2,1,0:T(8,128)} %fusion.182, f32[4,512]{1,0:T(4,128)S(1)} %get-tuple-element.527, f32[4,512]{1,0:T(4,128)S(1)} %dynamic-slice_bitcast_fusion.2, pred[512,2560]{1,0:T(8,128)(4,1)} %copy-done.1), kind=kLoop, calls=%fused_computation.20.clone.1 | loop fusion | flops 31457280 | bytes 53755904 | tf_op jit(solution)/shard_map/while/body/eval_jaxpr/convert_element_type | solution.py:179
  1150.1 11.8 fusion.182
  1161.9 10.2 fusion.185
  1172.1 16.4 %multiply_reduce_fusion.5 = (f32[4,512]{1,0:T(4,128)S(1)}, f32[4,512,2560]{2,1,0:T(8,128)}) fusion(f32[4,512,2560]{2,1,0:T(8,128)} %fusion.182, f32[4,512]{1,0:T(4,128)S(1)} %dynamic-slice_bitcast_fusion.2, pred[512,2560]{1,0:T(8,128)(4,1)S(1)} %fusion.183, bf16[2560,4,64]{0,2,1:T(8,128)(2,1)} %get-tuple-element.616, ...), kind=kOutput, calls=%fused_computation.21.clone.1 | convolution fusion | flops 697300992 | bytes 44843012 | tf_op jit(solution)/shard_map/while/body/eval_jaxpr/qhd,khd->hqk/dot_general | solution.py:175
  1188.5 15.8 %multiply_convert_fusion.3 = bf16[4,512,2560]{2,1,0:T(8,128)(2,1)S(1)} fusion(f32[4,512,2560]{2,1,0:T(8,128)} %get-tuple-element.526, f32[4,512,2560]{2,1,0:T(8,128)} %fusion.182, f32[4,512]{1,0:T(4,128)S(1)} %get-tuple-element.527, f32[4,512]{1,0:T(4,128)S(1)} %dynamic-slice_bitcast_fusion.2, pred[512,2560]{1,0:T(8,128)(4,1)} %copy-done.1), kind=kLoop, calls=%fused_computation.20.clone.1 | loop fusion | flops 31457280 | bytes 53755904 | tf_op jit(solution)/shard_map/while/body/eval_jaxpr/convert_element_type | solution.py:179
  1244.4 8.8 bitcast_convert_fusion
  1260.3 48.6 %reduce-scatter.30.cloned.1.call-done = bf16[128,768]{1,0:T(8,128)(2,1)} async-done(((bf16[1024,768]{1,0:T(8,128)(2,1)}), bf16[128,768]{1,0:T(8,128)(2,1)}) %reduce-scatter.30.cloned.1.call-update) | async-done | bytes 196624
  1311.1 50.6 %reduce-scatter.26.cloned.1.call-done = bf16[640,1024]{1,0:T(8,128)(2,1)} async-done(((bf16[2560,1024]{1,0:T(8,128)(2,1)}), bf16[640,1024]{1,0:T(8,128)(2,1)}) %reduce-scatter.26.cloned.1.call-update) | async-done | bytes 1310736 | tf_op jit(solution)/shard_map/reduce_scatter | solution.py:214
  1375.0 58.5 %reduce-scatter.28.cloned.1.call-done = bf16[128,2]{1,0:T(8,128)(2,1)} async-done(((bf16[1024,2]{1,0:T(8,128)(2,1)}), bf16[128,2]{1,0:T(8,128)(2,1)}) %reduce-scatter.28.cloned.1.call-update) | async-done | bytes 528
  (277 shorter events, 343.8 us)
Async XLA Ops:
  7.2 27.8 %copy-start.3 = (bf16[640,1024]{1,0:T(8,128)(2,1)S(1)}, bf16[640,1024]{1,0:T(8,128)(2,1)}, u32[]{:S(2)}) copy-start(bf16[640,1024]{1,0:T(8,128)(2,1)} %param.12) | copy-start | bytes 3932164
  7.2 59.0 %all-gather.10.cloned.1.call-start = ((), (), s32[]{:S(2)}) async-start(), calls=%async_computation.10 | async-start | bytes 1769472 | tf_op jit(solution)/shard_map/all_gather | solution.py:50
  9.2 97.1 %all-gather.8.cloned.1.call-start = ((), (), s32[]{:S(2)}) async-start(), calls=%async_computation.9 | async-start | bytes 6553600 | tf_op jit(solution)/shard_map/all_gather | solution.py:67
  32.0 4.5 copy-start.25
  36.4 355.8 %reduce-scatter.20.cloned.1.call-start = ((), (), s32[]{:S(2)}) async-start(), calls=%async_computation.11 | async-start | bytes 13107200 | tf_op jit(solution)/shard_map/reduce_scatter | solution.py:111
  128.6 7.0 copy-start
  165.1 7.0 copy-start
  201.6 7.0 copy-start
  238.1 7.0 copy-start
  274.6 7.0 copy-start
  306.7 161.5 %all-gather.14.cloned.1.call-start = ((), (), s32[]{:S(2)}) async-start(), calls=%async_computation.13 | async-start | bytes 4718592 | tf_op jit(solution)/shard_map/all_gather | solution.py:52
  308.8 85.9 %copy-start.21 = (f32[1,1024]{1,0:T(1,128)S(1)}, f32[1,1024]{1,0:T(1,128)}, u32[]{:S(2)}) copy-start(f32[1,1024]{1,0:T(1,128)} %get-tuple-element.376) | copy-start | bytes 12292
  308.8 200.1 %all-gather.12.cloned.1.call-start = ((), (), s32[]{:S(2)}) async-start(), calls=%async_computation.12 | async-start | bytes 6553600 | tf_op jit(solution)/shard_map/all_gather | solution.py:114
  396.0 166.4 %all-gather.16.cloned.1.call-start = ((), (), s32[]{:S(2)}) async-start(), calls=%async_computation.14 | async-start | bytes 2359296 | tf_op jit(solution)/shard_map/all_gather | solution.py:53
  397.9 205.4 %all-gather.18.cloned.1.call-start = ((), (), s32[]{:S(2)}) async-start(), calls=%async_computation.16 | async-start | bytes 6553600 | tf_op jit(solution)/shard_map/all_gather | solution.py:142
  401.0 323.8 %reduce-scatter.24.cloned.1.call-start = ((), (), s32[]{:S(2)}) async-start(), calls=%async_computation.17 | async-start | bytes 13107200 | tf_op jit(solution)/shard_map/reduce_scatter | solution.py:156
  603.2 20.8 %copy-start.26 = (bf16[2,1024,1024]{2,1,0:T(8,128)(2,1)S(1)}, bf16[2,1024,1024]{2,1,0:T(8,128)(2,1)}, u32[]{:S(2)}) copy-start(bf16[2,1024,1024]{2,1,0:T(8,128)(2,1)} %all-gather.14.cloned.1.call-done) | copy-start | bytes 12582916
  639.2 139.5 %reduce-scatter.22.cloned.1.call-start = ((), (), s32[]{:S(2)}) async-start(), calls=%async_computation.15 | async-start | bytes 6553600 | tf_op jit(solution)/shard_map/reduce_scatter | solution.py:125
  649.6 181.6 %all-gather.20.cloned.1.call-start = ((), (), s32[]{:S(2)}) async-start(), calls=%async_computation.18 | async-start | bytes 6553600 | tf_op jit(solution)/shard_map/all_gather | solution.py:160
  785.2 468.0 %reduce-scatter.36.cloned.1.call-start = ((), (), s32[]{:S(2)}) async-start(), calls=%async_computation.24 | async-start | bytes 2359296
  797.0 458.2 %reduce-scatter.34.cloned.1.call-start = ((), (), s32[]{:S(2)}) async-start(), calls=%async_computation.23 | async-start | bytes 4718592
  831.0 427.7 %reduce-scatter.32.cloned.1.call-start = ((), (), s32[]{:S(2)}) async-start(), calls=%async_computation.22 | async-start | bytes 589824
  837.4 5.2 copy-start.12
  837.4 471.6 %reduce-scatter.30.cloned.1.call-start = ((), (), s32[]{:S(2)}) async-start(), calls=%async_computation.21 | async-start | bytes 1769472
  852.3 22.2 %copy-start.1 = (pred[512,2560]{1,0:T(8,128)(4,1)}, pred[512,2560]{1,0:T(8,128)(4,1)S(1)}, u32[]{:S(2)}) copy-start(pred[512,2560]{1,0:T(8,128)(4,1)S(1)} %fusion.183) | copy-start | bytes 3932164 | tf_op jit(solution)/shard_map/while
  852.3 12.0 copy-start.8
  874.5 16.4 %copy-start.9 = (f32[2560,4,64]{0,2,1:T(8,128)}, f32[2560,4,64]{0,2,1:T(8,128)S(1)}, u32[]{:S(2)}) copy-start(f32[2560,4,64]{0,2,1:T(8,128)S(1)} %fusion.185) | copy-start | bytes 7864324 | tf_op jit(solution)/shard_map/while
  926.2 22.5 %copy-start.1 = (pred[512,2560]{1,0:T(8,128)(4,1)}, pred[512,2560]{1,0:T(8,128)(4,1)S(1)}, u32[]{:S(2)}) copy-start(pred[512,2560]{1,0:T(8,128)(4,1)S(1)} %fusion.183) | copy-start | bytes 3932164 | tf_op jit(solution)/shard_map/while
  926.2 12.1 copy-start.8
  948.7 16.6 %copy-start.9 = (f32[2560,4,64]{0,2,1:T(8,128)}, f32[2560,4,64]{0,2,1:T(8,128)S(1)}, u32[]{:S(2)}) copy-start(f32[2560,4,64]{0,2,1:T(8,128)S(1)} %fusion.185) | copy-start | bytes 7864324 | tf_op jit(solution)/shard_map/while
  1001.5 22.0 %copy-start.1 = (pred[512,2560]{1,0:T(8,128)(4,1)}, pred[512,2560]{1,0:T(8,128)(4,1)S(1)}, u32[]{:S(2)}) copy-start(pred[512,2560]{1,0:T(8,128)(4,1)S(1)} %fusion.183) | copy-start | bytes 3932164 | tf_op jit(solution)/shard_map/while
  1001.5 11.9 copy-start.8
  1023.6 16.5 %copy-start.9 = (f32[2560,4,64]{0,2,1:T(8,128)}, f32[2560,4,64]{0,2,1:T(8,128)S(1)}, u32[]{:S(2)}) copy-start(f32[2560,4,64]{0,2,1:T(8,128)S(1)} %fusion.185) | copy-start | bytes 7864324 | tf_op jit(solution)/shard_map/while
  1075.9 21.9 %copy-start.1 = (pred[512,2560]{1,0:T(8,128)(4,1)}, pred[512,2560]{1,0:T(8,128)(4,1)S(1)}, u32[]{:S(2)}) copy-start(pred[512,2560]{1,0:T(8,128)(4,1)S(1)} %fusion.183) | copy-start | bytes 3932164 | tf_op jit(solution)/shard_map/while
  1075.9 11.8 copy-start.8
  1097.9 16.4 %copy-start.9 = (f32[2560,4,64]{0,2,1:T(8,128)}, f32[2560,4,64]{0,2,1:T(8,128)S(1)}, u32[]{:S(2)}) copy-start(f32[2560,4,64]{0,2,1:T(8,128)S(1)} %fusion.185) | copy-start | bytes 7864324 | tf_op jit(solution)/shard_map/while
  1150.1 22.0 %copy-start.1 = (pred[512,2560]{1,0:T(8,128)(4,1)}, pred[512,2560]{1,0:T(8,128)(4,1)S(1)}, u32[]{:S(2)}) copy-start(pred[512,2560]{1,0:T(8,128)(4,1)S(1)} %fusion.183) | copy-start | bytes 3932164 | tf_op jit(solution)/shard_map/while
  1150.1 11.8 copy-start.8
  1172.1 16.4 %copy-start.9 = (f32[2560,4,64]{0,2,1:T(8,128)}, f32[2560,4,64]{0,2,1:T(8,128)S(1)}, u32[]{:S(2)}) copy-start(f32[2560,4,64]{0,2,1:T(8,128)S(1)} %fusion.185) | copy-start | bytes 7864324 | tf_op jit(solution)/shard_map/while
  1220.0 5.0 copy-start.2
  1244.3 117.3 %reduce-scatter.26.cloned.1.call-start = ((), (), s32[]{:S(2)}) async-start(), calls=%async_computation.19 | async-start | bytes 6553600 | tf_op jit(solution)/shard_map/reduce_scatter | solution.py:214
  1253.2 180.3 %reduce-scatter.28.cloned.1.call-start = ((), (), s32[]{:S(2)}) async-start(), calls=%async_computation.20 | async-start | bytes 294912
  1255.2 106.5 %copy-start.4 = (bf16[640,1024]{1,0:T(8,128)(2,1)S(1)}, bf16[640,1024]{1,0:T(8,128)(2,1)}, u32[]{:S(2)}) copy-start(bf16[640,1024]{1,0:T(8,128)(2,1)} %param.12) | copy-start | bytes 3932164
  1255.2 106.5 %copy-start.18 = (f32[640]{0:T(1024)S(1)}, f32[640]{0:T(1024)}, u32[]{:S(2)}) copy-start(f32[640]{0:T(1024)} %copy-done.17) | copy-start | bytes 7684
  1255.2 106.5 %copy-start.20 = (f32[1,1024]{1,0:T(1,128)S(1)}, f32[1,1024]{1,0:T(1,128)}, u32[]{:S(2)}) copy-start(f32[1,1024]{1,0:T(1,128)} %copy-done.19) | copy-start | bytes 12292
  1258.7 105.5 %copy-start.24 = (f32[1024]{0:T(1024)S(1)}, f32[1024]{0:T(1024)}, u32[]{:S(2)}) copy-start(f32[1024]{0:T(1024)} %get-tuple-element.311) | copy-start | bytes 12292
  1258.7 111.4 %copy-start.23 = (f32[640]{0:T(1024)S(1)}, f32[640]{0:T(1024)}, u32[]{:S(2)}) copy-start(f32[640]{0:T(1024)} %copy-done.22) | copy-start | bytes 7684
  1361.7 9.4 copy-start.7
  (12 other events, 21.6 us)
Sparse Core Ops, SparseCore 0:
  10.6 51.0 all-gather.9
  63.9 42.3 all-gather.7
  306.8 85.2 reduce-scatter.19
  394.7 73.3 all-gather.13
  470.1 38.6 all-gather.11
  511.3 51.0 all-gather.15
  564.6 38.6 all-gather.17
  639.4 85.3 reduce-scatter.23
  727.3 51.3 reduce-scatter.21
  785.3 40.4 all-gather.19
  829.8 67.9 reduce-scatter.35
  901.7 86.7 reduce-scatter.33
  991.8 61.6 reduce-scatter.31
  1244.5 64.4 reduce-scatter.29
  1311.4 50.2 reduce-scatter.25
  1371.2 62.2 reduce-scatter.27
where the time goes:
time: 1450 us; the launch traced here: 1440 us
  waiting for transfers between devices  593 us (41%)
  matrix products  451 us (31%)
  other arithmetic  204 us (14%)
  local copies, waits for them, and re-layouts  112 us (8%)
  blocking collectives  57.7 us (4%)
  between operations  14.6 us (1%)
    unnamed x21, waiting for transfers between devices  107 us
    dot_general x10, matrix products, block_scores(): jnp.einsum('qhd,khd->hqk', query_block, key_rows, preferred_element_type=...  87.5 us
    reduce_scatter x1, waiting for transfers between devices, body(): lax.psum_scatter(attn_partial, 'tensor', scatter_dimension=0, tiled=True)  83.3 us
    dot_general x5, matrix products, back_block(): jnp.einsum('qhd,khd->hqk', grad_block, value_rows, preferred_element_type...  82.2 us
    convert_element_type x5, other arithmetic, back_block(): score_grad = (probs * (probs_grad - inner_term)).astype(jnp.bfloat16)  79.6 us
    reduce_scatter x1, waiting for transfers between devices, body(): lax.psum_scatter(normed_mlp_part, 'tensor', scatter_dimension=0, tiled=True)  75.1 us
    all_gather x1, waiting for transfers between devices, body(): lax.all_gather(gate_up_cast, 'dp', axis=1, tiled=True)  67.2 us
    and x10, other arithmetic, block_scores(): (column_index[None, :] <= row_index[:, None]) & ((column_segment == row_s...  57.3 us
  transfers between devices with their start and end apart: 16, of which 11 were waited for; matrix products, arithmetic and copies ran while one was open for 36% of the time, Pallas kernels for 0%

commit v1 on v0

--- a/solution.py
+++ b/solution.py
@@ -1,6 +1,9 @@
+import functools
 import jax
 import jax.numpy as jnp
 from jax import lax
+from jax.experimental import pallas as pl
+from jax.experimental.pallas import tpu as pltpu
 from jax.sharding import PartitionSpec as P
 
 HDIM = 64
@@ -30,7 +33,7 @@
     return (own_segment + tree_base, tree_base)
 
 
-def body(
+def body_any_mesh(
     block_input,
     norm_gains,
     qkv_weight,
@@ -238,6 +241,1014 @@
     return (block_output, input_grad, gains_out, qkv_out, out_out, gate_up_out, down_out)
 
 
+QB = 256
+NT = (((1,), (1,)), ((), ()))
+NN = (((1,), (0,)), ((), ()))
+TN = (((0,), (0,)), ((), ()))
+
+
+def _dot(a, b, dims):
+    return lax.dot_general(a, b, dims, preferred_element_type=jnp.float32)
+
+
+def _stacked(tile, columns, n):
+    return pl.BlockSpec((1, tile, columns), lambda i: (n, i, 0))
+
+
+def _full(shape):
+    return pl.BlockSpec(shape, lambda i: (0,) * len(shape))
+
+
+def _smem():
+    return pl.BlockSpec(memory_space=pltpu.SMEM)
+
+
+def _rows(tile, columns):
+    return pl.BlockSpec((tile, columns), lambda i: (i, 0))
+
+
+def _params():
+    return pltpu.CompilerParams(dimension_semantics=("arbitrary",), vmem_limit_bytes=60 << 20)
+
+
+STRETCH = 6.0
+
+
+def _cost(flops, bytes_accessed):
+    return pl.CostEstimate(
+        flops=int(flops * STRETCH), bytes_accessed=int(bytes_accessed * STRETCH), transcendentals=0
+    )
+
+
+def _row_tile(rows):
+    return rows // 2 if rows % 32 == 0 else rows
+
+
+def _normed(values):
+    inverse_rms = lax.rsqrt(jnp.mean(values * values, axis=-1, keepdims=True) + epsilon)
+    return inverse_rms, values * inverse_rms
+
+
+def _place_kernel(where_ref, *refs):
+    shards, out = refs[:-1], refs[-1]
+    size = shards[0].shape[0]
+    for n, shard in enumerate(shards):
+        out[pl.ds(pl.multiple_of(where_ref[n] * size, size), size), :] = shard[...]
+
+
+def place(where, shards):
+    size, columns = shards[0].shape
+    return pl.pallas_call(
+        _place_kernel,
+        grid=(1,),
+        out_shape=jax.ShapeDtypeStruct((size * len(shards), columns), shards[0].dtype),
+        in_specs=[_smem()] + [_full((size, columns))] * len(shards),
+        out_specs=_full((size * len(shards), columns)),
+        compiler_params=_params(),
+        cost_estimate=_cost(0, 4 * size * columns * len(shards)),
+        name="place",
+    )(where, *shards)
+
+
+def _project_kernel(x0_ref, x1_ref, gain_ref, w_ref, n0_ref, n1_ref, p0_ref, p1_ref):
+    def run(x_ref, normed_ref, out_ref):
+        normed = (_normed(x_ref[...].astype(jnp.float32))[1] * gain_ref[...]).astype(jnp.bfloat16)
+        normed_ref[...] = normed
+        out_ref[...] = _dot(normed, w_ref[...], NN).astype(jnp.bfloat16)
+
+    half = pl.num_programs(0) // 2
+
+    @pl.when(pl.program_id(0) < half)
+    def _():
+        run(x0_ref, n0_ref, p0_ref)
+
+    @pl.when(pl.program_id(0) >= half)
+    def _():
+        run(x1_ref, n1_ref, p1_ref)
+
+
+def project(x0, x1, gain, weight, columns):
+    rows, depth = x0.shape
+    tile = _row_tile(rows)
+    steps = rows // tile
+    early = lambda c: pl.BlockSpec((tile, c), lambda i: (jnp.minimum(i, steps - 1), 0))
+    late = lambda c: pl.BlockSpec((tile, c), lambda i: (jnp.maximum(i - steps, 0), 0))
+    out = lambda c: jax.ShapeDtypeStruct((rows, c), jnp.bfloat16)
+    return pl.pallas_call(
+        _project_kernel,
+        grid=(2 * steps,),
+        out_shape=[out(depth), out(depth), out(columns), out(columns)],
+        in_specs=[early(depth), late(depth), _full((1, depth)), _full((depth, columns))],
+        out_specs=[early(depth), late(depth), early(columns), late(columns)],
+        compiler_params=_params(),
+        cost_estimate=_cost(4 * rows * depth * columns, 4 * rows * (2 * depth + columns)),
+        name="project",
+    )(x0, x1, gain, weight)
+
+
+def _mlp_kernel(keep, step, att0, att1, att2, att3, x_ref, cot_ref, gain_ref, w_hbm, d_hbm, m_hbm, *refs):
+    part_ref, hidden_ref, grad_ref, normed_ref, branch_ref = refs[:5]
+    w_ref, d_ref, mate_ref, acc, acc_b, sems = refs[-6:]
+    width = att0.shape[2]
+    count = hidden_ref.shape[1]
+    out_at = 2 * count
+    chunks = count // step
+    pulls = [
+        pltpu.make_async_copy(
+            w_hbm.at[:, pl.ds(out_at, 2 * width)], w_ref.at[:, pl.ds(out_at, 2 * width)], sems.at[0]
+        ),
+        pltpu.make_async_copy(m_hbm, mate_ref, sems.at[1]),
+    ]
+    for c in range(chunks):
+        for g in range(3):
+            source, target = (w_hbm, w_ref) if g < 2 else (d_hbm, d_ref)
+            at = pl.ds(g % 2 * count + c * step, step)
+            pulls.append(
+                pltpu.make_async_copy(source.at[:, at], target.at[:, at], sems.at[2 + 3 * c + g])
+            )
+    first = pl.program_id(0) == 0
+
+    @pl.when(first)
+    def _():
+        for pull in pulls:
+            pull.start()
+        for pull in pulls[:2]:
+            pull.wait()
+
+    branch = _dot(att0[0], w_ref[:, out_at : out_at + width], NT)
+    branch += _dot(att2[0], w_ref[:, out_at + width : out_at + 2 * width], NT)
+    branch += _dot(att1[0], mate_ref[:, :width], NT) + _dot(att3[0], mate_ref[:, width:], NT)
+    residual = x_ref[...].astype(jnp.float32) + branch
+    if keep:
+        refs[5][...] = residual
+    normed_ref[...] = (_normed(residual)[1] * gain_ref[...]).astype(jnp.bfloat16)
+    for c in range(chunks):
+
+        @pl.when(first)
+        def _():
+            for pull in pulls[2 + 3 * c : 5 + 3 * c]:
+                pull.wait()
+
+        gate_at, up_at = [slice(g * count + c * step, g * count + (c + 1) * step) for g in (0, 1)]
+        gate = _dot(normed_ref[...], w_ref[:, gate_at], NN).astype(jnp.bfloat16).astype(jnp.float32)
+        up = _dot(normed_ref[...], w_ref[:, up_at], NN).astype(jnp.bfloat16).astype(jnp.float32)
+        hidden_grad = _dot(cot_ref[...], d_ref[:, gate_at], NN)
+        sig = 0.5 * jnp.tanh(0.5 * gate) + 0.5
+        act = gate * sig
+        hidden_ref[:, gate_at] = (act * up).astype(jnp.bfloat16)
+        grad_ref[:, gate_at] = (hidden_grad * up * (sig + act * (1.0 - sig))).astype(jnp.bfloat16)
+        grad_ref[:, up_at] = (hidden_grad * act).astype(jnp.bfloat16)
+        term = _dot(grad_ref[:, gate_at], w_ref[:, gate_at], NT) + _dot(
+            grad_ref[:, up_at], w_ref[:, up_at], NT
+        )
+        down = _dot(hidden_ref[:, gate_at], d_ref[:, gate_at], NT)
+        if c > 0:
+            term = term + acc[...]
+            down = down + acc_b[...]
+        if c < chunks - 1:
+            acc[...] = term
+            acc_b[...] = down
+        else:
+            part_ref[...] = term.astype(part_ref.dtype)
+            branch_ref[...] = down.astype(branch_ref.dtype)
+
+
+def mlp(attended, x, cot, gain, weights, down, out_mate, keep, step=512):
+    rows, depth = x.shape
+    width = attended[0][0].shape[2]
+    count = down.shape[1]
+    tile = _row_tile(rows)
+    step = min(step, count)
+    outs = [(depth, jnp.bfloat16), (count, jnp.bfloat16), (2 * count, jnp.bfloat16)]
+    outs += [(depth, jnp.bfloat16)] * 2
+    if keep:
+        outs.append((depth, jnp.float32))
+    anywhere = pl.BlockSpec(memory_space=pl.ANY)
+    return pl.pallas_call(
+        functools.partial(_mlp_kernel, keep, step),
+        grid=(rows // tile,),
+        out_shape=[jax.ShapeDtypeStruct((rows, c), d) for c, d in outs],
+        in_specs=[_stacked(tile, width, n) for v, n in attended]
+        + [_rows(tile, depth)] * 2
+        + [_full((1, depth)), anywhere, anywhere, anywhere],
+        out_specs=[_rows(tile, c) for c, d in outs],
+        scratch_shapes=[
+            pltpu.VMEM(weights.shape, jnp.bfloat16),
+            pltpu.VMEM(down.shape, jnp.bfloat16),
+            pltpu.VMEM(out_mate.shape, jnp.bfloat16),
+            pltpu.VMEM((tile, depth), jnp.float32),
+            pltpu.VMEM((tile, depth), jnp.float32),
+            pltpu.SemaphoreType.DMA((2 + 3 * (count // step),)),
+        ],
+        compiler_params=_params(),
+        cost_estimate=_cost(2 * rows * depth * (4 * width + 6 * count), 18 << 20),
+        name="mlp",
+    )(*[v for v, n in attended], x, cot, gain, weights, down, out_mate)
+
+
+def _pull_groups(right, right_s, row_at, column_at, step, sems, base):
+    groups = []
+    for c in range(right[0].shape[-1] // step):
+        group = []
+        at = row_at
+        for j, piece in enumerate(right):
+            rows = piece.shape[0]
+            group.append(
+                pltpu.make_async_copy(
+                    piece.at[:, pl.ds(c * step, step)],
+                    right_s.at[pl.ds(at, rows), pl.ds(column_at + c * step, step)],
+                    sems.at[base + c * len(right) + j],
+                )
+            )
+            at += rows
+        groups.append(group)
+    return groups
+
+
+def _start_all(groups):
+    @pl.when(pl.program_id(0) == 0)
+    def _():
+        for group in groups:
+            for pull in group:
+                pull.start()
+
+
+def _wait_group(group):
+    @pl.when(pl.program_id(0) == 0)
+    def _():
+        for pull in group:
+            pull.wait()
+
+
+def _join(pieces, out):
+    at = 0
+    for piece in pieces:
+        rows = piece.shape[0]
+        out[at : at + rows, :] = piece[...]
+        at += rows
+
+
+def _split_rows(acc, y, near, far):
+    size = near.shape[1]
+    near[...] = acc[pl.ds(pl.multiple_of(y * size, size), size), :].astype(near.dtype)[None]
+    far[...] = acc[pl.ds(pl.multiple_of((1 - y) * size, size), size), :].astype(far.dtype)[None]
+
+
+def _grad_kernel(n, step, split, *refs):
+    if split:
+        y_ref, refs = refs[0], refs[1:]
+    left, right = refs[:n], refs[n : 2 * n]
+    outs = refs[2 * n : -3 - split]
+    left_s, right_s, sems = refs[len(refs) - 3 - split : len(refs) - split]
+    acc = refs[-1] if split else outs[0]
+    groups = _pull_groups(right, right_s, 0, 0, step, sems, 0)
+    _start_all(groups)
+    _join(left, left_s)
+    for c, group in enumerate(groups):
+        at = slice(c * step, (c + 1) * step)
+        _wait_group(group)
+        acc[:, at] = _dot(left_s[...], right_s[:, at], TN).astype(acc.dtype)
+    if split:
+        _split_rows(acc, y_ref[0], *outs)
+
+
+def row_grads(left, right, name, y=None, size=128):
+    n, depth = len(left), left[0].shape[1]
+    rows = sum(v.shape[0] for v in left)
+    columns = right[0].shape[1]
+    step = min(columns, 1024)
+    block = 2 * size
+    split = y is not None
+    anywhere = pl.BlockSpec(memory_space=pl.ANY)
+    if split:
+        out = [jax.ShapeDtypeStruct((depth // block, size, columns), jnp.bfloat16)] * 2
+        out_spec = [pl.BlockSpec((1, size, columns), lambda i: (i, 0, 0))] * 2
+    else:
+        out = jax.ShapeDtypeStruct((depth, columns), jnp.bfloat16)
+        out_spec = _rows(block, columns)
+    return pl.pallas_call(
+        functools.partial(_grad_kernel, n, step, split),
+        grid=(depth // block,),
+        out_shape=out,
+        in_specs=[_smem()] * split
+        + [pl.BlockSpec((v.shape[0], block), lambda i: (0, i)) for v in left]
+        + [anywhere] * n,
+        out_specs=out_spec,
+        scratch_shapes=[
+            pltpu.VMEM((rows, block), jnp.bfloat16),
+            pltpu.VMEM((rows, columns), jnp.bfloat16),
+            pltpu.SemaphoreType.DMA((n * (columns // step),)),
+        ]
+        + [pltpu.VMEM((block, columns), jnp.float32)] * split,
+        compiler_params=_params(),
+        cost_estimate=_cost(2 * rows * depth * columns, 2 * rows * (depth + columns) + 2 * depth * columns),
+        name=name,
+    )(*([y] * split), *left, *right)
+
+
+def _qkv_grad_kernel(n, y_ref, *refs):
+    left, right = refs[:n], refs[n : 2 * n]
+    w_ref, gain_ref, row_ref, near, far, left_s, right_s, acc, sems = refs[2 * n :]
+    columns = right_s.shape[1]
+    groups = _pull_groups(right, right_s, 0, 0, columns, sems, 0)
+    _start_all(groups)
+    _join(left, left_s)
+    _wait_group(groups[0])
+    total = _dot(left_s[...], right_s[...], TN)
+    acc[:, :columns] = total
+    row = jnp.concatenate(
+        [1.0 / gain_ref[...], row_ref[...], jnp.zeros((SEG - 9, row_ref.shape[1]), jnp.float32)], axis=0
+    ).T
+    attn = jnp.sum(total * w_ref[...].astype(jnp.float32), axis=-1, keepdims=True) * row[:, 0:1]
+    lane = lax.broadcasted_iota(jnp.int32, row.shape, 1)
+    acc[:, columns:] = jnp.where(lane == 0, attn, row)
+    _split_rows(acc, y_ref[0], near, far)
+
+
+def qkv_grads(y, normed, grads, weight, gain, mlp_sum, size):
+    n, depth = len(normed), normed[0].shape[1]
+    rows = sum(v.shape[0] for v in normed)
+    columns = grads[0].shape[1]
+    block = 2 * size
+    anywhere = pl.BlockSpec(memory_space=pl.ANY)
+    out = jax.ShapeDtypeStruct((depth // block, size, columns + SEG), jnp.bfloat16)
+    out_spec = pl.BlockSpec((1, size, columns + SEG), lambda i: (i, 0, 0))
+    lanes = lambda r: pl.BlockSpec((r, block), lambda i: (0, i))
+    return pl.pallas_call(
+        functools.partial(_qkv_grad_kernel, n),
+        grid=(depth // block,),
+        out_shape=[out, out],
+        in_specs=[_smem()]
+        + [lanes(v.shape[0]) for v in normed]
+        + [anywhere] * n
+        + [_rows(block, columns), lanes(1), lanes(8)],
+        out_specs=[out_spec, out_spec],
+        scratch_shapes=[
+            pltpu.VMEM((rows, block), jnp.bfloat16),
+            pltpu.VMEM((rows, columns), jnp.bfloat16),
+            pltpu.VMEM((block, columns + SEG), jnp.float32),
+            pltpu.SemaphoreType.DMA((n,)),
+        ],
+        compiler_params=_params(),
+        cost_estimate=_cost(2 * rows * depth * columns, 2 * rows * (depth + columns) + 2 * depth * columns),
+        name="qkv_grads",
+    )(y, *normed, *grads, weight, gain, mlp_sum)
+
+
+def _out_grad_kernel(y_ref, left_ref, a0, a1, a2, a3, near, far, right_s, acc):
+    width = a0.shape[2]
+
+    @pl.when(pl.program_id(0) == 0)
+    def _():
+        for i, a in enumerate((a0, a1, a2, a3)):
+            right_s[:, i * width : (i + 1) * width] = a[0]
+
+    acc[...] = _dot(left_ref[...], right_s[...], TN)
+    _split_rows(acc, y_ref[0], near, far)
+
+
+def out_grads(y, left, attended, size):
+    rows, depth = left.shape
+    width = attended[0][0].shape[2]
+    block = 2 * size
+    out = jax.ShapeDtypeStruct((depth // block, size, 4 * width), jnp.bfloat16)
+    out_spec = pl.BlockSpec((1, size, 4 * width), lambda i: (i, 0, 0))
+    member = lambda n: pl.BlockSpec((1, rows, width), lambda i: (n, 0, 0))
+    return pl.pallas_call(
+        _out_grad_kernel,
+        grid=(depth // block,),
+        out_shape=[out, out],
+        in_specs=[_smem(), pl.BlockSpec((rows, block), lambda i: (0, i))]
+        + [member(n) for v, n in attended],
+        out_specs=[out_spec, out_spec],
+        scratch_shapes=[
+            pltpu.VMEM((rows, 4 * width), jnp.bfloat16),
+            pltpu.VMEM((block, 4 * width), jnp.float32),
+        ],
+        compiler_params=_params(),
+        cost_estimate=_cost(8 * rows * depth * width, 2 * rows * (depth + 4 * width) + 8 * depth * width),
+        name="out_grads",
+    )(y, left, *[v for v, n in attended])
+
+
+def _fold_kernel(z_ref, near, passed, *outs):
+    count = near.shape[0]
+    for step, out in enumerate(outs):
+        row = lax.rem(z_ref[0] + step, count)
+        out[...] = (near[row].astype(jnp.float32) + passed[row].astype(jnp.float32)).astype(out.dtype)
+
+
+def fold(z, near, passed):
+    count, size, columns = near.shape
+    return pl.pallas_call(
+        _fold_kernel,
+        grid=(1,),
+        out_shape=[jax.ShapeDtypeStruct((size, columns), jnp.bfloat16)] * count,
+        in_specs=[_smem(), _full(near.shape), _full(near.shape)],
+        out_specs=[_full((size, columns))] * count,
+        compiler_params=_params(),
+        cost_estimate=_cost(0, 6 * count * size * columns),
+        name="fold",
+    )(z, near, passed)
+
+
+def _mid_kernel(p0, p1, p2, res_ref, cot_ref, gain_ref, near_ref, mate_ref, mid_ref, attn_ref, a0, a1, a2, a3, sum_ref):
+    width = a0.shape[1]
+    grad = p0[...].astype(jnp.float32) + p1[...].astype(jnp.float32) + p2[...].astype(jnp.float32)
+    inverse, normed = _normed(res_ref[...])
+    term = jnp.sum(grad * normed, axis=0, keepdims=True)
+
+    @pl.when(pl.program_id(0) == 0)
+    def _():
+        sum_ref[...] = jnp.zeros_like(sum_ref)
+
+    sum_ref[0:1, :] += term
+    scaled = grad * gain_ref[...]
+    mid = cot_ref[...] + inverse * (scaled - normed * jnp.mean(scaled * normed, axis=-1, keepdims=True))
+    mid_ref[...] = mid
+    low = mid.astype(jnp.bfloat16)
+    attn_ref[...] = low
+    a0[...] = _dot(low, near_ref[:, :width], NN).astype(jnp.bfloat16)
+    a1[...] = _dot(low, mate_ref[:, :width], NN).astype(jnp.bfloat16)
+    a2[...] = _dot(low, near_ref[:, width : 2 * width], NN).astype(jnp.bfloat16)
+    a3[...] = _dot(low, mate_ref[:, width:], NN).astype(jnp.bfloat16)
+
+
+def middle(parts, residual, cot, gain, weights, out_mate):
+    rows, depth = residual.shape
+    width = out_mate.shape[1] // 2
+    tile = _row_tile(rows)
+    return pl.pallas_call(
+        _mid_kernel,
+        grid=(rows // tile,),
+        out_shape=[
+            jax.ShapeDtypeStruct((rows, depth), jnp.float32),
+            jax.ShapeDtypeStruct((rows, depth), jnp.bfloat16),
+        ]
+        + [jax.ShapeDtypeStruct((rows, width), jnp.bfloat16)] * 4
+        + [jax.ShapeDtypeStruct((8, depth), jnp.float32)],
+        in_specs=[_rows(tile, depth)] * 5
+        + [
+            _full((1, depth)),
+            pl.BlockSpec((depth, 2 * width), lambda i: (0, weights.shape[1] // (2 * width) - 1)),
+            _full(out_mate.shape),
+        ],
+        out_specs=[_rows(tile, depth)] * 2 + [_rows(tile, width)] * 4 + [_full((8, depth))],
+        compiler_params=_params(),
+        cost_estimate=_cost(2 * rows * depth * 4 * width, rows * depth * 20),
+        name="middle",
+    )(*parts, residual, cot, gain, weights, out_mate)
+
+
+def _back_kernel(add, grad_ref, w_ref, *refs):
+    part = _dot(grad_ref[...], w_ref[...], NT)
+    if add:
+        part = part + refs[0][...].astype(jnp.float32)
+    refs[-1][...] = part.astype(refs[-1].dtype)
+
+
+def project_back(grad, weight, add=None):
+    rows, columns = grad.shape
+    depth = weight.shape[0]
+    tile = _row_tile(rows)
+    extra = [] if add is None else [add]
+    return pl.pallas_call(
+        functools.partial(_back_kernel, add is not None),
+        grid=(rows // tile,),
+        out_shape=jax.ShapeDtypeStruct((rows, depth), jnp.bfloat16),
+        in_specs=[_rows(tile, columns), _full((depth, columns))] + [_rows(tile, depth)] * len(extra),
+        out_specs=_rows(tile, depth),
+        compiler_params=_params(),
+        cost_estimate=_cost(2 * rows * depth * columns, 2 * rows * (columns + 2 * depth)),
+        name="project_back",
+    )(grad, weight, *extra)
+
+
+def _last_kernel(p0, p1, p2, x_ref, mid_ref, gain_ref, out_ref):
+    grad = p0[...].astype(jnp.float32) + p1[...].astype(jnp.float32) + p2[...].astype(jnp.float32)
+    inverse, normed = _normed(x_ref[...].astype(jnp.float32))
+    scaled = grad * gain_ref[...]
+    out_ref[...] = mid_ref[...] + inverse * (
+        scaled - normed * jnp.mean(scaled * normed, axis=-1, keepdims=True)
+    )
+
+
+def last(parts, x, mid, gain):
+    rows, depth = x.shape
+    tile = _row_tile(rows)
+    return pl.pallas_call(
+        _last_kernel,
+        grid=(rows // tile,),
+        out_shape=jax.ShapeDtypeStruct((rows, depth), jnp.float32),
+        in_specs=[_rows(tile, depth)] * 5 + [_full((1, depth))],
+        out_specs=_rows(tile, depth),
+        compiler_params=_params(),
+        cost_estimate=_cost(0, rows * depth * 16),
+        name="last",
+    )(*parts, x, mid, gain)
+
+
+def _half_place(info_ref, b, half, piece_blocks):
+    block = 2 * b + half
+    piece = lax.bitwise_xor(lax.div(block, piece_blocks), info_ref[0])
+    return piece, lax.rem(block, piece_blocks) * SEG
+
+
+def _mask(heads, same, causal):
+    key = lax.broadcasted_iota(jnp.int32, (QB, heads * QB), 0)
+    query = lax.broadcasted_iota(jnp.int32, (QB, heads * QB), 1) % QB
+    allowed = jnp.logical_not(same & ((key // SEG) != (query // SEG)))
+    if causal:
+        allowed = allowed & (key <= query)
+    return allowed
+
+
+def _spread(block, heads):
+    turned = block.T
+    lane = lax.broadcasted_iota(jnp.int32, turned.shape, 0) // HDIM
+    zero = jnp.zeros_like(turned)
+    return jnp.concatenate([jnp.where(lane == h, turned, zero) for h in range(heads)], axis=1)
+
+
+def _stack(block, heads):
+    lane = lax.broadcasted_iota(jnp.int32, block.shape, 1) // HDIM
+    zero = jnp.zeros_like(block)
+    return jnp.concatenate([jnp.where(lane == h, block, zero) for h in range(heads)], axis=0)
+
+
+def _parents(info_ref, b):
+    leaf = 2 * (b - (TRUNK + 4 * SEG) // QB)
+    return [pl.multiple_of(TRUNK - SEG + SEG * info_ref[2 + leaf + side], SEG) for side in (0, 1)]
+
+
+def _attn_fwd_kernel(heads, piece_count, info_ref, *refs):
+    pieces = refs[:piece_count]
+    out_ref, lse_ref = refs[piece_count : piece_count + 2]
+    q_s, k_s, vt_s, qt_s, s_s, p_s, m_s, l_s, acc_s, kp_s, vp_s = refs[piece_count + 2 :]
+    width = heads * HDIM
+    piece_rows = pieces[0].shape[0]
+    tensor = info_ref[0]
+    base = info_ref[1]
+    trunk_blocks = TRUNK // QB
+    leaf_block = (TRUNK + 4 * SEG) // QB
+    for j in range(piece_count):
+        at = pl.multiple_of(piece_rows * lax.bitwise_xor(tensor, j), SEG)
+        q_s[pl.ds(at, piece_rows), :] = pieces[j][:, :width] * jnp.asarray(HDIM**-0.5, jnp.bfloat16)
+        k_s[pl.ds(at, piece_rows), :] = pieces[j][:, width : 2 * width]
+        vt_s[:, pl.ds(at, piece_rows)] = pieces[j][:, 2 * width :].T
+
+    def q_block(i, carry):
+        b = base + i
+        row = pl.multiple_of(b * QB, QB)
+        own = pl.ds(row, QB)
+        leaf = b >= leaf_block
+        qt_s[...] = _spread(q_s[own, :], heads)
+
+        def score(keys, at, size, allowed):
+            scores = _dot(keys, qt_s[...], NN)
+            if allowed is not None:
+                scores = jnp.where(allowed, scores, -1e30)
+            s_s[pl.ds(at, size), :] = scores
+            return jnp.max(scores, axis=0, keepdims=True)
+
+        m_s[0:1, :] = score(k_s[own, :], TRUNK, QB, _mask(heads, b >= trunk_blocks, True))
+
+        @pl.when(leaf)
+        def _():
+            for side, at in enumerate(_parents(info_ref, b)):
+                kp_s[side * SEG : (side + 1) * SEG, :] = k_s[pl.ds(at, SEG), :]
+                vp_s[:, side * SEG : (side + 1) * SEG] = vt_s[:, pl.ds(at, SEG)]
+            top = score(kp_s[...], TRUNK + QB, QB, _mask(heads, True, False))
+            m_s[0:1, :] = jnp.maximum(m_s[0:1, :], top)
+
+        @pl.when(b >= trunk_blocks)
+        def _():
+            m_s[0:1, :] = jnp.maximum(m_s[0:1, :], score(k_s[:TRUNK, :], 0, TRUNK, None))
+
+        @pl.when(b < trunk_blocks)
+        def _():
+            def chunk(c, carry):
+                at = pl.multiple_of(c * QB, QB)
+                m_s[0:1, :] = jnp.maximum(m_s[0:1, :], score(k_s[pl.ds(at, QB), :], at, QB, None))
+                return carry
+
+            lax.fori_loop(0, b, chunk, 0)
+
+        def mix(values, at, size, fresh):
+            probs = jnp.exp(s_s[pl.ds(at, size), :] - m_s[0:1, :])
+            total = jnp.sum(probs, axis=0, keepdims=True)
+            p_s[pl.ds(at, size), :] = probs.astype(jnp.bfloat16)
+            l_s[0:1, :] = total if fresh else l_s[0:1, :] + total
+            for h in range(heads):
+                of = slice(h * HDIM, (h + 1) * HDIM)
+                term = _dot(values(of), p_s[pl.ds(at, size), h * QB : (h + 1) * QB], NN)
+                acc_s[of, :] = term if fresh else acc_s[of, :] + term
+
+        mix(lambda of: vt_s[of, own], TRUNK, QB, True)
+
+        @pl.when(leaf)
+        def _():
+            mix(lambda of: vp_s[of, :], TRUNK + QB, QB, False)
+
+        @pl.when(b >= trunk_blocks)
+        def _():
+            mix(lambda of: vt_s[of, :TRUNK], 0, TRUNK, False)
+
+        @pl.when(b < trunk_blocks)
+        def _():
+            def chunk(c, carry):
+                at = pl.multiple_of(c * QB, QB)
+                mix(lambda of: vt_s[of, pl.ds(at, QB)], at, QB, False)
+                return carry
+
+            lax.fori_loop(0, b, chunk, 0)
+
+        mixed = []
+        for h in range(heads):
+            columns = slice(h * QB, (h + 1) * QB)
+            total = l_s[0:1, columns]
+            lse_ref[h : h + 1, pl.ds(pl.multiple_of(i * QB, QB), QB)] = m_s[0:1, columns] + jnp.log(total)
+            mixed.append(acc_s[h * HDIM : (h + 1) * HDIM, :] / total)
+        mixed = jnp.concatenate(mixed, axis=0).T.astype(jnp.bfloat16)
+        for half in (0, 1):
+            piece, at = _half_place(info_ref, b, half, piece_rows // SEG)
+            at = pl.multiple_of(at, SEG)
+            out_ref[lax.bitwise_and(piece, 1), pl.ds(at, SEG), :] = mixed[half * SEG : (half + 1) * SEG]
+        return carry
+
+    lax.fori_loop(0, lse_ref.shape[1] // QB, q_block, 0)
+
+
+def attention_forward(info, pieces, heads):
+    rows = sum(p.shape[0] for p in pieces)
+    piece_rows = pieces[0].shape[0]
+    width = heads * HDIM
+    half = rows // 2
+    bf16, f32 = jnp.bfloat16, jnp.float32
+    return pl.pallas_call(
+        functools.partial(_attn_fwd_kernel, heads, len(pieces)),
+        out_shape=[
+            jax.ShapeDtypeStruct((2, piece_rows, width), bf16),
+            jax.ShapeDtypeStruct((8, half), f32),
+        ],
+        grid=(1,),
+        in_specs=[_smem()] + [_full(p.shape) for p in pieces],
+        out_specs=[_full((2, piece_rows, width)), _full((8, half))],
+        scratch_shapes=[
+            pltpu.VMEM((rows, width), bf16),
+            pltpu.VMEM((rows, width), bf16),
+            pltpu.VMEM((width, rows), bf16),
+            pltpu.VMEM((width, heads * QB), bf16),
+            pltpu.VMEM((TRUNK + 2 * QB, heads * QB), f32),
+            pltpu.VMEM((TRUNK + 2 * QB, heads * QB), bf16),
+            pltpu.VMEM((8, heads * QB), f32),
+            pltpu.VMEM((8, heads * QB), f32),
+            pltpu.VMEM((width, QB), f32),
+            pltpu.VMEM((QB, width), bf16),
+            pltpu.VMEM((width, QB), bf16),
+        ],
+        compiler_params=_params(),
+        cost_estimate=_cost(rows * 1400 * width * 4, rows * width * 8),
+        name="attn_fwd",
+    )(info, *pieces)
+
+
+def _attn_bwd_kernel(heads, info_ref, *refs):
+    n = 4
+    pieces, mixed_in, grads = refs[:n], refs[n : n + 2], refs[n + 2 : 2 * n + 2]
+    lse_refs = refs[2 * n + 2 : 2 * n + 4]
+    outs = refs[2 * n + 4 : 3 * n + 4]
+    q_s, k_s, kt_s, v_s, o_s, g_s, dk_s, dv_s, lse_s = refs[3 * n + 4 : 3 * n + 13]
+    qt_s, gt_s, qm_s, gm_s, row_s, delta_s, acc_s, kp_s, vp_s, kpt_s = refs[3 * n + 13 :]
+    width = heads * HDIM
+    piece_rows = pieces[0].shape[0]
+    tensor = info_ref[0]
+    chip = lax.div(tensor, 2)
+    half_rows = lse_refs[0].shape[1]
+    scale = HDIM**-0.5
+    trunk_blocks = TRUNK // QB
+    leaf_block = (TRUNK + 4 * SEG) // QB
+    for j in range(n):
+        rows_at = pl.ds(pl.multiple_of(piece_rows * lax.bitwise_xor(tensor, j), SEG), piece_rows)
+        q_s[rows_at, :] = pieces[j][:, :width] * jnp.asarray(scale, jnp.bfloat16)
+        k_s[rows_at, :] = pieces[j][:, width : 2 * width]
+        kt_s[:, rows_at] = pieces[j][:, width : 2 * width].T
+        v_s[rows_at, :] = pieces[j][:, 2 * width :]
+        o_s[rows_at, :] = mixed_in[j // 2][j % 2]
+        g_s[rows_at, :] = grads[j][...]
+    lse_s[:, pl.ds(pl.multiple_of(chip * half_rows, SEG), half_rows)] = lse_refs[0][...]
+    lse_s[:, pl.ds(pl.multiple_of((1 - chip) * half_rows, SEG), half_rows)] = lse_refs[1][...]
+    dk_s[...] = jnp.zeros_like(dk_s)
+    dv_s[...] = jnp.zeros_like(dv_s)
+    head_of_lane = lax.broadcasted_iota(jnp.int32, (8, width), 1) // HDIM
+    pick = jnp.where(lax.broadcasted_iota(jnp.int32, (8, width), 0) == head_of_lane, 1.0, 0.0)
+
+    def q_block(b, carry):
+        row = pl.multiple_of(b * QB, QB)
+        own = pl.ds(row, QB)
+        both = o_s[own, :].astype(jnp.float32) * g_s[own, :].astype(jnp.float32)
+        delta = lax.dot_general(
+            pick, both, NT, precision=lax.Precision.HIGHEST, preferred_element_type=jnp.float32
+        )
+        for h in range(heads):
+            columns = slice(h * QB, (h + 1) * QB)
+            delta_s[0:1, columns] = delta[h : h + 1, :]
+            row_s[0:1, columns] = lse_s[h : h + 1, own]
+        qt_s[...] = _spread(q_s[own, :], heads)
+        gt_s[...] = _spread(g_s[own, :], heads)
+        qm_s[...] = _stack(q_s[own, :], heads)
+        gm_s[...] = _stack(g_s[own, :], heads)
+
+        def step(k, v, kt, allowed, fresh, targets):
+            scores = _dot(k, qt_s[...], NN)
+            probs_grad = _dot(v, gt_s[...], NN)
+            probs = jnp.exp(scores - row_s[0:1, :])
+            if allowed is not None:
+                probs = jnp.where(allowed, probs, 0.0)
+            ds = (probs * (probs_grad - delta_s[0:1, :])).astype(jnp.bfloat16)
+            dv = _dot(probs.astype(jnp.bfloat16), gm_s[...], NN)
+            dk = _dot(ds, qm_s[...], NN)
+            for h in range(heads):
+                of = slice(h * HDIM, (h + 1) * HDIM)
+                term = _dot(kt(of), ds[:, h * QB : (h + 1) * QB], NN)
+                acc_s[of, :] = term if fresh else acc_s[of, :] + term
+            first = 0
+            for at, size in targets:
+                dv_s[pl.ds(at, size), :] += dv[first : first + size]
+                dk_s[pl.ds(at, size), :] += dk[first : first + size]
+                first += size
+
+        step(
+            k_s[own, :], v_s[own, :], lambda of: kt_s[of, own],
+            _mask(heads, b >= trunk_blocks, True), True, [(row, QB)],
+        )
+
+        @pl.when(b >= leaf_block)
+        def _():
+            ats = _parents(info_ref, b)
+            for side, at in enumerate(ats):
+                part = slice(side * SEG, (side + 1) * SEG)
+                kp_s[part, :] = k_s[pl.ds(at, SEG), :]
+                vp_s[part, :] = v_s[pl.ds(at, SEG), :]
+                kpt_s[:, part] = kt_s[:, pl.ds(at, SEG)]
+            step(
+                kp_s[...], vp_s[...], lambda of: kpt_s[of, :],
+                _mask(heads, True, False), False, [(at, SEG) for at in ats],
+            )
+
+        def trunk_chunk(c, carry):
+            at = pl.multiple_of(c * QB, QB)
+            here = pl.ds(at, QB)
+            step(k_s[here, :], v_s[here, :], lambda of: kt_s[of, here], None, False, [(at, QB)])
+            return carry
+
+        lax.fori_loop(0, jnp.minimum(b, trunk_blocks), trunk_chunk, 0)
+        q_s[own, :] = (acc_s[...] * scale).T.astype(jnp.bfloat16)
+        return carry
+
+    lax.fori_loop(0, q_s.shape[0] // QB, q_block, 0)
+    for j in range(n):
+        rows_at = pl.ds(pl.multiple_of(piece_rows * lax.bitwise_xor(tensor, j), SEG), piece_rows)
+        outs[j][:, :width] = q_s[rows_at, :]
+        outs[j][:, width : 2 * width] = dk_s[rows_at, :].astype(jnp.bfloat16)
+        outs[j][:, 2 * width :] = dv_s[rows_at, :].astype(jnp.bfloat16)
+
+
+def attention_backward(info, pieces, mixed, grads, lses, heads):
+    n = len(pieces)
+    piece_rows = pieces[0].shape[0]
+    rows = n * piece_rows
+    width = heads * HDIM
+    bf16, f32 = jnp.bfloat16, jnp.float32
+    rows_low = pltpu.VMEM((rows, width), bf16)
+    return pl.pallas_call(
+        functools.partial(_attn_bwd_kernel, heads),
+        out_shape=[jax.ShapeDtypeStruct((piece_rows, 3 * width), bf16)] * n,
+        grid=(1,),
+        in_specs=[_smem()] + [_full(v.shape) for v in (*pieces, *mixed, *grads, *lses)],
+        out_specs=[_full((piece_rows, 3 * width))] * n,
+        scratch_shapes=[
+            rows_low,
+            rows_low,
+            pltpu.VMEM((width, rows), bf16),
+            rows_low,
+            rows_low,
+            rows_low,
+            pltpu.VMEM((rows, width), f32),
+            pltpu.VMEM((rows, width), f32),
+            pltpu.VMEM((8, rows), f32),
+            pltpu.VMEM((width, heads * QB), bf16),
+            pltpu.VMEM((width, heads * QB), bf16),
+            pltpu.VMEM((heads * QB, width), bf16),
+            pltpu.VMEM((heads * QB, width), bf16),
+            pltpu.VMEM((8, heads * QB), f32),
+            pltpu.VMEM((8, heads * QB), f32),
+            pltpu.VMEM((width, QB), f32),
+            pltpu.VMEM((QB, width), bf16),
+            pltpu.VMEM((QB, width), bf16),
+            pltpu.VMEM((width, QB), bf16),
+        ],
+        compiler_params=_params(),
+        cost_estimate=_cost(rows * 1400 * width * 20, rows * width * 16),
+        name="attn_bwd",
+    )(info, *pieces, *mixed, *grads, *lses)
+
+
+def mate(x):
+    return lax.ppermute(x, "tensor", [(i, i ^ 1) for i in range(4)])
+
+
+def across(x):
+    return lax.ppermute(x, "tensor", [(i, i ^ 2) for i in range(4)])
+
+
+def corner(x):
+    return lax.ppermute(x, "tensor", [(i, i ^ 3) for i in range(4)])
+
+
+def beside(x):
+    return lax.ppermute(x, "dp", [(i, i ^ 1) for i in range(8)])
+
+
+def ahead(x, step):
+    return lax.ppermute(x, "dp", [(i, (i + 2 * step) % 8) for i in range(8)])
+
+
+def after(x, *others):
+    return lax.optimization_barrier((x, *others))[0]
+
+
+def after_all(values, *others):
+    return list(lax.optimization_barrier((*values, *others))[: len(values)])
+
+
+def line_hops(x):
+    return [x] + [ahead(x, step) for step in (1, 3, 2)]
+
+
+def spread_hops(line, far):
+    dp = lax.axis_index("dp")
+    z, y = dp // 2, dp % 2
+    order = jnp.array([0, 1, 3, 2], jnp.int32)
+    from_z = (z - order) % 4
+    where = jnp.concatenate([2 * from_z + y, 2 * from_z + 1 - y]).astype(jnp.int32)
+    return place(where, line + far)
+
+
+def fold_hops(near, passed):
+    z = (lax.axis_index("dp") // 2).astype(jnp.int32)[None]
+    return fold(z, near, passed)
+
+
+def send_hops(chunks):
+    return [chunks[0]] + [ahead(chunks[step], step) for step in (2, 1, 3)]
+
+
+def sum_hops(received):
+    return sum(v.astype(jnp.float32) for v in received)
+
+
+def body(
+    block_input,
+    norm_gains,
+    qkv_weight,
+    out_weight,
+    gate_up_weight,
+    down_weight,
+    parent_of_row,
+    cotangent,
+):
+    bf16, f32 = jnp.bfloat16, jnp.float32
+    shard = qkv_weight.shape[1]
+    width = qkv_weight.shape[2]
+    hidden_width = gate_up_weight.shape[2]
+    heads = width // HDIM
+    rows = parent_of_row.shape[0]
+    tensor = lax.axis_index("tensor")
+    chip = tensor // 2
+    y = (lax.axis_index("dp") % 2).astype(jnp.int32)[None]
+    leaf_first = TRUNK + 4 * SEG
+    parents = parent_of_row[leaf_first::SEG]
+    half_blocks = rows // (2 * QB)
+    place_own = jnp.stack([tensor, half_blocks * chip]).astype(jnp.int32)
+    place_far = jnp.stack([tensor, half_blocks * (1 - chip)]).astype(jnp.int32)
+    info_own = jnp.concatenate([place_own, parents])
+    info_far = jnp.concatenate([place_far, parents])
+
+    half = block_input.shape[0] // 2
+    gains_shard = jnp.pad(norm_gains.astype(bf16).T, ((0, 0), (0, SEG - 2)))
+    qkv_shard = qkv_weight.astype(bf16).transpose(1, 0, 2).reshape(shard, 3 * width)
+    out_shard = out_weight.astype(bf16).T
+    gate_up_shard = gate_up_weight.astype(bf16).transpose(1, 0, 2).reshape(shard, 2 * hidden_width)
+    first_line = line_hops(jnp.concatenate([qkv_shard, gains_shard], axis=1))
+    beyond = [across(block_input[:half])]
+    rest_shard = jnp.concatenate([gate_up_shard, out_shard, across(out_shard)], axis=1)
+    rest = lax.all_gather(after(rest_shard, *first_line), "dp", axis=0, tiled=True)
+    first_far = [beside(first_line[0])] + [beside(after(v, beyond[0])) for v in first_line[1:]]
+    beyond.append(across(after(block_input[half:], beyond[0])))
+    near_x = mate(block_input)
+    first = spread_hops(first_line, first_far)
+    down_line = line_hops(after(down_weight.astype(bf16).T, *first_far))
+    gains_low = first[:, 3 * width : 3 * width + 2].T.astype(f32)
+    gain_attn, gain_mlp = gains_low[0:1], gains_low[1:2]
+    n0, n1, p0, p1 = project(block_input, near_x, gain_attn, first, 3 * width)
+    beyond = jnp.concatenate([beyond[0], beyond[1]], axis=0)
+    inputs = [block_input, near_x, beyond, mate(beyond)]
+    n2, n3, p2, p3 = project(inputs[2], after(inputs[3], p1), gain_attn, first, 3 * width)
+    normed_attn, projected = [n0, n1, n2, n3], [p0, p1, p2, p3]
+    cot_low = cotangent.astype(bf16)
+    cot_x = across(after(cot_low, beyond))
+
+    own, lse_own = attention_forward(info_own, projected, heads)
+    own_x, own_m = across(after(own, cot_x)), mate(own)
+    down_far = [beside(after(v, own)) for v in down_line]
+    cot_near = mate(after(cot_low, own))
+    far, lse_far = attention_forward(after(info_far, own), projected, heads)
+    far_m, own_xm = mate(far), mate(after(own_x, far))
+    far_x = across(after(far, own_x))
+    down_low = spread_hops(down_line, after_all(down_far, far))
+    cot_rows = [cot_low, cot_near, cot_x, mate(after(cot_x, far))]
+    out_far = mate(after(rest[:, 2 * hidden_width :], down_low))
+
+    def run_mlp(attended, j, cot):
+        return mlp(attended, inputs[j], cot, gain_mlp, rest, down_low, out_far, j == 0)
+
+    stage = [None] * 4
+    stage[3] = run_mlp([(far, 1), (far_m, 0), (own_x, 1), (own_xm, 0)], 3, cot_rows[3])
+    stage[2] = run_mlp(
+        [(far, 0), (far_m, 1), (own_x, 0), (own_xm, 1)], 2, after(cot_rows[2], stage[3][0])
+    )
+    far_xm = mate(after(far_x, stage[3][0]))
+    passed = (stage[2][0].astype(f32) + mate(stage[3][0]).astype(f32)).astype(bf16)
+    passed_x = [across(passed[:half])]
+    stage[1] = run_mlp(
+        [(own, 1), (own_m, 0), (far_x, 1), (far_xm, 0)], 1, after(cot_rows[1], passed)
+    )
+    passed_x.append(across(after(passed[half:], passed_x[0])))
+    own_rows = [(own, 0), (own_m, 1), (far_x, 0), (far_xm, 1)]
+    stage[0] = run_mlp(own_rows, 0, after(cot_rows[0], stage[1][0], passed_x[0]))
+    part, hidden, grads_low, normed_mlp, branch = [[s[n] for s in stage] for n in range(5)]
+    residual_mid = stage[0][5]
+    mlp_parts = [part[0], mate(part[1]), jnp.concatenate(passed_x, axis=0)]
+
+    mid_grad, attn_grad, g0, g1, g2, g3, mlp_sum = middle(
+        mlp_parts, residual_mid, cotangent, gain_mlp, rest, out_far
+    )
+    g_x, g_c, g_m = across(g2), corner(g3), mate(g1)
+    down_pair = row_grads([after(cot_low, attn_grad), *cot_rows[1:]], hidden, "down_grads", y, shard)
+    down_y = beside(down_pair[1])
+    gate_up_grad = row_grads(
+        [after(normed_mlp[0], down_pair[1]), *normed_mlp[1:]], grads_low, "gate_up_grads"
+    )
+    gate_up_sum = lax.psum_scatter(gate_up_grad, "dp", scatter_dimension=0, tiled=True)
+    down_chunks = fold_hops(down_pair[0], after(down_y, gate_up_grad))
+    branch_passed = (branch[2].astype(f32) + mate(branch[3]).astype(f32)).astype(bf16)
+    out_pair = out_grads(y, after(attn_grad, down_chunks[1]), own_rows, shard)
+    out_y = beside(out_pair[1])
+    branch_x = across(after(branch_passed, g_x, g_c))
+
+    bwd_grads = after_all([g0, g_m, g_x, g_c], out_pair[1], branch_passed)
+    projected_grad = attention_backward(
+        info_own, projected, [own, far], bwd_grads, [lse_own, lse_far], heads
+    )
+    out_chunks = fold_hops(out_pair[0], after(out_y, *projected_grad))
+    out_received = send_hops(out_chunks)
+    down_received = send_hops(down_chunks)
+    qkv_pair = qkv_grads(
+        y, [after(normed_attn[0], out_chunks[1]), *normed_attn[1:]], projected_grad, first, gain_attn, mlp_sum, shard
+    )
+    qkv_y = beside(qkv_pair[1])
+    back3 = project_back(after(projected_grad[3], qkv_pair[1], branch_x), first)
+    back2 = project_back(projected_grad[2], first, mate(back3))
+    back_x = [across(back2[:half])]
+    back1 = project_back(after(projected_grad[1], back2, *out_received), first)
+    back_m = mate(back1)
+    back0 = project_back(after(projected_grad[0], back1), first)
+    back_x.append(across(after(back2[half:], back_x[0])))
+    branch_sum = branch[0].astype(f32) + mate(branch[1]).astype(f32)
+    block_output = residual_mid + branch_sum + after(branch_x, back0).astype(f32)
+    qkv_chunks = fold_hops(qkv_pair[0], after(qkv_y, back_x[0], block_output))
+    qkv_received = send_hops(qkv_chunks)
+    down_out = sum_hops(after_all(down_received, qkv_chunks[1])).T
+    gate_up_out = (
+        after(gate_up_sum, qkv_chunks[1]).astype(f32).reshape(shard, 2, hidden_width).transpose(1, 0, 2)
+    )
+    out_sum = sum_hops(after_all(out_received, qkv_chunks[1]))
+    quarter = lambda i: out_sum[:, i * width : (i + 1) * width]
+    from_mate = mate(jnp.concatenate([quarter(1), quarter(3)], axis=1).astype(bf16)).astype(f32)
+    out_out = quarter(0) + from_mate[:, :width]
+    out_x = across((quarter(2) + from_mate[:, width:]).astype(bf16))
+    out_out = (out_out + out_x.astype(f32)).T
+    back_x = jnp.concatenate([back_x[0], after(back_x[1], out_x, gate_up_out, down_out)], axis=0)
+    input_grad = last([back0, back_m, back_x], block_input, mid_grad, gain_attn)
+    qkv_sum = sum_hops(after_all(qkv_received, input_grad))
+    qkv_out = qkv_sum[:, : 3 * width].reshape(shard, 3, width).transpose(1, 0, 2)
+    gains_out = qkv_sum[:, 3 * width :]
+    gains_out = gains_out + mate(gains_out.astype(bf16)).astype(f32)
+    gains_out = (gains_out + across(gains_out.astype(bf16)).astype(f32))[:, :2].T
+    return (block_output, input_grad, gains_out, qkv_out, out_out, gate_up_out, down_out)
+
+
 def solution(mesh):
     placed = (
         P(("dp", "tensor"), None),
@@ -249,8 +1260,9 @@
         P("dp"),
         P(("dp", "tensor"), None),
     )
+    four_by_eight = mesh.shape["tensor"] == 4 and mesh.shape["dp"] == 8
     return jax.shard_map(
-        body,
+        body if four_by_eight else body_any_mesh,
         mesh=mesh,
         in_specs=placed,
         out_specs=(

time: 1450 us -> 472 us (0.33)
  waiting for transfers between devices: 593 us -> 83.3 us
  matrix products: 451 us -> 0 us
  Pallas kernels: 0 us -> 244 us
  other arithmetic: 204 us -> 20.2 us
  local copies, waits for them, and re-layouts: 112 us -> 24.8 us
  starting transfers between devices: 0.67 us -> 78.9 us
  blocking collectives: 57.7 us -> 0 us
    dot_general x47 -> x0, matrix products: 451 us -> none  [the longest x10 87.5 us: block_scores(): jnp.einsum('qhd,khd->hqk', query_block, key_rows, preferred_element_type=...]
    reduce_scatter x4 -> x1, waiting for transfers between devices: 260 us -> 0.02 us  [body(): lax.psum_scatter(gate_up_grad, 'dp', scatter_dimension=0, tiled=True)]
    pallas_call x0 -> x24, Pallas kernels: none -> 244 us  [the longest x4 65.4 us: mlp(): pl.pallas_call(functools.partial(_mlp_kernel, keep, step), grid=(rows //...]
    all_gather x7 -> x1, waiting for transfers between devices: 226 us -> 0.01 us  [body(): lax.all_gather(after(rest_shard, *first_line), 'dp', axis=0, tiled=True)]
    unnamed x21 -> x2, waiting for transfers between devices: 107 us -> 0.03 us
    convert_element_type x16 -> x8, other arithmetic: 97.3 us -> 7.72 us  [the longest x1 2.23 us: body(): (stage[2][0].astype(f32) + mate(stage[3][0]).astype(f32)).astype(bf16)]
    ppermute x0 -> x59, waiting for transfers between devices: none -> 83.2 us  [the longest x15 39.3 us: ahead(): return lax.ppermute(x, 'dp', [(i, (i + 2 * step) % 8) for i in range(8)])]
    ppermute x0 -> x59, starting transfers between devices: none -> 78.8 us  [the longest x15 43.8 us: ahead(): return lax.ppermute(x, 'dp', [(i, (i + 2 * step) % 8) for i in range(8)])]
  transfers between devices with their start and end apart: 16 -> 61, of which waited for: 11 -> 15; matrix products, arithmetic and copies ran while one was open for 36% -> 7% of each run, Pallas kernels for 0% -> 48%
where the time goes in v1:
time: 472 us; the launch traced here: 467 us
  Pallas kernels  244 us (52%)
  waiting for transfers between devices  83.3 us (18%)
  starting transfers between devices  78.9 us (17%)
  local copies, waits for them, and re-layouts  24.8 us (5%)
  other arithmetic  20.2 us (4%)
  between operations  15.1 us (3%)
    pallas_call x4, Pallas kernels, mlp(): pl.pallas_call(functools.partial(_mlp_kernel, keep, step), grid=(rows //...  65.4 us
    pallas_call x1, Pallas kernels, attention_backward(): pl.pallas_call(functools.partial(_attn_bwd_kernel, heads), out_shape=[jax...  45.4 us
    ppermute x15, starting transfers between devices, ahead(): return lax.ppermute(x, 'dp', [(i, (i + 2 * step) % 8) for i in range(8)])  43.8 us
    ppermute x15, waiting for transfers between devices, ahead(): return lax.ppermute(x, 'dp', [(i, (i + 2 * step) % 8) for i in range(8)])  39.3 us
    pallas_call x2, Pallas kernels, attention_forward(): pl.pallas_call(functools.partial(_attn_fwd_kernel, heads, len(pieces)), o...  31.1 us
    pallas_call x2, Pallas kernels, row_grads(): pl.pallas_call(functools.partial(_grad_kernel, n, step, split), grid=(dep...  29.4 us
    ppermute x14, waiting for transfers between devices, across(): return lax.ppermute(x, 'tensor', [(i, i ^ 2) for i in range(4)])  25.1 us
    ppermute x14, starting transfers between devices, across(): return lax.ppermute(x, 'tensor', [(i, i ^ 2) for i in range(4)])  17.9 us
  transfers between devices with their start and end apart: 61, of which 15 were waited for; matrix products, arithmetic and copies ran while one was open for 7% of the time, Pallas kernels for 48%

profile of v1, /device:TPU:0, one launch (start us, length us, event | category | flops | bytes accessed | tf_op | source)
XLA Modules:
  0.0 466.7 jit_solution(16144305685385209006)
XLA Ops:
  9.5 4.1 collective-permute-start.3
  17.4 2.6 collective-permute-done.18
  20.9 4.9 %collective-permute-done.3.refs_3_ = bf16[128,896]{1,0:T(8,128)(2,1)S(1)} collective-permute-done((bf16[128,896]{1,0:T(8,128)(2,1)S(1)}, bf16[128,896]{1,0:T(8,128)(2,1)S(1)}, u32[]{:S(2)}, u32[]{:S(2)}) %collective-permute-start.3) | collective-permute-done | bytes 229408 | tf_op jit(solution)/shard_map/ppermute | solution.py:1074
  25.9 4.4 collective-permute-done.1.refs_1_
  39.1 9.0 %collective-permute-done.5 = bf16[320,1024]{1,0:T(8,128)(2,1)} collective-permute-done((bf16[320,1024]{1,0:T(8,128)(2,1)}, bf16[320,1024]{1,0:T(8,128)(2,1)}, u32[]{:S(2)}, u32[]{:S(2)}) %collective-permute-start.5) | collective-permute-done | bytes 655392 | tf_op jit(solution)/shard_map/ppermute | solution.py:1062
  55.7 3.3 collective-permute-done.6.refs_5_
  59.0 4.9 %collective-permute-done.7.refs_6_ = bf16[128,896]{1,0:T(8,128)(2,1)S(1)} collective-permute-done((bf16[128,896]{1,0:T(8,128)(2,1)S(1)}, bf16[128,896]{1,0:T(8,128)(2,1)S(1)}, u32[]{:S(2)}, u32[]{:S(2)}) %collective-permute-start.7) | collective-permute-done | bytes 229408 | tf_op jit(solution)/shard_map/ppermute | solution.py:1070
  64.0 3.8 collective-permute-done.8.refs_7_
  67.8 5.5 %collective-permute-start.21 = (bf16[128,1024]{1,0:T(8,128)(2,1)S(1)}, bf16[128,1024]{1,0:T(8,128)(2,1)}, u32[]{:S(2)}, u32[]{:S(2)}) collective-permute-start(bf16[128,1024]{1,0:T(8,128)(2,1)S(1)} %bitcast.39), channel_id=1, source_target_pairs={{0,16},{4,20},{8,24},{12,28},{16,0},{20,4},{24,8},{28,12},{1,17},{... | collective-permute-start | bytes 786440 | tf_op jit(solution)/shard_map/ppermute | solution.py:1074
  75.6 3.0 place.2.w_ref.refs_8_
  82.9 7.0 %project.2 = (bf16[640,1024]{1,0:T(8,128)(2,1)}, bf16[640,1024]{1,0:T(8,128)(2,1)}, bf16[640,768]{1,0:T(8,128)(2,1)}, bf16[640,768]{1,0:T(8,128)(2,1)}) custom-call(bf16[640,1024]{1,0:T(8,128)(2,1)} %x_ref.3, bf16[640,1024]{1,0:T(8,128)(2,1)} %collective-permute-done.x1_ref.x_ref, f32[1,1024]{1,0:T(1,128)} %get-tuple-element.278.gain_ref.refs_9_, ...), custom_call_target="tpu_custom_call" | custom-call | flops 12079595520 | bytes 43253760 | tf_op jit(solution)/shard_map/project/pallas_call | solution.py:337
  89.9 7.0 %project.3 = (bf16[640,1024]{1,0:T(8,128)(2,1)}, bf16[640,1024]{1,0:T(8,128)(2,1)}, bf16[640,768]{1,0:T(8,128)(2,1)}, bf16[640,768]{1,0:T(8,128)(2,1)}) custom-call(bf16[640,1024]{1,0:T(8,128)(2,1)} %constant_dynamic-update-slice_fusion.x0_ref.x_ref, bf16[640,1024]{1,0:T(8,128)(2,1)} %collective-permute-done.10.x1_ref.x_ref, ...), custom_call_target="tpu_custom_call" | custom-call | flops 12079595520 | bytes 43253760 | tf_op jit(solution)/shard_map/project/pallas_call | solution.py:337
  96.8 13.1 %attn_fwd.2 = (bf16[2,640,256]{2,1,0:T(8,128)(2,1)}, f32[8,1280]{1,0:T(8,128)}) custom-call(s32[10]{0:T(128)} %get-tuple-element.279.info_ref, bf16[640,768]{1,0:T(8,128)(2,1)} %get-tuple-element.131.refs_0_, bf16[640,768]{1,0:T(8,128)(2,1)} %get-tuple-element.132.refs_1_, bf16[640,768]{1,0:T(8,128)(2,1)} %get-tuple-element.135.refs_2_, ...), custom_call_target="tpu_custom_call" | custom-call | flops 22020096000 | bytes 31457280 | tf_op jit(solution)/shard_map/attn_fwd/pallas_call | solution.py:888
  109.9 3.7 collective-permute-done.12.cot_ref.refs_3_
  117.6 2.9 collective-permute-start.13
  120.5 18.0 %attn_fwd.3 = (bf16[2,640,256]{2,1,0:T(8,128)(2,1)}, f32[8,1280]{1,0:T(8,128)}) custom-call(s32[10]{0:T(128)} %get-tuple-element.138.info_ref, bf16[640,768]{1,0:T(8,128)(2,1)} %get-tuple-element.131.refs_0_, bf16[640,768]{1,0:T(8,128)(2,1)} %get-tuple-element.132.refs_1_, bf16[640,768]{1,0:T(8,128)(2,1)} %get-tuple-element.135.refs_2_, ...), custom_call_target="tpu_custom_call" | custom-call | flops 22020096000 | bytes 31457280 | tf_op jit(solution)/shard_map/attn_fwd/pallas_call | solution.py:888
  140.1 3.1 place.3.d_hbm
  145.7 4.5 collective-permute-done.15.att1
  153.6 16.4 %mlp.4 = (bf16[640,1024]{1,0:T(8,128)(2,1)}, bf16[640,1024]{1,0:T(8,128)(2,1)}, bf16[640,2048]{1,0:T(8,128)(2,1)}, bf16[640,1024]{1,0:T(8,128)(2,1)}, bf16[640,1024]{1,0:T(8,128)(2,1)}) custom-call(bf16[2,640,256]{2,1,0:T(8,128)(2,1)} %get-tuple-element.142.att0.refs_5_, bf16[2,640,256]{2,1,0:T(8,128)(2,1)} %copy-done.42, ...), custom_call_target="tpu_custom_call" | custom-call | flops 56371445760 | bytes 113246208 | tf_op jit(solution)/shard_map/mlp/pallas_call | solution.py:427
  170.7 16.2 %mlp.5 = (bf16[640,1024]{1,0:T(8,128)(2,1)}, bf16[640,1024]{1,0:T(8,128)(2,1)}, bf16[640,2048]{1,0:T(8,128)(2,1)}, bf16[640,1024]{1,0:T(8,128)(2,1)}, bf16[640,1024]{1,0:T(8,128)(2,1)}) custom-call(bf16[2,640,256]{2,1,0:T(8,128)(2,1)} %get-tuple-element.142.att0.refs_5_, bf16[2,640,256]{2,1,0:T(8,128)(2,1)} %copy-done.42, ...), custom_call_target="tpu_custom_call" | custom-call | flops 56371445760 | bytes 113246208 | tf_op jit(solution)/shard_map/mlp/pallas_call | solution.py:427
  186.9 2.2 add_convert_fusion.1
  191.2 16.1 %mlp.6 = (bf16[640,1024]{1,0:T(8,128)(2,1)}, bf16[640,1024]{1,0:T(8,128)(2,1)}, bf16[640,2048]{1,0:T(8,128)(2,1)}, bf16[640,1024]{1,0:T(8,128)(2,1)}, bf16[640,1024]{1,0:T(8,128)(2,1)}) custom-call(bf16[2,640,256]{2,1,0:T(8,128)(2,1)} %get-tuple-element.141.att0.a0.refs_4_, bf16[2,640,256]{2,1,0:T(8,128)(2,1)} %collective-permute-done.11.att1.a1, ...), custom_call_target="tpu_custom_call" | custom-call | flops 56371445760 | bytes 113246208 | tf_op jit(solution)/shard_map/mlp/pallas_call | solution.py:427
  210.1 16.7 %mlp.7 = (bf16[640,1024]{1,0:T(8,128)(2,1)}, bf16[640,1024]{1,0:T(8,128)(2,1)}, bf16[640,2048]{1,0:T(8,128)(2,1)}, bf16[640,1024]{1,0:T(8,128)(2,1)}, bf16[640,1024]{1,0:T(8,128)(2,1)}, /*index=5*/f32[640,1024]{1,0:T(8,128)}) custom-call(bf16[2,640,256]{2,1,0:T(8,128)(2,1)} %get-tuple-element.141.att0.a0.refs_4_, ...), custom_call_target="tpu_custom_call" | custom-call | flops 56371445760 | bytes 113246208 | tf_op jit(solution)/shard_map/mlp/pallas_call | solution.py:427
  228.0 7.5 %middle.1 = (f32[640,1024]{1,0:T(8,128)}, bf16[640,1024]{1,0:T(8,128)(2,1)}, bf16[640,256]{1,0:T(8,128)(2,1)}, bf16[640,256]{1,0:T(8,128)(2,1)}, bf16[640,256]{1...) custom-call(bf16[640,1024]{1,0:T(8,128)(2,1)} %get-tuple-element.169.p0, ...), custom_call_target="tpu_custom_call" | custom-call | flops 8053063680 | bytes 78643200 | tf_op jit(solution)/shard_map/middle/pallas_call | solution.py:681
  235.5 11.7 %down_grads.1 = (bf16[4,128,1024]{2,1,0:T(8,128)(2,1)}, bf16[4,128,1024]{2,1,0:T(8,128)(2,1)}) custom-call(s32[1]{0:T(128)} %bitcast.10.refs_0_.y_ref, bf16[640,1024]{1,0:T(8,128)(2,1)} %copy-done.5, bf16[640,1024]{1,0:T(8,128)(2,1)} %collective-permute-done.28.cot_ref.refs_2_, bf16[640,1024]{1,0:T(8,128)(2,1)} %copy-done.38, ...), custom_call_target="tpu_custom_call" | custom-call | flops 32212254720 | bytes 75497472 | tf_op jit(solution)/shard_map/down_grads/pallas_call | solution.py:529
  250.0 17.7 %gate_up_grads.1 = bf16[1024,2048]{1,0:T(8,128)(2,1)} custom-call(bf16[640,1024]{1,0:T(8,128)(2,1)} %get-tuple-element.185.refs_0_, bf16[640,1024]{1,0:T(8,128)(2,1)} %get-tuple-element.186.refs_1_, bf16[640,1024]{1,0:T(8,128)(2,1)} %get-tuple-element.187.refs_2_, bf16[640,1024]{1,0:T(8,128)(2,1)} %get-tuple-element.188.refs_3_, ...), custom_call_target="tpu_custom_call" | custom-call | flops 64424509440 | bytes 119537664 | tf_op jit(solution)/shard_map/gate_up_grads/pallas_call | solution.py:529
  272.7 2.7 fold.3
  275.5 5.5 %out_grads.1 = (bf16[4,128,1024]{2,1,0:T(8,128)(2,1)}, bf16[4,128,1024]{2,1,0:T(8,128)(2,1)}) custom-call(s32[1]{0:T(128)} %bitcast.10.refs_0_.y_ref, bf16[640,1024]{1,0:T(8,128)(2,1)} %get-tuple-element.195.left_ref, bf16[2,640,256]{2,1,0:T(8,128)(2,1)} %get-tuple-element.141.att0.a0.refs_4_, bf16[2,640,256]{2,1,0:T(8,128)(2,1)} %collective-permute-done.11.att1.a1, ...), custom_call_target="tpu_custom_call" | custom-call | flops 8053063680 | bytes 28311552 | tf_op jit(solution)/shard_map/out_grads/pallas_call | solution.py:617
  283.3 45.4 %attn_bwd.1 = (bf16[640,768]{1,0:T(8,128)(2,1)}, bf16[640,768]{1,0:T(8,128)(2,1)}, bf16[640,768]{1,0:T(8,128)(2,1)}, bf16[640,768]{1,0:T(8,128)(2,1)}) custom-call(s32[10]{0:T(128)} %get-tuple-element.279.info_ref, bf16[640,768]{1,0:T(8,128)(2,1)} %get-tuple-element.131.refs_0_, bf16[640,768]{1,0:T(8,128)(2,1)} %get-tuple-element.132.refs_1_, ...), custom_call_target="tpu_custom_call" | custom-call | flops 110100480000 | bytes 62914560 | tf_op jit(solution)/shard_map/attn_bwd/pallas_call | solution.py:1024
  328.7 2.7 fold.4
  331.4 10.6 %qkv_grads.1 = (bf16[4,128,896]{2,1,0:T(8,128)(2,1)}, bf16[4,128,896]{2,1,0:T(8,128)(2,1)}) custom-call(s32[1]{0:T(128)} %bitcast.10.refs_0_.y_ref, bf16[640,1024]{1,0:T(8,128)(2,1)} %get-tuple-element.211.refs_0_, bf16[640,1024]{1,0:T(8,128)(2,1)} %get-tuple-element.212.refs_1_, bf16[640,1024]{1,0:T(8,128)(2,1)} %get-tuple-element.213.refs_2_, ...), custom_call_target="tpu_custom_call" | custom-call | flops 24159191040 | bytes 64487424 | tf_op jit(solution)/shard_map/qkv_grads/pallas_call | solution.py:577
  342.1 4.3 project_back.4
  346.9 6.4 %collective-permute-start.43 = (bf16[128,1024]{1,0:T(8,128)(2,1)S(1)}, bf16[128,1024]{1,0:T(8,128)(2,1)S(1)}, u32[]{:S(2)}, u32[]{:S(2)}) collective-permute-start(bf16[128,1024]{1,0:T(8,128)(2,1)S(1)} %copy-done.52), channel_id=1, source_target_pairs={{0,8},{4,12},{8,16},{12,20},{16,24},{20,28},{24,0},{28,4},{1,9},{5... | collective-permute-start | bytes 786440 | tf_op jit(solution)/shard_map/ppermute | solution.py:1074
  355.1 2.9 collective-permute-start.44
  358.0 4.3 project_back.5
  362.3 15.4 %collective-permute-done.42 = bf16[128,1024]{1,0:T(8,128)(2,1)S(1)} collective-permute-done((bf16[128,1024]{1,0:T(8,128)(2,1)S(1)}, bf16[128,1024]{1,0:T(8,128)(2,1)S(1)}, u32[]{:S(2)}, u32[]{:S(2)}) %collective-permute-start.42) | collective-permute-done | bytes 262176 | tf_op jit(solution)/shard_map/ppermute | solution.py:1074
  379.3 3.9 project_back.6
  385.9 4.0 project_back.7.p0
  389.9 4.2 convert_add_fusion
  394.1 7.8 %collective-permute-done.46 = bf16[320,1024]{1,0:T(8,128)(2,1)} collective-permute-done((bf16[320,1024]{1,0:T(8,128)(2,1)}, bf16[320,1024]{1,0:T(8,128)(2,1)}, u32[]{:S(2)}, u32[]{:S(2)}) %collective-permute-start.46) | collective-permute-done | bytes 655392 | tf_op jit(solution)/shard_map/ppermute | solution.py:1062
  401.9 2.5 fold.5
  407.0 5.0 %collective-permute-start.51 = (bf16[128,1024]{1,0:T(8,128)(2,1)S(1)}, bf16[128,1024]{1,0:T(8,128)(2,1)S(1)}, u32[]{:S(2)}, u32[]{:S(2)}) collective-permute-start(bf16[128,1024]{1,0:T(8,128)(2,1)S(1)} %copy-done.51), channel_id=1, source_target_pairs={{0,16},{4,20},{8,24},{12,28},{16,0},{20,4},{24,8},{28,12},{1,17},{... | collective-permute-start | bytes 786440 | tf_op jit(solution)/shard_map/ppermute | solution.py:1074
  411.9 2.5 collective-permute-start.52
  415.8 14.6 %collective-permute-done.51 = bf16[128,1024]{1,0:T(8,128)(2,1)S(1)} collective-permute-done((bf16[128,1024]{1,0:T(8,128)(2,1)S(1)}, bf16[128,1024]{1,0:T(8,128)(2,1)S(1)}, u32[]{:S(2)}, u32[]{:S(2)}) %collective-permute-start.51) | collective-permute-done | bytes 262176 | tf_op jit(solution)/shard_map/ppermute | solution.py:1074
  431.0 9.3 %collective-permute-start.55 = (bf16[128,896]{1,0:T(8,128)(2,1)}, bf16[128,896]{1,0:T(8,128)(2,1)S(1)}, u32[]{:S(2)}, u32[]{:S(2)}) collective-permute-start(bf16[128,896]{1,0:T(8,128)(2,1)} %get-tuple-element.227), channel_id=1, source_target_pairs={{0,8},{4,12},{8,16},{12,20},{16,24},{20,28},{24,0},{28,4},{1,9},{5... | collective-permute-start | bytes 688136 | tf_op jit(solution)/shard_map/ppermute | solution.py:1074
  440.3 2.4 collective-permute-start.56
  445.1 2.3 pad_maximum_fusion.1.p2
  447.4 5.1 %last.1 = f32[640,1024]{1,0:T(8,128)} custom-call(bf16[640,1024]{1,0:T(8,128)(2,1)} %project_back.7.p0, bf16[640,1024]{1,0:T(8,128)(2,1)} %collective-permute-done.45.p1, bf16[640,1024]{1,0:T(8,128)(2,1)} %pad_maximum_fusion.1.p2, bf16[640,1024]{1,0:T(8,128)(2,1)} %x_ref.3, f32[640,1024]{1,0:T(8,128)} %get-tuple-element.241.mid_ref, ...), custom_call_target="tpu_custom_call" | custom-call | bytes 62914560 | tf_op jit(solution)/shard_map/last/pallas_call | solution.py:739
  (259 shorter events, 78.6 us)
Async XLA Ops:
  7.2 136.0 %all-gather.2.cloned.1.call-start = ((), (), s32[]{:S(2)}) async-start(), calls=%async_computation.1 | async-start | bytes 5898240 | tf_op jit(solution)/shard_map/all_gather | solution.py:1146
  9.5 16.4 %collective-permute-start.3 = (bf16[128,896]{1,0:T(8,128)(2,1)S(1)}, bf16[128,896]{1,0:T(8,128)(2,1)S(1)}, u32[]{:S(2)}, u32[]{:S(2)}) collective-permute-start(bf16[128,896]{1,0:T(8,128)(2,1)S(1)} %fusion.1.refs_0_), channel_id=1, source_target_pairs={{0,16},{4,20},{8,24},{12,28},{16,0},{20,4},{24,8},{28,12},{1,17},{... | collective-permute-start | bytes 688136 | tf_op jit(solution)/shard_map/ppermute | solution.py:1074
  13.6 12.3 %collective-permute-start.2 = (bf16[128,896]{1,0:T(8,128)(2,1)S(1)}, bf16[128,896]{1,0:T(8,128)(2,1)S(1)}, u32[]{:S(2)}, u32[]{:S(2)}) collective-permute-start(bf16[128,896]{1,0:T(8,128)(2,1)S(1)} %fusion.1.refs_0_), channel_id=1, source_target_pairs={{0,24},{4,28},{8,0},{12,4},{16,8},{20,12},{24,16},{28,20},{1,25},{... | collective-permute-start | bytes 688136 | tf_op jit(solution)/shard_map/ppermute | solution.py:1074
  14.9 15.3 %collective-permute-start.1 = (bf16[128,896]{1,0:T(8,128)(2,1)S(1)}, bf16[128,896]{1,0:T(8,128)(2,1)S(1)}, u32[]{:S(2)}, u32[]{:S(2)}) collective-permute-start(bf16[128,896]{1,0:T(8,128)(2,1)S(1)} %fusion.1.refs_0_), channel_id=1, source_target_pairs={{0,8},{4,12},{8,16},{12,20},{16,24},{20,28},{24,0},{28,4},{1,9},{5... | collective-permute-start | bytes 688136 | tf_op jit(solution)/shard_map/ppermute | solution.py:1074
  31.0 411.9 %reduce-scatter.2.cloned.1.call-start = ((), (), s32[]{:S(2)}) async-start(), calls=%async_computation.2 | async-start | bytes 4718592 | tf_op jit(solution)/shard_map/reduce_scatter | solution.py:1203
  32.2 15.9 %collective-permute-start.5 = (bf16[320,1024]{1,0:T(8,128)(2,1)}, bf16[320,1024]{1,0:T(8,128)(2,1)}, u32[]{:S(2)}, u32[]{:S(2)}) collective-permute-start(bf16[320,1024]{1,0:T(8,128)(2,1)} %get-tuple-element.274), channel_id=1, source_target_pairs={{0,2},{1,3},{2,0},{3,1},{4,6},{5,7},{6,4},{7,5},{8,10},{9,11},{10,... | collective-permute-start | bytes 1966088 | tf_op jit(solution)/shard_map/ppermute | solution.py:1062
  33.8 17.8 %collective-permute-start.4 = (bf16[128,896]{1,0:T(8,128)(2,1)S(1)}, bf16[128,896]{1,0:T(8,128)(2,1)}, u32[]{:S(2)}, u32[]{:S(2)}) collective-permute-start(bf16[128,896]{1,0:T(8,128)(2,1)S(1)} %fusion.1.refs_0_), channel_id=1, source_target_pairs={{0,4},{4,0},{8,12},{12,8},{16,20},{20,16},{24,28},{28,24},{1,5},{5... | collective-permute-start | bytes 688136 | tf_op jit(solution)/shard_map/ppermute | solution.py:1070
  35.3 47.0 %collective-permute-start = (bf16[640,1024]{1,0:T(8,128)(2,1)S(1)}, bf16[640,1024]{1,0:T(8,128)(2,1)}, u32[]{:S(2)}, u32[]{:S(2)}) collective-permute-start(bf16[640,1024]{1,0:T(8,128)(2,1)S(1)} %copy-done), channel_id=1, source_target_pairs={{0,1},{1,0},{2,3},{3,2},{4,5},{5,4},{6,7},{7,6},{8,9},{9,8},{10,11... | collective-permute-start | bytes 3932168 | tf_op jit(solution)/shard_map/ppermute | solution.py:1058
  48.1 31.6 %collective-permute-start.9 = (bf16[320,1024]{1,0:T(8,128)(2,1)}, bf16[320,1024]{1,0:T(8,128)(2,1)}, u32[]{:S(2)}, u32[]{:S(2)}) collective-permute-start(bf16[320,1024]{1,0:T(8,128)(2,1)} %get-tuple-element.133), channel_id=1, source_target_pairs={{0,2},{1,3},{2,0},{3,1},{4,6},{5,7},{6,4},{7,5},{8,10},{9,11},{10,... | collective-permute-start | bytes 1966088 | tf_op jit(solution)/shard_map/ppermute | solution.py:1062
  51.1 12.8 %collective-permute-start.7 = (bf16[128,896]{1,0:T(8,128)(2,1)S(1)}, bf16[128,896]{1,0:T(8,128)(2,1)S(1)}, u32[]{:S(2)}, u32[]{:S(2)}) collective-permute-start(bf16[128,896]{1,0:T(8,128)(2,1)S(1)} %copy-done.27), channel_id=1, source_target_pairs={{0,4},{4,0},{8,12},{12,8},{16,20},{20,16},{24,28},{28,24},{1,5},{5... | collective-permute-start | bytes 688136 | tf_op jit(solution)/shard_map/ppermute | solution.py:1070
  51.6 16.1 %collective-permute-start.8 = (bf16[128,896]{1,0:T(8,128)(2,1)S(1)}, bf16[128,896]{1,0:T(8,128)(2,1)S(1)}, u32[]{:S(2)}, u32[]{:S(2)}) collective-permute-start(bf16[128,896]{1,0:T(8,128)(2,1)S(1)} %collective-permute-done.3.refs_3_), channel_id=1, source_target_pairs={{0,4},{4,0},{8,12},{12,8},{16,20},{20,16},{24,28},{28,24},{1,5},{5... | collective-permute-start | bytes 688136 | tf_op jit(solution)/shard_map/ppermute | solution.py:1070
  67.8 42.1 %collective-permute-start.21 = (bf16[128,1024]{1,0:T(8,128)(2,1)S(1)}, bf16[128,1024]{1,0:T(8,128)(2,1)}, u32[]{:S(2)}, u32[]{:S(2)}) collective-permute-start(bf16[128,1024]{1,0:T(8,128)(2,1)S(1)} %bitcast.39), channel_id=1, source_target_pairs={{0,16},{4,20},{8,24},{12,28},{16,0},{20,4},{24,8},{28,12},{1,17},{... | collective-permute-start | bytes 786440 | tf_op jit(solution)/shard_map/ppermute | solution.py:1074
  73.3 36.6 %collective-permute-start.20 = (bf16[128,1024]{1,0:T(8,128)(2,1)S(1)}, bf16[128,1024]{1,0:T(8,128)(2,1)}, u32[]{:S(2)}, u32[]{:S(2)}) collective-permute-start(bf16[128,1024]{1,0:T(8,128)(2,1)S(1)} %bitcast.40), channel_id=1, source_target_pairs={{0,24},{4,28},{8,0},{12,4},{16,8},{20,12},{24,16},{28,20},{1,25},{... | collective-permute-start | bytes 786440 | tf_op jit(solution)/shard_map/ppermute | solution.py:1074
  73.7 36.2 %collective-permute-start.19 = (bf16[128,1024]{1,0:T(8,128)(2,1)S(1)}, bf16[128,1024]{1,0:T(8,128)(2,1)}, u32[]{:S(2)}, u32[]{:S(2)}) collective-permute-start(bf16[128,1024]{1,0:T(8,128)(2,1)S(1)} %bitcast.41), channel_id=1, source_target_pairs={{0,8},{4,12},{8,16},{12,20},{16,24},{20,28},{24,0},{28,4},{1,9},{5... | collective-permute-start | bytes 786440 | tf_op jit(solution)/shard_map/ppermute | solution.py:1074
  82.4 31.2 %collective-permute-start.12 = (bf16[640,1024]{1,0:T(8,128)(2,1)S(1)}, bf16[640,1024]{1,0:T(8,128)(2,1)S(1)}, u32[]{:S(2)}, u32[]{:S(2)}) collective-permute-start(bf16[640,1024]{1,0:T(8,128)(2,1)S(1)} %convert_element_type.116.cot_ref.refs_1_), channel_id=1, source_target_pairs={{0,2},{1,3},{2,0},{3,1},{4,6},{5,7},{6,4},{7,5},{8,10},{9,11},{10,... | collective-permute-start | bytes 3932168 | tf_op jit(solution)/shard_map/ppermute | solution.py:1062
  113.6 25.0 %collective-permute-start.22 = (bf16[128,1024]{1,0:T(8,128)(2,1)S(1)}, bf16[128,1024]{1,0:T(8,128)(2,1)S(1)}, u32[]{:S(2)}, u32[]{:S(2)}) collective-permute-start(bf16[128,1024]{1,0:T(8,128)(2,1)S(1)} %bitcast.42), channel_id=1, source_target_pairs={{0,4},{4,0},{8,12},{12,8},{16,20},{20,16},{24,28},{28,24},{1,5},{5... | collective-permute-start | bytes 786440 | tf_op jit(solution)/shard_map/ppermute | solution.py:1070
  115.1 23.6 %collective-permute-start.23 = (bf16[128,1024]{1,0:T(8,128)(2,1)}, bf16[128,1024]{1,0:T(8,128)(2,1)S(1)}, u32[]{:S(2)}, u32[]{:S(2)}) collective-permute-start(bf16[128,1024]{1,0:T(8,128)(2,1)} %collective-permute-done.19.refs_1_), channel_id=1, source_target_pairs={{0,4},{4,0},{8,12},{12,8},{16,20},{20,16},{24,28},{28,24},{1,5},{5... | collective-permute-start | bytes 786440 | tf_op jit(solution)/shard_map/ppermute | solution.py:1070
  115.6 23.1 %collective-permute-start.24 = (bf16[128,1024]{1,0:T(8,128)(2,1)}, bf16[128,1024]{1,0:T(8,128)(2,1)S(1)}, u32[]{:S(2)}, u32[]{:S(2)}) collective-permute-start(bf16[128,1024]{1,0:T(8,128)(2,1)} %collective-permute-done.20.refs_2_), channel_id=1, source_target_pairs={{0,4},{4,0},{8,12},{12,8},{16,20},{20,16},{24,28},{28,24},{1,5},{5... | collective-permute-start | bytes 786440 | tf_op jit(solution)/shard_map/ppermute | solution.py:1070
  117.1 21.6 %collective-permute-start.25 = (bf16[128,1024]{1,0:T(8,128)(2,1)}, bf16[128,1024]{1,0:T(8,128)(2,1)S(1)}, u32[]{:S(2)}, u32[]{:S(2)}) collective-permute-start(bf16[128,1024]{1,0:T(8,128)(2,1)} %collective-permute-done.21.refs_3_), channel_id=1, source_target_pairs={{0,4},{4,0},{8,12},{12,8},{16,20},{20,16},{24,28},{28,24},{1,5},{5... | collective-permute-start | bytes 786440 | tf_op jit(solution)/shard_map/ppermute | solution.py:1070
  117.6 27.6 %collective-permute-start.13 = (bf16[2,640,256]{2,1,0:T(8,128)(2,1)}, bf16[2,640,256]{2,1,0:T(8,128)(2,1)}, u32[]{:S(2)}, u32[]{:S(2)}) collective-permute-start(bf16[2,640,256]{2,1,0:T(8,128)(2,1)} %get-tuple-element.141.att0.a0.refs_4_), channel_id=1, source_target_pairs={{0,2},{1,3},{2,0},{3,1},{4,6},{5,7},{6,4},{7,5},{8,10},{9,11},{10,... | collective-permute-start | bytes 1966088 | tf_op jit(solution)/shard_map/ppermute | solution.py:1062
  138.6 14.1 %collective-permute-start.17 = (bf16[640,1024]{1,0:T(8,128)(2,1)S(1)}, bf16[640,1024]{1,0:T(8,128)(2,1)}, u32[]{:S(2)}, u32[]{:S(2)}) collective-permute-start(bf16[640,1024]{1,0:T(8,128)(2,1)S(1)} %collective-permute-done.12.cot_ref.refs_3_), channel_id=1, source_target_pairs={{0,1},{1,0},{2,3},{3,2},{4,5},{5,4},{6,7},{7,6},{8,9},{9,8},{10,11... | collective-permute-start | bytes 3932168 | tf_op jit(solution)/shard_map/ppermute | solution.py:1058
  145.6 45.6 %collective-permute-start.11 = (bf16[2,640,256]{2,1,0:T(8,128)(2,1)}, bf16[2,640,256]{2,1,0:T(8,128)(2,1)}, u32[]{:S(2)}, u32[]{:S(2)}) collective-permute-start(bf16[2,640,256]{2,1,0:T(8,128)(2,1)} %get-tuple-element.141.att0.a0.refs_4_), channel_id=1, source_target_pairs={{0,1},{1,0},{2,3},{3,2},{4,5},{5,4},{6,7},{7,6},{8,9},{9,8},{10,11... | collective-permute-start | bytes 1966088 | tf_op jit(solution)/shard_map/ppermute | solution.py:1058
  150.2 38.9 %collective-permute-start.28 = (bf16[640,1024]{1,0:T(8,128)(2,1)S(1)}, bf16[640,1024]{1,0:T(8,128)(2,1)}, u32[]{:S(2)}, u32[]{:S(2)}) collective-permute-start(bf16[640,1024]{1,0:T(8,128)(2,1)S(1)} %convert_element_type.116.cot_ref.refs_1_), channel_id=1, source_target_pairs={{0,1},{1,0},{2,3},{3,2},{4,5},{5,4},{6,7},{7,6},{8,9},{9,8},{10,11... | collective-permute-start | bytes 3932168 | tf_op jit(solution)/shard_map/ppermute | solution.py:1058
  150.6 19.6 %collective-permute-start.14 = (bf16[2,640,256]{2,1,0:T(8,128)(2,1)S(1)}, bf16[2,640,256]{2,1,0:T(8,128)(2,1)}, u32[]{:S(2)}, u32[]{:S(2)}) collective-permute-start(bf16[2,640,256]{2,1,0:T(8,128)(2,1)S(1)} %copy-done.41), channel_id=1, source_target_pairs={{0,2},{1,3},{2,0},{3,1},{4,6},{5,7},{6,4},{7,5},{8,10},{9,11},{10,... | collective-permute-start | bytes 1966088 | tf_op jit(solution)/shard_map/ppermute | solution.py:1062
  170.1 16.8 %collective-permute-start.29 = (bf16[640,1024]{1,0:T(8,128)(2,1)}, bf16[640,1024]{1,0:T(8,128)(2,1)}, u32[]{:S(2)}, u32[]{:S(2)}) collective-permute-start(bf16[640,1024]{1,0:T(8,128)(2,1)} %get-tuple-element.156), channel_id=1, source_target_pairs={{0,1},{1,0},{2,3},{3,2},{4,5},{5,4},{6,7},{7,6},{8,9},{9,8},{10,11... | collective-permute-start | bytes 3932168 | tf_op jit(solution)/shard_map/ppermute | solution.py:1058
  170.2 21.0 %collective-permute-start.27 = (bf16[2,640,256]{2,1,0:T(8,128)(2,1)}, bf16[2,640,256]{2,1,0:T(8,128)(2,1)}, u32[]{:S(2)}, u32[]{:S(2)}) collective-permute-start(bf16[2,640,256]{2,1,0:T(8,128)(2,1)} %collective-permute-done.14.att2.a2), channel_id=1, source_target_pairs={{0,1},{1,0},{2,3},{3,2},{4,5},{5,4},{6,7},{7,6},{8,9},{9,8},{10,11... | collective-permute-start | bytes 1966088 | tf_op jit(solution)/shard_map/ppermute | solution.py:1058
  170.6 36.8 %collective-permute-start.32 = (bf16[640,1024]{1,0:T(8,128)(2,1)}, bf16[640,1024]{1,0:T(8,128)(2,1)S(1)}, u32[]{:S(2)}, u32[]{:S(2)}) collective-permute-start(bf16[640,1024]{1,0:T(8,128)(2,1)} %get-tuple-element.168), channel_id=1, source_target_pairs={{0,1},{1,0},{2,3},{3,2},{4,5},{5,4},{6,7},{7,6},{8,9},{9,8},{10,11... | collective-permute-start | bytes 3932168 | tf_op jit(solution)/shard_map/ppermute | solution.py:1058
  190.1 18.9 %collective-permute-start.30 = (bf16[320,1024]{1,0:T(8,128)(2,1)}, bf16[320,1024]{1,0:T(8,128)(2,1)S(1)}, u32[]{:S(2)}, u32[]{:S(2)}) collective-permute-start(bf16[320,1024]{1,0:T(8,128)(2,1)} %get-tuple-element.272), channel_id=1, source_target_pairs={{0,2},{1,3},{2,0},{3,1},{4,6},{5,7},{6,4},{7,5},{8,10},{9,11},{10,... | collective-permute-start | bytes 1966088 | tf_op jit(solution)/shard_map/ppermute | solution.py:1062
  207.3 20.7 %collective-permute-start.33 = (bf16[640,1024]{1,0:T(8,128)(2,1)}, bf16[640,1024]{1,0:T(8,128)(2,1)}, u32[]{:S(2)}, u32[]{:S(2)}) collective-permute-start(bf16[640,1024]{1,0:T(8,128)(2,1)} %get-tuple-element.162), channel_id=1, source_target_pairs={{0,1},{1,0},{2,3},{3,2},{4,5},{5,4},{6,7},{7,6},{8,9},{9,8},{10,11... | collective-permute-start | bytes 3932168 | tf_op jit(solution)/shard_map/ppermute | solution.py:1058
  209.0 17.8 %collective-permute-start.34 = (bf16[320,1024]{1,0:T(8,128)(2,1)S(1)}, bf16[320,1024]{1,0:T(8,128)(2,1)S(1)}, u32[]{:S(2)}, u32[]{:S(2)}) collective-permute-start(bf16[320,1024]{1,0:T(8,128)(2,1)S(1)} %get-tuple-element.170), channel_id=1, source_target_pairs={{0,2},{1,3},{2,0},{3,1},{4,6},{5,7},{6,4},{7,5},{8,10},{9,11},{10,... | collective-permute-start | bytes 1966088 | tf_op jit(solution)/shard_map/ppermute | solution.py:1062
  247.2 25.5 %collective-permute-start.39 = (bf16[4,128,1024]{2,1,0:T(8,128)(2,1)}, bf16[4,128,1024]{2,1,0:T(8,128)(2,1)}, u32[]{:S(2)}, u32[]{:S(2)}) collective-permute-start(bf16[4,128,1024]{2,1,0:T(8,128)(2,1)} %get-tuple-element.183), channel_id=1, source_target_pairs={{0,4},{4,0},{8,12},{12,8},{16,20},{20,16},{24,28},{28,24},{1,5},{5... | collective-permute-start | bytes 3145736 | tf_op jit(solution)/shard_map/ppermute | solution.py:1070
  248.8 20.8 %collective-permute-start.35 = (bf16[640,256]{1,0:T(8,128)(2,1)S(1)}, bf16[640,256]{1,0:T(8,128)(2,1)S(1)}, u32[]{:S(2)}, u32[]{:S(2)}) collective-permute-start(bf16[640,256]{1,0:T(8,128)(2,1)S(1)} %copy-done.47), channel_id=1, source_target_pairs={{0,2},{1,3},{2,0},{3,1},{4,6},{5,7},{6,4},{7,5},{8,10},{9,11},{10,... | collective-permute-start | bytes 983048 | tf_op jit(solution)/shard_map/ppermute | solution.py:1062
  249.8 19.9 %collective-permute-start.36 = (bf16[640,256]{1,0:T(8,128)(2,1)S(1)}, bf16[640,256]{1,0:T(8,128)(2,1)}, u32[]{:S(2)}, u32[]{:S(2)}) collective-permute-start(bf16[640,256]{1,0:T(8,128)(2,1)S(1)} %copy-done.46), channel_id=1, source_target_pairs={{0,3},{1,2},{2,1},{3,0},{4,7},{5,6},{6,5},{7,4},{8,11},{9,10},{10,... | collective-permute-start | bytes 983048 | tf_op jit(solution)/shard_map/ppermute | solution.py:1066
  268.7 13.9 %collective-permute-start.38 = (bf16[640,256]{1,0:T(8,128)(2,1)S(1)}, bf16[640,256]{1,0:T(8,128)(2,1)S(1)}, u32[]{:S(2)}, u32[]{:S(2)}) collective-permute-start(bf16[640,256]{1,0:T(8,128)(2,1)S(1)} %copy-done.44), channel_id=1, source_target_pairs={{0,1},{1,0},{2,3},{3,2},{4,5},{5,4},{6,7},{7,6},{8,9},{9,8},{10,11... | collective-permute-start | bytes 983048 | tf_op jit(solution)/shard_map/ppermute | solution.py:1058
  269.7 72.4 %collective-permute-start.37 = (bf16[640,1024]{1,0:T(8,128)(2,1)S(1)}, bf16[640,1024]{1,0:T(8,128)(2,1)S(1)}, u32[]{:S(2)}, u32[]{:S(2)}) collective-permute-start(bf16[640,1024]{1,0:T(8,128)(2,1)S(1)} %copy-done.6), channel_id=1, source_target_pairs={{0,2},{1,3},{2,0},{3,1},{4,6},{5,7},{6,4},{7,5},{8,10},{9,11},{10,... | collective-permute-start | bytes 3932168 | tf_op jit(solution)/shard_map/ppermute | solution.py:1062
  281.0 47.7 %collective-permute-start.40 = (bf16[4,128,1024]{2,1,0:T(8,128)(2,1)}, bf16[4,128,1024]{2,1,0:T(8,128)(2,1)}, u32[]{:S(2)}, u32[]{:S(2)}) collective-permute-start(bf16[4,128,1024]{2,1,0:T(8,128)(2,1)} %get-tuple-element.196), channel_id=1, source_target_pairs={{0,4},{4,0},{8,12},{12,8},{16,20},{20,16},{24,28},{28,24},{1,5},{5... | collective-permute-start | bytes 3145736 | tf_op jit(solution)/shard_map/ppermute | solution.py:1070
  346.4 43.5 %collective-permute-start.31 = (bf16[640,1024]{1,0:T(8,128)(2,1)}, bf16[640,1024]{1,0:T(8,128)(2,1)}, u32[]{:S(2)}, u32[]{:S(2)}) collective-permute-start(bf16[640,1024]{1,0:T(8,128)(2,1)} %get-tuple-element.166), channel_id=1, source_target_pairs={{0,1},{1,0},{2,3},{3,2},{4,5},{5,4},{6,7},{7,6},{8,9},{9,8},{10,11... | collective-permute-start | bytes 3932168 | tf_op jit(solution)/shard_map/ppermute | solution.py:1058
  346.9 30.9 %collective-permute-start.43 = (bf16[128,1024]{1,0:T(8,128)(2,1)S(1)}, bf16[128,1024]{1,0:T(8,128)(2,1)S(1)}, u32[]{:S(2)}, u32[]{:S(2)}) collective-permute-start(bf16[128,1024]{1,0:T(8,128)(2,1)S(1)} %copy-done.52), channel_id=1, source_target_pairs={{0,8},{4,12},{8,16},{12,20},{16,24},{20,28},{24,0},{28,4},{1,9},{5... | collective-permute-start | bytes 786440 | tf_op jit(solution)/shard_map/ppermute | solution.py:1074
  353.3 40.8 %collective-permute-start.48 = (bf16[4,128,896]{2,1,0:T(8,128)(2,1)}, bf16[4,128,896]{2,1,0:T(8,128)(2,1)}, u32[]{:S(2)}, u32[]{:S(2)}) collective-permute-start(bf16[4,128,896]{2,1,0:T(8,128)(2,1)} %get-tuple-element.216), channel_id=1, source_target_pairs={{0,4},{4,0},{8,12},{12,8},{16,20},{20,16},{24,28},{28,24},{1,5},{5... | collective-permute-start | bytes 2752520 | tf_op jit(solution)/shard_map/ppermute | solution.py:1070
  354.0 23.8 %collective-permute-start.42 = (bf16[128,1024]{1,0:T(8,128)(2,1)S(1)}, bf16[128,1024]{1,0:T(8,128)(2,1)S(1)}, u32[]{:S(2)}, u32[]{:S(2)}) collective-permute-start(bf16[128,1024]{1,0:T(8,128)(2,1)S(1)} %copy-done.54), channel_id=1, source_target_pairs={{0,16},{4,20},{8,24},{12,28},{16,0},{20,4},{24,8},{28,12},{1,17},{... | collective-permute-start | bytes 786440 | tf_op jit(solution)/shard_map/ppermute | solution.py:1074
  355.1 22.7 %collective-permute-start.44 = (bf16[128,1024]{1,0:T(8,128)(2,1)S(1)}, bf16[128,1024]{1,0:T(8,128)(2,1)S(1)}, u32[]{:S(2)}, u32[]{:S(2)}) collective-permute-start(bf16[128,1024]{1,0:T(8,128)(2,1)S(1)} %copy-done.53), channel_id=1, source_target_pairs={{0,24},{4,28},{8,0},{12,4},{16,8},{20,12},{24,16},{28,20},{1,25},{... | collective-permute-start | bytes 786440 | tf_op jit(solution)/shard_map/ppermute | solution.py:1074
  383.2 64.1 %collective-permute-start.45 = (bf16[640,1024]{1,0:T(8,128)(2,1)}, bf16[640,1024]{1,0:T(8,128)(2,1)}, u32[]{:S(2)}, u32[]{:S(2)}) collective-permute-start(bf16[640,1024]{1,0:T(8,128)(2,1)} %project_back.6), channel_id=1, source_target_pairs={{0,1},{1,0},{2,3},{3,2},{4,5},{5,4},{6,7},{7,6},{8,9},{9,8},{10,11... | collective-permute-start | bytes 3932168 | tf_op jit(solution)/shard_map/ppermute | solution.py:1058
  384.4 17.5 %collective-permute-start.46 = (bf16[320,1024]{1,0:T(8,128)(2,1)}, bf16[320,1024]{1,0:T(8,128)(2,1)}, u32[]{:S(2)}, u32[]{:S(2)}) collective-permute-start(bf16[320,1024]{1,0:T(8,128)(2,1)} %get-tuple-element.269), channel_id=1, source_target_pairs={{0,2},{1,3},{2,0},{3,1},{4,6},{5,7},{6,4},{7,5},{8,10},{9,11},{10,... | collective-permute-start | bytes 1966088 | tf_op jit(solution)/shard_map/ppermute | solution.py:1062
  405.4 39.7 %collective-permute-start.47 = (bf16[320,1024]{1,0:T(8,128)(2,1)S(1)}, bf16[320,1024]{1,0:T(8,128)(2,1)S(1)}, u32[]{:S(2)}, u32[]{:S(2)}) collective-permute-start(bf16[320,1024]{1,0:T(8,128)(2,1)S(1)} %copy-done.11), channel_id=1, source_target_pairs={{0,2},{1,3},{2,0},{3,1},{4,6},{5,7},{6,4},{7,5},{8,10},{9,11},{10,... | collective-permute-start | bytes 1966088 | tf_op jit(solution)/shard_map/ppermute | solution.py:1062
  407.0 23.4 %collective-permute-start.51 = (bf16[128,1024]{1,0:T(8,128)(2,1)S(1)}, bf16[128,1024]{1,0:T(8,128)(2,1)S(1)}, u32[]{:S(2)}, u32[]{:S(2)}) collective-permute-start(bf16[128,1024]{1,0:T(8,128)(2,1)S(1)} %copy-done.51), channel_id=1, source_target_pairs={{0,16},{4,20},{8,24},{12,28},{16,0},{20,4},{24,8},{28,12},{1,17},{... | collective-permute-start | bytes 786440 | tf_op jit(solution)/shard_map/ppermute | solution.py:1074
  411.9 28.3 %collective-permute-start.52 = (bf16[128,1024]{1,0:T(8,128)(2,1)S(1)}, bf16[128,1024]{1,0:T(8,128)(2,1)S(1)}, u32[]{:S(2)}, u32[]{:S(2)}) collective-permute-start(bf16[128,1024]{1,0:T(8,128)(2,1)S(1)} %copy-done.49), channel_id=1, source_target_pairs={{0,8},{4,12},{8,16},{12,20},{16,24},{20,28},{24,0},{28,4},{1,9},{5... | collective-permute-start | bytes 786440 | tf_op jit(solution)/shard_map/ppermute | solution.py:1074
  414.4 16.5 %collective-permute-start.53 = (bf16[128,1024]{1,0:T(8,128)(2,1)S(1)}, bf16[128,1024]{1,0:T(8,128)(2,1)S(1)}, u32[]{:S(2)}, u32[]{:S(2)}) collective-permute-start(bf16[128,1024]{1,0:T(8,128)(2,1)S(1)} %copy-done.50), channel_id=1, source_target_pairs={{0,24},{4,28},{8,0},{12,4},{16,8},{20,12},{24,16},{28,20},{1,25},{... | collective-permute-start | bytes 786440 | tf_op jit(solution)/shard_map/ppermute | solution.py:1074
  431.0 21.5 %collective-permute-start.55 = (bf16[128,896]{1,0:T(8,128)(2,1)}, bf16[128,896]{1,0:T(8,128)(2,1)S(1)}, u32[]{:S(2)}, u32[]{:S(2)}) collective-permute-start(bf16[128,896]{1,0:T(8,128)(2,1)} %get-tuple-element.227), channel_id=1, source_target_pairs={{0,8},{4,12},{8,16},{12,20},{16,24},{20,28},{24,0},{28,4},{1,9},{5... | collective-permute-start | bytes 688136 | tf_op jit(solution)/shard_map/ppermute | solution.py:1074
  (68 other events, 700.2 us)
Sparse Core Ops, SparseCore 0:
  31.1 106.1 all-gather.1
  267.8 108.2 reduce-scatter.1

commit v2 on v1

--- a/solution.py
+++ b/solution.py
@@ -346,104 +346,128 @@
     )(x0, x1, gain, weight)
 
 
-def _mlp_kernel(keep, step, att0, att1, att2, att3, x_ref, cot_ref, gain_ref, w_hbm, d_hbm, m_hbm, *refs):
-    part_ref, hidden_ref, grad_ref, normed_ref, branch_ref = refs[:5]
-    w_ref, d_ref, mate_ref, acc, acc_b, sems = refs[-6:]
-    width = att0.shape[2]
-    count = hidden_ref.shape[1]
-    out_at = 2 * count
-    chunks = count // step
+def _mlp_kernel(keep, *refs):
+    att_a, att_b, (xa, xb, ca, cb) = refs[:4], refs[4:8], refs[8:12]
+    gain_ref, w_hbm, d_hbm, m_hbm = refs[12:16]
+    hidden_ref, grad_ref, normed_ref = refs[16:19]
+    part_a, part_b, branch_a, branch_b = refs[19:23]
+    att_s, x_s, cot_s, o_s, w_s, d_s, sems = refs[-7:]
+    width = att_a[0].shape[2]
+    count = hidden_ref.shape[2]
     pulls = [
         pltpu.make_async_copy(
-            w_hbm.at[:, pl.ds(out_at, 2 * width)], w_ref.at[:, pl.ds(out_at, 2 * width)], sems.at[0]
+            w_hbm.at[:, pl.ds(2 * count, 2 * width)], o_s.at[:, pl.ds(0, 2 * width)], sems.at[0]
         ),
-        pltpu.make_async_copy(m_hbm, mate_ref, sems.at[1]),
+        pltpu.make_async_copy(m_hbm, o_s.at[:, pl.ds(2 * width, 2 * width)], sems.at[1]),
+        pltpu.make_async_copy(w_hbm.at[:, pl.ds(0, 2 * count)], w_s, sems.at[2]),
+        pltpu.make_async_copy(d_hbm, d_s, sems.at[3]),
     ]
-    for c in range(chunks):
-        for g in range(3):
-            source, target = (w_hbm, w_ref) if g < 2 else (d_hbm, d_ref)
-            at = pl.ds(g % 2 * count + c * step, step)
-            pulls.append(
-                pltpu.make_async_copy(source.at[:, at], target.at[:, at], sems.at[2 + 3 * c + g])
-            )
     first = pl.program_id(0) == 0
+    late = pl.program_id(0) >= pl.num_programs(0) // 2
 
     @pl.when(first)
     def _():
         for pull in pulls:
             pull.start()
+
+    def take(att, x_ref, cot_ref):
+        for i, of in enumerate((0, 2, 1, 3)):
+            att_s[:, i * width : (i + 1) * width] = att[of][0]
+        x_s[...] = x_ref[...]
+        cot_s[...] = cot_ref[...]
+
+    @pl.when(jnp.logical_not(late))
+    def _():
+        take(att_a, xa, ca)
+
+    @pl.when(late)
+    def _():
+        take(att_b, xb, cb)
+
+    @pl.when(first)
+    def _():
         for pull in pulls[:2]:
             pull.wait()
 
-    branch = _dot(att0[0], w_ref[:, out_at : out_at + width], NT)
-    branch += _dot(att2[0], w_ref[:, out_at + width : out_at + 2 * width], NT)
-    branch += _dot(att1[0], mate_ref[:, :width], NT) + _dot(att3[0], mate_ref[:, width:], NT)
-    residual = x_ref[...].astype(jnp.float32) + branch
+    residual = x_s[...].astype(jnp.float32) + _dot(att_s[...], o_s[...], NT)
     if keep:
-        refs[5][...] = residual
-    normed_ref[...] = (_normed(residual)[1] * gain_ref[...]).astype(jnp.bfloat16)
-    for c in range(chunks):
-
-        @pl.when(first)
+        keep_ref = refs[23]
+
+        @pl.when(late)
         def _():
-            for pull in pulls[2 + 3 * c : 5 + 3 * c]:
-                pull.wait()
-
-        gate_at, up_at = [slice(g * count + c * step, g * count + (c + 1) * step) for g in (0, 1)]
-        gate = _dot(normed_ref[...], w_ref[:, gate_at], NN).astype(jnp.bfloat16).astype(jnp.float32)
-        up = _dot(normed_ref[...], w_ref[:, up_at], NN).astype(jnp.bfloat16).astype(jnp.float32)
-        hidden_grad = _dot(cot_ref[...], d_ref[:, gate_at], NN)
-        sig = 0.5 * jnp.tanh(0.5 * gate) + 0.5
-        act = gate * sig
-        hidden_ref[:, gate_at] = (act * up).astype(jnp.bfloat16)
-        grad_ref[:, gate_at] = (hidden_grad * up * (sig + act * (1.0 - sig))).astype(jnp.bfloat16)
-        grad_ref[:, up_at] = (hidden_grad * act).astype(jnp.bfloat16)
-        term = _dot(grad_ref[:, gate_at], w_ref[:, gate_at], NT) + _dot(
-            grad_ref[:, up_at], w_ref[:, up_at], NT
-        )
-        down = _dot(hidden_ref[:, gate_at], d_ref[:, gate_at], NT)
-        if c > 0:
-            term = term + acc[...]
-            down = down + acc_b[...]
-        if c < chunks - 1:
-            acc[...] = term
-            acc_b[...] = down
-        else:
-            part_ref[...] = term.astype(part_ref.dtype)
-            branch_ref[...] = down.astype(branch_ref.dtype)
-
-
-def mlp(attended, x, cot, gain, weights, down, out_mate, keep, step=512):
-    rows, depth = x.shape
-    width = attended[0][0].shape[2]
+            keep_ref[...] = residual
+
+    normed_ref[0] = (_normed(residual)[1] * gain_ref[...]).astype(jnp.bfloat16)
+
+    @pl.when(first)
+    def _():
+        for pull in pulls[2:]:
+            pull.wait()
+
+    both = _dot(normed_ref[0], w_s[...], NN).astype(jnp.bfloat16).astype(jnp.float32)
+    gate, up = both[:, :count], both[:, count:]
+    hidden_grad = _dot(cot_s[...], d_s[...], NN)
+    sig = 0.5 * jnp.tanh(0.5 * gate) + 0.5
+    act = gate * sig
+    hidden = (act * up).astype(jnp.bfloat16)
+    hidden_ref[0] = hidden
+    grad_ref[0, :, :count] = (hidden_grad * up * (sig + act * (1.0 - sig))).astype(jnp.bfloat16)
+    grad_ref[0, :, count:] = (hidden_grad * act).astype(jnp.bfloat16)
+    part = _dot(grad_ref[0], w_s[...], NT).astype(jnp.bfloat16)
+    branch = _dot(hidden, d_s[...], NT).astype(jnp.bfloat16)
+
+    @pl.when(jnp.logical_not(late))
+    def _():
+        part_a[...] = part
+        branch_a[...] = branch
+
+    @pl.when(late)
+    def _():
+        part_b[...] = part
+        branch_b[...] = branch
+
+
+def mlp(attended_a, attended_b, x, cot, gain, weights, down, out_mate, keep):
+    rows, depth = x[0].shape
+    width = attended_a[0][0].shape[2]
     count = down.shape[1]
     tile = _row_tile(rows)
-    step = min(step, count)
-    outs = [(depth, jnp.bfloat16), (count, jnp.bfloat16), (2 * count, jnp.bfloat16)]
-    outs += [(depth, jnp.bfloat16)] * 2
+    steps = rows // tile
+    bf16, f32 = jnp.bfloat16, jnp.float32
+    early = lambda i: jnp.minimum(i, steps - 1)
+    late = lambda i: jnp.maximum(i - steps, 0)
+    rows_of = lambda where: pl.BlockSpec((tile, depth), lambda i: (where(i), 0))
+    stack = lambda c: pl.BlockSpec((1, tile, c), lambda i: (i // steps, i % steps, 0))
+    member = lambda n, where: pl.BlockSpec((1, tile, width), lambda i: (n, where(i), 0))
+    outs = [jax.ShapeDtypeStruct((2, rows, c), bf16) for c in (count, 2 * count, depth)]
+    outs += [jax.ShapeDtypeStruct((rows, depth), bf16)] * 4
+    out_specs = [stack(count), stack(2 * count), stack(depth)] + [rows_of(early), rows_of(late)] * 2
     if keep:
-        outs.append((depth, jnp.float32))
+        outs.append(jax.ShapeDtypeStruct((rows, depth), f32))
+        out_specs.append(rows_of(late))
     anywhere = pl.BlockSpec(memory_space=pl.ANY)
     return pl.pallas_call(
-        functools.partial(_mlp_kernel, keep, step),
-        grid=(rows // tile,),
-        out_shape=[jax.ShapeDtypeStruct((rows, c), d) for c, d in outs],
-        in_specs=[_stacked(tile, width, n) for v, n in attended]
-        + [_rows(tile, depth)] * 2
+        functools.partial(_mlp_kernel, keep),
+        grid=(2 * steps,),
+        out_shape=outs,
+        in_specs=[member(n, early) for v, n in attended_a]
+        + [member(n, late) for v, n in attended_b]
+        + [rows_of(early), rows_of(late)] * 2
         + [_full((1, depth)), anywhere, anywhere, anywhere],
-        out_specs=[_rows(tile, c) for c, d in outs],
+        out_specs=out_specs,
         scratch_shapes=[
-            pltpu.VMEM(weights.shape, jnp.bfloat16),
-            pltpu.VMEM(down.shape, jnp.bfloat16),
-            pltpu.VMEM(out_mate.shape, jnp.bfloat16),
-            pltpu.VMEM((tile, depth), jnp.float32),
-            pltpu.VMEM((tile, depth), jnp.float32),
-            pltpu.SemaphoreType.DMA((2 + 3 * (count // step),)),
+            pltpu.VMEM((tile, 4 * width), bf16),
+            pltpu.VMEM((tile, depth), bf16),
+            pltpu.VMEM((tile, depth), bf16),
+            pltpu.VMEM((depth, 4 * width), bf16),
+            pltpu.VMEM((depth, 2 * count), bf16),
+            pltpu.VMEM((depth, count), bf16),
+            pltpu.SemaphoreType.DMA((4,)),
         ],
         compiler_params=_params(),
-        cost_estimate=_cost(2 * rows * depth * (4 * width + 6 * count), 18 << 20),
+        cost_estimate=_cost(4 * rows * depth * (4 * width + 6 * count), 28 << 20),
         name="mlp",
-    )(*[v for v, n in attended], x, cot, gain, weights, down, out_mate)
+    )(*[v for v, n in (*attended_a, *attended_b)], *x, *cot, gain, weights, down, out_mate)
 
 
 def _pull_groups(right, right_s, row_at, column_at, step, sems, base):
@@ -488,62 +512,56 @@
         at += rows
 
 
+def _mlp_grad_kernel(n, step, *refs):
+    normed, cot = refs[:2], refs[2 : 2 + n]
+    grads, hidden = refs[2 + n : 4 + n], refs[4 + n : 6 + n]
+    out_ref, left_s, right_s, sems = refs[6 + n :]
+    members = lambda pair: [v.at[m] for v in pair for m in (0, 1)]
+    wide = grads[0].shape[2]
+    rows = left_s.shape[0] // n
+    groups = _pull_groups(members(grads), right_s, 0, 0, step, sems, 0)
+    groups += _pull_groups(members(hidden), right_s, 0, wide, step, sems, 4 * (wide // step))
+    _start_all(groups)
+    for m in range(n):
+        left_s[m * rows : (m + 1) * rows, :] = normed[m // 2][m % 2]
+    for c, group in enumerate(groups):
+        at = slice(c * step, (c + 1) * step)
+        if c * step == wide:
+            _join(cot, left_s)
+        _wait_group(group)
+        out_ref[:, at] = _dot(left_s[...], right_s[:, at], TN).astype(out_ref.dtype)
+
+
+def mlp_grads(normed, cot, grads, hidden, block=256):
+    n = len(cot)
+    piece, depth = cot[0].shape
+    rows = n * piece
+    columns = grads[0].shape[2] + hidden[0].shape[2]
+    step = hidden[0].shape[2]
+    anywhere = pl.BlockSpec(memory_space=pl.ANY)
+    return pl.pallas_call(
+        functools.partial(_mlp_grad_kernel, n, step),
+        grid=(depth // block,),
+        out_shape=jax.ShapeDtypeStruct((depth, columns), jnp.bfloat16),
+        in_specs=[pl.BlockSpec((2, piece, block), lambda i: (0, 0, i))] * 2
+        + [pl.BlockSpec((piece, block), lambda i: (0, i))] * n
+        + [anywhere] * 4,
+        out_specs=_rows(block, columns),
+        scratch_shapes=[
+            pltpu.VMEM((rows, block), jnp.bfloat16),
+            pltpu.VMEM((rows, columns), jnp.bfloat16),
+            pltpu.SemaphoreType.DMA((n * (columns // step),)),
+        ],
+        compiler_params=_params(),
+        cost_estimate=_cost(2 * rows * depth * columns, 2 * rows * (depth + columns) + 2 * depth * columns),
+        name="mlp_grads",
+    )(*normed, *cot, *grads, *hidden)
+
+
 def _split_rows(acc, y, near, far):
     size = near.shape[1]
     near[...] = acc[pl.ds(pl.multiple_of(y * size, size), size), :].astype(near.dtype)[None]
     far[...] = acc[pl.ds(pl.multiple_of((1 - y) * size, size), size), :].astype(far.dtype)[None]
-
-
-def _grad_kernel(n, step, split, *refs):
-    if split:
-        y_ref, refs = refs[0], refs[1:]
-    left, right = refs[:n], refs[n : 2 * n]
-    outs = refs[2 * n : -3 - split]
-    left_s, right_s, sems = refs[len(refs) - 3 - split : len(refs) - split]
-    acc = refs[-1] if split else outs[0]
-    groups = _pull_groups(right, right_s, 0, 0, step, sems, 0)
-    _start_all(groups)
-    _join(left, left_s)
-    for c, group in enumerate(groups):
-        at = slice(c * step, (c + 1) * step)
-        _wait_group(group)
-        acc[:, at] = _dot(left_s[...], right_s[:, at], TN).astype(acc.dtype)
-    if split:
-        _split_rows(acc, y_ref[0], *outs)
-
-
-def row_grads(left, right, name, y=None, size=128):
-    n, depth = len(left), left[0].shape[1]
-    rows = sum(v.shape[0] for v in left)
-    columns = right[0].shape[1]
-    step = min(columns, 1024)
-    block = 2 * size
-    split = y is not None
-    anywhere = pl.BlockSpec(memory_space=pl.ANY)
-    if split:
-        out = [jax.ShapeDtypeStruct((depth // block, size, columns), jnp.bfloat16)] * 2
-        out_spec = [pl.BlockSpec((1, size, columns), lambda i: (i, 0, 0))] * 2
-    else:
-        out = jax.ShapeDtypeStruct((depth, columns), jnp.bfloat16)
-        out_spec = _rows(block, columns)
-    return pl.pallas_call(
-        functools.partial(_grad_kernel, n, step, split),
-        grid=(depth // block,),
-        out_shape=out,
-        in_specs=[_smem()] * split
-        + [pl.BlockSpec((v.shape[0], block), lambda i: (0, i)) for v in left]
-        + [anywhere] * n,
-        out_specs=out_spec,
-        scratch_shapes=[
-            pltpu.VMEM((rows, block), jnp.bfloat16),
-            pltpu.VMEM((rows, columns), jnp.bfloat16),
-            pltpu.SemaphoreType.DMA((n * (columns // step),)),
-        ]
-        + [pltpu.VMEM((block, columns), jnp.float32)] * split,
-        compiler_params=_params(),
-        cost_estimate=_cost(2 * rows * depth * columns, 2 * rows * (depth + columns) + 2 * depth * columns),
-        name=name,
-    )(*([y] * split), *left, *right)
 
 
 def _qkv_grad_kernel(n, y_ref, *refs):
@@ -590,45 +608,63 @@
             pltpu.SemaphoreType.DMA((n,)),
         ],
         compiler_params=_params(),
-        cost_estimate=_cost(2 * rows * depth * columns, 2 * rows * (depth + columns) + 2 * depth * columns),
+        cost_estimate=_cost(0, 0),
         name="qkv_grads",
     )(y, *normed, *grads, weight, gain, mlp_sum)
 
 
-def _out_grad_kernel(y_ref, left_ref, a0, a1, a2, a3, near, far, right_s, acc):
+def _out_grad_kernel(left_ref, a0, a1, a2, a3, mine, theirs, right_s):
     width = a0.shape[2]
 
     @pl.when(pl.program_id(0) == 0)
     def _():
-        for i, a in enumerate((a0, a1, a2, a3)):
+        for i, a in enumerate((a0, a2, a1, a3)):
             right_s[:, i * width : (i + 1) * width] = a[0]
 
-    acc[...] = _dot(left_ref[...], right_s[...], TN)
-    _split_rows(acc, y_ref[0], near, far)
-
-
-def out_grads(y, left, attended, size):
+    total = _dot(left_ref[...], right_s[...], TN).astype(mine.dtype)
+    mine[...] = total[:, : 2 * width]
+    theirs[...] = total[:, 2 * width :]
+
+
+def out_grads(left, attended, block=256):
     rows, depth = left.shape
     width = attended[0][0].shape[2]
-    block = 2 * size
-    out = jax.ShapeDtypeStruct((depth // block, size, 4 * width), jnp.bfloat16)
-    out_spec = pl.BlockSpec((1, size, 4 * width), lambda i: (i, 0, 0))
+    out = jax.ShapeDtypeStruct((depth, 2 * width), jnp.bfloat16)
     member = lambda n: pl.BlockSpec((1, rows, width), lambda i: (n, 0, 0))
     return pl.pallas_call(
         _out_grad_kernel,
         grid=(depth // block,),
         out_shape=[out, out],
-        in_specs=[_smem(), pl.BlockSpec((rows, block), lambda i: (0, i))]
-        + [member(n) for v, n in attended],
-        out_specs=[out_spec, out_spec],
-        scratch_shapes=[
-            pltpu.VMEM((rows, 4 * width), jnp.bfloat16),
-            pltpu.VMEM((block, 4 * width), jnp.float32),
-        ],
+        in_specs=[pl.BlockSpec((rows, block), lambda i: (0, i))] + [member(n) for v, n in attended],
+        out_specs=[_rows(block, 2 * width)] * 2,
+        scratch_shapes=[pltpu.VMEM((rows, 4 * width), jnp.bfloat16)],
         compiler_params=_params(),
         cost_estimate=_cost(8 * rows * depth * width, 2 * rows * (depth + 4 * width) + 8 * depth * width),
         name="out_grads",
-    )(y, left, *[v for v, n in attended])
+    )(left, *[v for v, n in attended])
+
+
+def _pair_kernel(y_ref, a_ref, b_ref, near, far, acc):
+    acc[...] = a_ref[...].astype(jnp.float32) + b_ref[...].astype(jnp.float32)
+    _split_rows(acc, y_ref[0], near, far)
+
+
+def pair_sum(y, a, b, size):
+    depth, columns = a.shape
+    block = 2 * size
+    out = jax.ShapeDtypeStruct((depth // block, size, columns), jnp.bfloat16)
+    out_spec = pl.BlockSpec((1, size, columns), lambda i: (i, 0, 0))
+    return pl.pallas_call(
+        _pair_kernel,
+        grid=(depth // block,),
+        out_shape=[out, out],
+        in_specs=[_smem()] + [_rows(block, columns)] * 2,
+        out_specs=[out_spec, out_spec],
+        scratch_shapes=[pltpu.VMEM((block, columns), jnp.float32)],
+        compiler_params=_params(),
+        cost_estimate=_cost(0, 6 * depth * columns),
+        name="pair_sum",
+    )(y, a, b)
 
 
 def _fold_kernel(z_ref, near, passed, *outs):
@@ -647,7 +683,7 @@
         in_specs=[_smem(), _full(near.shape), _full(near.shape)],
         out_specs=[_full((size, columns))] * count,
         compiler_params=_params(),
-        cost_estimate=_cost(0, 6 * count * size * columns),
+        cost_estimate=_cost(0, 0),
         name="fold",
     )(z, near, passed)
 
@@ -719,7 +755,7 @@
         in_specs=[_rows(tile, columns), _full((depth, columns))] + [_rows(tile, depth)] * len(extra),
         out_specs=_rows(tile, depth),
         compiler_params=_params(),
-        cost_estimate=_cost(2 * rows * depth * columns, 2 * rows * (columns + 2 * depth)),
+        cost_estimate=_cost(0, 0),
         name="project_back",
     )(grad, weight, *extra)
 
@@ -996,13 +1032,23 @@
                 _mask(heads, True, False), False, [(at, SEG) for at in ats],
             )
 
-        def trunk_chunk(c, carry):
+        def trunk_step(c):
             at = pl.multiple_of(c * QB, QB)
             here = pl.ds(at, QB)
             step(k_s[here, :], v_s[here, :], lambda of: kt_s[of, here], None, False, [(at, QB)])
+
+        def trunk_pair(c, carry):
+            trunk_step(2 * c)
+            trunk_step(2 * c + 1)
             return carry
 
-        lax.fori_loop(0, jnp.minimum(b, trunk_blocks), trunk_chunk, 0)
+        count = jnp.minimum(b, trunk_blocks)
+        lax.fori_loop(0, lax.div(count, 2), trunk_pair, 0)
+
+        @pl.when(lax.rem(count, 2) == 1)
+        def _():
+            trunk_step(count - 1)
+
         q_s[own, :] = (acc_s[...] * scale).T.astype(jnp.bfloat16)
         return carry
 
@@ -1141,11 +1187,10 @@
     out_shard = out_weight.astype(bf16).T
     gate_up_shard = gate_up_weight.astype(bf16).transpose(1, 0, 2).reshape(shard, 2 * hidden_width)
     first_line = line_hops(jnp.concatenate([qkv_shard, gains_shard], axis=1))
-    beyond = [across(block_input[:half])]
+    beyond = [across(block_input[:half]), across(block_input[half:])]
     rest_shard = jnp.concatenate([gate_up_shard, out_shard, across(out_shard)], axis=1)
-    rest = lax.all_gather(after(rest_shard, *first_line), "dp", axis=0, tiled=True)
-    first_far = [beside(first_line[0])] + [beside(after(v, beyond[0])) for v in first_line[1:]]
-    beyond.append(across(after(block_input[half:], beyond[0])))
+    rest = lax.all_gather(after(rest_shard, beyond[0], *first_line), "dp", axis=0, tiled=True)
+    first_far = [beside(v) for v in first_line]
     near_x = mate(block_input)
     first = spread_hops(first_line, first_far)
     down_line = line_hops(after(down_weight.astype(bf16).T, *first_far))
@@ -1165,45 +1210,43 @@
     cot_near = mate(after(cot_low, own))
     far, lse_far = attention_forward(after(info_far, own), projected, heads)
     far_m, own_xm = mate(far), mate(after(own_x, far))
-    far_x = across(after(far, own_x))
+    far_x = across(far)
     down_low = spread_hops(down_line, after_all(down_far, far))
     cot_rows = [cot_low, cot_near, cot_x, mate(after(cot_x, far))]
     out_far = mate(after(rest[:, 2 * hidden_width :], down_low))
 
-    def run_mlp(attended, j, cot):
-        return mlp(attended, inputs[j], cot, gain_mlp, rest, down_low, out_far, j == 0)
-
-    stage = [None] * 4
-    stage[3] = run_mlp([(far, 1), (far_m, 0), (own_x, 1), (own_xm, 0)], 3, cot_rows[3])
-    stage[2] = run_mlp(
-        [(far, 0), (far_m, 1), (own_x, 0), (own_xm, 1)], 2, after(cot_rows[2], stage[3][0])
-    )
-    far_xm = mate(after(far_x, stage[3][0]))
-    passed = (stage[2][0].astype(f32) + mate(stage[3][0]).astype(f32)).astype(bf16)
-    passed_x = [across(passed[:half])]
-    stage[1] = run_mlp(
-        [(own, 1), (own_m, 0), (far_x, 1), (far_xm, 0)], 1, after(cot_rows[1], passed)
-    )
-    passed_x.append(across(after(passed[half:], passed_x[0])))
-    own_rows = [(own, 0), (own_m, 1), (far_x, 0), (far_xm, 1)]
-    stage[0] = run_mlp(own_rows, 0, after(cot_rows[0], stage[1][0], passed_x[0]))
-    part, hidden, grads_low, normed_mlp, branch = [[s[n] for s in stage] for n in range(5)]
-    residual_mid = stage[0][5]
-    mlp_parts = [part[0], mate(part[1]), jnp.concatenate(passed_x, axis=0)]
-
+    own_rows = [(own, 0), (own_m, 1), (far_x, 0), None]
+    hidden_far, grads_far, normed_far, part3, part2, branch3, branch2 = mlp(
+        [(far, 1), (far_m, 0), (own_x, 1), (own_xm, 0)],
+        [(far, 0), (far_m, 1), (own_x, 0), (own_xm, 1)],
+        [inputs[3], inputs[2]], [cot_rows[3], cot_rows[2]], gain_mlp, rest, down_low, out_far, False,
+    )
+    far_xm = mate(after(far_x, part3))
+    own_rows[3] = (far_xm, 1)
+    passed = (part2.astype(f32) + mate(after(part3, far_x)).astype(f32)).astype(bf16)
+    passed_x = across(passed)
+    hidden_own, grads_own, normed_own, part1, part0, branch1, branch0, residual_mid = mlp(
+        [(own, 1), (own_m, 0), (far_x, 1), (far_xm, 0)], own_rows,
+        [inputs[1], inputs[0]], [after(cot_rows[1], passed), cot_rows[0]],
+        gain_mlp, rest, down_low, out_far, True,
+    )
+    mlp_parts = [part0, mate(after(part1, passed_x)), passed_x]
+
+    grad_sum = mlp_grads(
+        [normed_far, normed_own],
+        [cot_rows[n] for n in (3, 2, 1, 0)],
+        [grads_far, grads_own],
+        [hidden_far, hidden_own],
+    )
     mid_grad, attn_grad, g0, g1, g2, g3, mlp_sum = middle(
-        mlp_parts, residual_mid, cotangent, gain_mlp, rest, out_far
-    )
+        [after(mlp_parts[0], grad_sum), *mlp_parts[1:]], residual_mid, cotangent, gain_mlp, rest, out_far
+    )
+    grad_sum = lax.psum_scatter(grad_sum, "dp", scatter_dimension=0, tiled=True)
     g_x, g_c, g_m = across(g2), corner(g3), mate(g1)
-    down_pair = row_grads([after(cot_low, attn_grad), *cot_rows[1:]], hidden, "down_grads", y, shard)
-    down_y = beside(down_pair[1])
-    gate_up_grad = row_grads(
-        [after(normed_mlp[0], down_pair[1]), *normed_mlp[1:]], grads_low, "gate_up_grads"
-    )
-    gate_up_sum = lax.psum_scatter(gate_up_grad, "dp", scatter_dimension=0, tiled=True)
-    down_chunks = fold_hops(down_pair[0], after(down_y, gate_up_grad))
-    branch_passed = (branch[2].astype(f32) + mate(branch[3]).astype(f32)).astype(bf16)
-    out_pair = out_grads(y, after(attn_grad, down_chunks[1]), own_rows, shard)
+    out_mine, out_theirs = out_grads(attn_grad, own_rows)
+    out_theirs = mate(out_theirs)
+    branch_passed = (branch2.astype(f32) + mate(branch3).astype(f32)).astype(bf16)
+    out_pair = pair_sum(y, out_mine, after(out_theirs, branch_passed), shard)
     out_y = beside(out_pair[1])
     branch_x = across(after(branch_passed, g_x, g_c))
 
@@ -1211,41 +1254,34 @@
     projected_grad = attention_backward(
         info_own, projected, [own, far], bwd_grads, [lse_own, lse_far], heads
     )
-    out_chunks = fold_hops(out_pair[0], after(out_y, *projected_grad))
+    out_chunks = fold_hops(out_pair[0], after(out_y, *projected_grad, branch_x))
     out_received = send_hops(out_chunks)
-    down_received = send_hops(down_chunks)
     qkv_pair = qkv_grads(
-        y, [after(normed_attn[0], out_chunks[1]), *normed_attn[1:]], projected_grad, first, gain_attn, mlp_sum, shard
+        y, normed_attn, after_all(projected_grad, out_chunks[1]), first, gain_attn, mlp_sum, shard
     )
     qkv_y = beside(qkv_pair[1])
-    back3 = project_back(after(projected_grad[3], qkv_pair[1], branch_x), first)
+    back3 = project_back(after(projected_grad[3], qkv_pair[1]), first)
     back2 = project_back(projected_grad[2], first, mate(back3))
-    back_x = [across(back2[:half])]
+    back_x = across(back2)
     back1 = project_back(after(projected_grad[1], back2, *out_received), first)
-    back_m = mate(back1)
     back0 = project_back(after(projected_grad[0], back1), first)
-    back_x.append(across(after(back2[half:], back_x[0])))
-    branch_sum = branch[0].astype(f32) + mate(branch[1]).astype(f32)
+    branch_sum = branch0.astype(f32) + mate(branch1).astype(f32)
     block_output = residual_mid + branch_sum + after(branch_x, back0).astype(f32)
-    qkv_chunks = fold_hops(qkv_pair[0], after(qkv_y, back_x[0], block_output))
+    qkv_chunks = fold_hops(qkv_pair[0], after(qkv_y, back0, block_output))
     qkv_received = send_hops(qkv_chunks)
-    down_out = sum_hops(after_all(down_received, qkv_chunks[1])).T
-    gate_up_out = (
-        after(gate_up_sum, qkv_chunks[1]).astype(f32).reshape(shard, 2, hidden_width).transpose(1, 0, 2)
-    )
-    out_sum = sum_hops(after_all(out_received, qkv_chunks[1]))
-    quarter = lambda i: out_sum[:, i * width : (i + 1) * width]
-    from_mate = mate(jnp.concatenate([quarter(1), quarter(3)], axis=1).astype(bf16)).astype(f32)
-    out_out = quarter(0) + from_mate[:, :width]
-    out_x = across((quarter(2) + from_mate[:, width:]).astype(bf16))
-    out_out = (out_out + out_x.astype(f32)).T
-    back_x = jnp.concatenate([back_x[0], after(back_x[1], out_x, gate_up_out, down_out)], axis=0)
-    input_grad = last([back0, back_m, back_x], block_input, mid_grad, gain_attn)
+    back_m = mate(after(back1, qkv_y))
+    input_grad = last([back0, back_m, after(back_x, qkv_chunks[1])], block_input, mid_grad, gain_attn)
+    grad_sum = after(grad_sum, input_grad).astype(f32)
+    down_out = grad_sum[:, 2 * hidden_width :].T
+    gate_up_out = grad_sum[:, : 2 * hidden_width].reshape(shard, 2, hidden_width).transpose(1, 0, 2)
+    out_sum = sum_hops(out_received)
     qkv_sum = sum_hops(after_all(qkv_received, input_grad))
     qkv_out = qkv_sum[:, : 3 * width].reshape(shard, 3, width).transpose(1, 0, 2)
-    gains_out = qkv_sum[:, 3 * width :]
-    gains_out = gains_out + mate(gains_out.astype(bf16)).astype(f32)
-    gains_out = (gains_out + across(gains_out.astype(bf16)).astype(f32))[:, :2].T
+    gains_sum = qkv_sum[:, 3 * width :]
+    gains_sum = gains_sum + mate(gains_sum.astype(bf16)).astype(f32)
+    from_x = across(jnp.concatenate([out_sum[:, width:], gains_sum], axis=1).astype(bf16)).astype(f32)
+    out_out = (out_sum[:, :width] + from_x[:, :width]).T
+    gains_out = (gains_sum + from_x[:, width:])[:, :2].T
     return (block_output, input_grad, gains_out, qkv_out, out_out, gate_up_out, down_out)
 
 

time: 472 us -> 438 us (0.928)
  starting transfers between devices: 78.9 us -> 51.2 us
  waiting for transfers between devices: 83.3 us -> 94.5 us
  Pallas kernels: 244 us -> 236 us
  other arithmetic: 20.2 us -> 13.8 us
    ppermute x15 -> x12, starting transfers between devices: 43.8 us -> 25.6 us  [ahead(): return lax.ppermute(x, 'dp', [(i, (i + 2 * step) % 8) for i in range(8)])]
    ppermute x15 -> x12, waiting for transfers between devices: 39.3 us -> 21.8 us  [ahead(): return lax.ppermute(x, 'dp', [(i, (i + 2 * step) % 8) for i in range(8)])]
    ppermute x11 -> x10, waiting for transfers between devices: 14.1 us -> 31.2 us  [beside(): return lax.ppermute(x, 'dp', [(i, i ^ 1) for i in range(8)])]
    ppermute x14 -> x11, starting transfers between devices: 17.9 us -> 9.3 us  [across(): return lax.ppermute(x, 'tensor', [(i, i ^ 2) for i in range(4)])]
    ppermute x1, waiting for transfers between devices: 0.01 us -> 6.02 us  [corner(): return lax.ppermute(x, 'tensor', [(i, i ^ 3) for i in range(4)])]
    pallas_call x6 -> x4, Pallas kernels: 94.8 us -> 91.7 us  [the longest x2 63 us: mlp(): pl.pallas_call(functools.partial(_mlp_kernel, keep), grid=(2 * steps,), o...]
    unnamed x119 -> x93, local copies, waits for them, and re-layouts: 15.1 us -> 13.9 us
    ppermute x11 -> x10, starting transfers between devices: 12.9 us -> 11.9 us  [beside(): return lax.ppermute(x, 'dp', [(i, i ^ 1) for i in range(8)])]
  transfers between devices with their start and end apart: 61 -> 54, of which waited for: 15 -> 23; matrix products, arithmetic and copies ran while one was open for 7% -> 6% of each run, Pallas kernels for 48% -> 54%
where the time goes in v2:
time: 438 us; the launch traced here: 434 us
  Pallas kernels  236 us (54%)
  waiting for transfers between devices  94.5 us (22%)
  starting transfers between devices  51.2 us (12%)
  local copies, waits for them, and re-layouts  23.7 us (5%)
  between operations  14.9 us (3%)
  other arithmetic  13.8 us (3%)
    pallas_call x2, Pallas kernels, mlp(): pl.pallas_call(functools.partial(_mlp_kernel, keep), grid=(2 * steps,), o...  63 us
    pallas_call x1, Pallas kernels, attention_backward(): pl.pallas_call(functools.partial(_attn_bwd_kernel, heads), out_shape=[jax...  44 us
    ppermute x10, waiting for transfers between devices, beside(): return lax.ppermute(x, 'dp', [(i, i ^ 1) for i in range(8)])  31.2 us
    pallas_call x2, Pallas kernels, attention_forward(): pl.pallas_call(functools.partial(_attn_fwd_kernel, heads, len(pieces)), o...  31 us
    ppermute x12, starting transfers between devices, ahead(): return lax.ppermute(x, 'dp', [(i, (i + 2 * step) % 8) for i in range(8)])  25.6 us
    pallas_call x1, Pallas kernels, mlp_grads(): pl.pallas_call(functools.partial(_mlp_grad_kernel, n, step), grid=(depth...  25 us
    ppermute x11, waiting for transfers between devices, across(): return lax.ppermute(x, 'tensor', [(i, i ^ 2) for i in range(4)])  24.3 us
    ppermute x12, waiting for transfers between devices, ahead(): return lax.ppermute(x, 'dp', [(i, (i + 2 * step) % 8) for i in range(8)])  21.8 us
  transfers between devices with their start and end apart: 54, of which 23 were waited for; matrix products, arithmetic and copies ran while one was open for 6% of the time, Pallas kernels for 54%

profile of v2, /device:TPU:0, one launch (start us, length us, event | category | flops | bytes accessed | tf_op | source)
XLA Modules:
  0.0 433.7 jit_solution(17822583251027679073)
XLA Ops:
  7.2 2.3 fusion.8
  9.5 2.9 collective-permute-start.8
  12.9 2.7 collective-permute-start.3
  18.5 10.1 %collective-permute-done.18 = bf16[128,256]{1,0:T(8,128)(2,1)S(1)} collective-permute-done((bf16[128,256]{1,0:T(8,128)(2,1)S(1)}, bf16[128,256]{1,0:T(8,128)(2,1)S(1)}, u32[]{:S(2)}, u32[]{:S(2)}) %collective-permute-start.18) | collective-permute-done | bytes 65568 | tf_op jit(solution)/shard_map/ppermute | solution.py:1108
  29.4 2.7 collective-permute-done.3.refs_3_
  36.5 3.0 collective-permute-done.4.refs_4_
  39.4 2.5 collective-permute-start.5
  44.0 2.2 convert_element_type.94.refs_11_.refs_5_
  47.6 6.9 %collective-permute-done.6.refs_6_ = bf16[128,896]{1,0:T(8,128)(2,1)} collective-permute-done((bf16[128,896]{1,0:T(8,128)(2,1)}, bf16[128,896]{1,0:T(8,128)(2,1)}, u32[]{:S(2)}, u32[]{:S(2)}) %collective-permute-start.6) | collective-permute-done | bytes 229408 | tf_op jit(solution)/shard_map/ppermute | solution.py:1116
  54.5 5.6 %collective-permute-done.5.refs_5_ = bf16[128,896]{1,0:T(8,128)(2,1)S(1)} collective-permute-done((bf16[128,896]{1,0:T(8,128)(2,1)}, bf16[128,896]{1,0:T(8,128)(2,1)S(1)}, u32[]{:S(2)}, u32[]{:S(2)}) %collective-permute-start.5) | collective-permute-done | bytes 229408 | tf_op jit(solution)/shard_map/ppermute | solution.py:1116
  60.1 7.8 %collective-permute-start.21 = (bf16[128,1024]{1,0:T(8,128)(2,1)S(1)}, bf16[128,1024]{1,0:T(8,128)(2,1)}, u32[]{:S(2)}, u32[]{:S(2)}) collective-permute-start(bf16[128,1024]{1,0:T(8,128)(2,1)S(1)} %bitcast.39), channel_id=1, source_target_pairs={{0,16},{4,20},{8,24},{12,28},{16,0},{20,4},{24,8},{28,12},{1,17},{... | collective-permute-start | bytes 786440 | tf_op jit(solution)/shard_map/ppermute | solution.py:1120
  70.1 2.9 place.2.w_ref.refs_8_
  74.2 2.0 constant_dynamic-update-slice_fusion.1
  79.4 6.9 %project.2 = (bf16[640,1024]{1,0:T(8,128)(2,1)}, bf16[640,1024]{1,0:T(8,128)(2,1)}, bf16[640,768]{1,0:T(8,128)(2,1)}, bf16[640,768]{1,0:T(8,128)(2,1)}) custom-call(bf16[640,1024]{1,0:T(8,128)(2,1)} %x_ref.1, bf16[640,1024]{1,0:T(8,128)(2,1)} %collective-permute-done.x1_ref.refs_8_, f32[1,1024]{1,0:T(1,128)} %get-tuple-element.224.gain_ref.refs_9_, ...), custom_call_target="tpu_custom_call" | custom-call | flops 12079595520 | bytes 43253760 | tf_op jit(solution)/shard_map/project/pallas_call | solution.py:337
  86.3 7.1 %project.3 = (bf16[640,1024]{1,0:T(8,128)(2,1)}, bf16[640,1024]{1,0:T(8,128)(2,1)}, bf16[640,768]{1,0:T(8,128)(2,1)}, bf16[640,768]{1,0:T(8,128)(2,1)}) custom-call(bf16[640,1024]{1,0:T(8,128)(2,1)} %constant_dynamic-update-slice_fusion.x0_ref.refs_9_, bf16[640,1024]{1,0:T(8,128)(2,1)} %collective-permute-done.10.x1_ref.refs_8_, ...), custom_call_target="tpu_custom_call" | custom-call | flops 12079595520 | bytes 43253760 | tf_op jit(solution)/shard_map/project/pallas_call | solution.py:337
  93.4 13.1 %attn_fwd.2 = (bf16[2,640,256]{2,1,0:T(8,128)(2,1)}, f32[8,1280]{1,0:T(8,128)}) custom-call(s32[10]{0:T(128)} %get-tuple-element.225.info_ref, bf16[640,768]{1,0:T(8,128)(2,1)} %get-tuple-element.105.refs_0_, bf16[640,768]{1,0:T(8,128)(2,1)} %get-tuple-element.106.refs_1_, bf16[640,768]{1,0:T(8,128)(2,1)} %get-tuple-element.108.refs_2_, ...), custom_call_target="tpu_custom_call" | custom-call | flops 22020096000 | bytes 31457280 | tf_op jit(solution)/shard_map/attn_fwd/pallas_call | solution.py:924
  106.5 3.6 collective-permute-done.14.refs_11_.refs_3_
  114.1 2.8 collective-permute-start.15
  116.9 18.0 %attn_fwd.3 = (bf16[2,640,256]{2,1,0:T(8,128)(2,1)}, f32[8,1280]{1,0:T(8,128)}) custom-call(s32[10]{0:T(128)} %get-tuple-element.111.info_ref, bf16[640,768]{1,0:T(8,128)(2,1)} %get-tuple-element.105.refs_0_, bf16[640,768]{1,0:T(8,128)(2,1)} %get-tuple-element.106.refs_1_, bf16[640,768]{1,0:T(8,128)(2,1)} %get-tuple-element.108.refs_2_, ...), custom_call_target="tpu_custom_call" | custom-call | flops 22020096000 | bytes 31457280 | tf_op jit(solution)/shard_map/attn_fwd/pallas_call | solution.py:924
  135.0 3.2 collective-permute-done.24.refs_6_
  138.2 5.2 %collective-permute-done.25.refs_7_ = bf16[128,1024]{1,0:T(8,128)(2,1)S(1)} collective-permute-done((bf16[128,1024]{1,0:T(8,128)(2,1)}, bf16[128,1024]{1,0:T(8,128)(2,1)S(1)}, u32[]{:S(2)}, u32[]{:S(2)}) %collective-permute-start.25) | collective-permute-done | bytes 262176 | tf_op jit(solution)/shard_map/ppermute | solution.py:1116
  144.1 3.0 place.3.refs_14_
  151.0 3.2 collective-permute-done.13.refs_1_.refs_5_
  157.0 31.2 %mlp.2 = (bf16[2,640,1024]{2,1,0:T(8,128)(2,1)}, bf16[2,640,2048]{2,1,0:T(8,128)(2,1)}, bf16[2,640,1024]{2,1,0:T(8,128)(2,1)}, bf16[640,1024]{1,0:T(8,128)(2,1)}...) custom-call(bf16[2,640,256]{2,1,0:T(8,128)(2,1)} %get-tuple-element.112.refs_0_.refs_4_.refs_5_, ...), custom_call_target="tpu_custom_call" | custom-call | flops 112742891520 | bytes 176160768 | tf_op jit(solution)/shard_map/mlp/pallas_call | solution.py:449
  189.4 2.6 collective-permute-done.29
  195.9 31.7 %mlp.3 = (bf16[2,640,1024]{2,1,0:T(8,128)(2,1)}, bf16[2,640,2048]{2,1,0:T(8,128)(2,1)}, bf16[2,640,1024]{2,1,0:T(8,128)(2,1)}, bf16[640,1024]{1,0:T(8,128)(2,1)}...) custom-call(bf16[2,640,256]{2,1,0:T(8,128)(2,1)} %get-tuple-element.11, ...), custom_call_target="tpu_custom_call" | custom-call | flops 112742891520 | bytes 176160768 | tf_op jit(solution)/shard_map/mlp/pallas_call | solution.py:449
  228.1 25.0 %mlp_grads.1 = bf16[1024,3072]{1,0:T(8,128)(2,1)} custom-call(bf16[2,640,1024]{2,1,0:T(8,128)(2,1)} %get-tuple-element.140.refs_0_, bf16[2,640,1024]{2,1,0:T(8,128)(2,1)} %get-tuple-element.141.refs_1_, bf16[640,1024]{1,0:T(8,128)(2,1)} %copy-done.30, bf16[640,1024]{1,0:T(8,128)(2,1)} %copy-done.29, bf16[640,1024]{1,0:T(8,128)(2,1)} %copy-done.31, ...), custom_call_target="tpu_custom_call" | custom-call | flops 96636764160 | bytes 163577856 | tf_op jit(solution)/shard_map/mlp_grads/pallas_call | solution.py:542
  254.1 7.5 %middle.1 = (f32[640,1024]{1,0:T(8,128)}, bf16[640,1024]{1,0:T(8,128)(2,1)}, bf16[640,256]{1,0:T(8,128)(2,1)}, bf16[640,256]{1,0:T(8,128)(2,1)}, bf16[640,256]{1...) custom-call(bf16[640,1024]{1,0:T(8,128)(2,1)} %get-tuple-element.146.p0, bf16[640,1024]{1,0:T(8,128)(2,1)} %copy-done.32, ...), custom_call_target="tpu_custom_call" | custom-call | flops 8053063680 | bytes 78643200 | tf_op jit(solution)/shard_map/middle/pallas_call | solution.py:717
  261.7 5.2 %out_grads.1 = (bf16[1024,512]{1,0:T(8,128)(2,1)}, bf16[1024,512]{1,0:T(8,128)(2,1)}) custom-call(bf16[640,1024]{1,0:T(8,128)(2,1)} %get-tuple-element.154.left_ref, bf16[2,640,256]{2,1,0:T(8,128)(2,1)} %get-tuple-element.114.refs_0_.refs_4_.a0, bf16[2,640,256]{2,1,0:T(8,128)(2,1)} %collective-permute-done.11.refs_1_.refs_5_.a1, ...), custom_call_target="tpu_custom_call" | custom-call | flops 8053063680 | bytes 28311552 | tf_op jit(solution)/shard_map/out_grads/pallas_call | solution.py:634
  271.9 5.9 %collective-permute-done.34.refs_8_ = bf16[640,256]{1,0:T(8,128)(2,1)S(1)} collective-permute-done((bf16[640,256]{1,0:T(8,128)(2,1)}, bf16[640,256]{1,0:T(8,128)(2,1)S(1)}, u32[]{:S(2)}, u32[]{:S(2)}) %collective-permute-start.34) | collective-permute-done | bytes 327712 | tf_op jit(solution)/shard_map/ppermute | solution.py:1108
  277.8 6.0 %collective-permute-done.35.refs_9_ = bf16[640,256]{1,0:T(8,128)(2,1)} collective-permute-done((bf16[640,256]{1,0:T(8,128)(2,1)}, bf16[640,256]{1,0:T(8,128)(2,1)}, u32[]{:S(2)}, u32[]{:S(2)}) %collective-permute-start.35) | collective-permute-done | bytes 327712 | tf_op jit(solution)/shard_map/ppermute | solution.py:1112
  284.3 3.7 pair_sum.1
  288.0 44.0 %attn_bwd.1 = (bf16[640,768]{1,0:T(8,128)(2,1)}, bf16[640,768]{1,0:T(8,128)(2,1)}, bf16[640,768]{1,0:T(8,128)(2,1)}, bf16[640,768]{1,0:T(8,128)(2,1)}) custom-call(s32[10]{0:T(128)} %get-tuple-element.225.info_ref, bf16[640,768]{1,0:T(8,128)(2,1)} %get-tuple-element.105.refs_0_, bf16[640,768]{1,0:T(8,128)(2,1)} %get-tuple-element.106.refs_1_, ...), custom_call_target="tpu_custom_call" | custom-call | flops 110100480000 | bytes 62914560 | tf_op jit(solution)/shard_map/attn_bwd/pallas_call | solution.py:1070
  332.8 2.0 fold.2
  334.9 10.8 %qkv_grads.1 = (bf16[4,128,896]{2,1,0:T(8,128)(2,1)}, bf16[4,128,896]{2,1,0:T(8,128)(2,1)}) custom-call(s32[1]{0:T(128)} %bitcast.10.y_ref, bf16[640,1024]{1,0:T(8,128)(2,1)} %get-tuple-element.169.refs_0_, bf16[640,1024]{1,0:T(8,128)(2,1)} %get-tuple-element.170.refs_1_, bf16[640,1024]{1,0:T(8,128)(2,1)} %get-tuple-element.171.refs_2_, ...), custom_call_target="tpu_custom_call" | custom-call | tf_op jit(solution)/shard_map/qkv_grads/pallas_call | solution.py:595
  345.7 3.9 project_back.4
  355.8 4.2 project_back.5
  360.0 9.7 %collective-permute-done.41 = bf16[128,512]{1,0:T(8,128)(2,1)S(1)} collective-permute-done((bf16[128,512]{1,0:T(8,128)(2,1)S(1)}, bf16[128,512]{1,0:T(8,128)(2,1)S(1)}, u32[]{:S(2)}, u32[]{:S(2)}) %collective-permute-start.41) | collective-permute-done | bytes 131104 | tf_op jit(solution)/shard_map/ppermute | solution.py:1120
  370.4 3.8 project_back.6
  374.2 7.2 %collective-permute-done.44.passed = bf16[4,128,896]{2,1,0:T(8,128)(2,1)} collective-permute-done((bf16[4,128,896]{2,1,0:T(8,128)(2,1)}, bf16[4,128,896]{2,1,0:T(8,128)(2,1)}, u32[]{:S(2)}, u32[]{:S(2)}) %collective-permute-start.44) | collective-permute-done | bytes 917536 | tf_op jit(solution)/shard_map/ppermute | solution.py:1116
  381.5 3.9 project_back.7.p0
  385.4 4.2 convert_add_fusion
  389.6 2.5 fold.3
  392.0 5.6 %collective-permute-start.47 = (bf16[128,896]{1,0:T(8,128)(2,1)}, bf16[128,896]{1,0:T(8,128)(2,1)S(1)}, u32[]{:S(2)}, u32[]{:S(2)}) collective-permute-start(bf16[128,896]{1,0:T(8,128)(2,1)} %get-tuple-element.196), channel_id=1, source_target_pairs={{0,16},{4,20},{8,24},{12,28},{16,0},{20,4},{24,8},{28,12},{1,17},{... | collective-permute-start | bytes 688136 | tf_op jit(solution)/shard_map/ppermute | solution.py:1120
  400.7 5.1 %last.1 = f32[640,1024]{1,0:T(8,128)} custom-call(bf16[640,1024]{1,0:T(8,128)(2,1)} %project_back.7.p0, bf16[640,1024]{1,0:T(8,128)(2,1)} %collective-permute-done.45.p1, bf16[640,1024]{1,0:T(8,128)(2,1)} %collective-permute-done.46.p2, bf16[640,1024]{1,0:T(8,128)(2,1)} %x_ref.1, f32[640,1024]{1,0:T(8,128)} %get-tuple-element.194.mid_ref, ...), custom_call_target="tpu_custom_call" | custom-call | bytes 62914560 | tf_op jit(solution)/shard_map/last/pallas_call | solution.py:775
  405.8 3.5 collective-permute-done.47
  409.3 5.9 %collective-permute-done.49 = bf16[128,896]{1,0:T(8,128)(2,1)S(1)} collective-permute-done((bf16[128,896]{1,0:T(8,128)(2,1)}, bf16[128,896]{1,0:T(8,128)(2,1)S(1)}, u32[]{:S(2)}, u32[]{:S(2)}) %collective-permute-start.49) | collective-permute-done | bytes 229408 | tf_op jit(solution)/shard_map/ppermute | solution.py:1120
  417.9 3.7 collective-permute-done.51
  (213 shorter events, 60.4 us)
Async XLA Ops:
  7.2 141.8 %all-gather.2.cloned.1.call-start = ((), (), s32[]{:S(2)}) async-start(), calls=%async_computation.1 | async-start | bytes 5898240 | tf_op jit(solution)/shard_map/all_gather | solution.py:1192
  9.5 22.6 %collective-permute-start.8 = (bf16[320,1024]{1,0:T(8,128)(2,1)S(1)}, bf16[320,1024]{1,0:T(8,128)(2,1)S(1)}, u32[]{:S(2)}, u32[]{:S(2)}) collective-permute-start(bf16[320,1024]{1,0:T(8,128)(2,1)S(1)} %get-tuple-element.222), channel_id=1, source_target_pairs={{0,2},{1,3},{2,0},{3,1},{4,6},{5,7},{6,4},{7,5},{8,10},{9,11},{10,... | collective-permute-start | bytes 1966088 | tf_op jit(solution)/shard_map/ppermute | solution.py:1108
  12.9 19.2 %collective-permute-start.3 = (bf16[128,896]{1,0:T(8,128)(2,1)S(1)}, bf16[128,896]{1,0:T(8,128)(2,1)}, u32[]{:S(2)}, u32[]{:S(2)}) collective-permute-start(bf16[128,896]{1,0:T(8,128)(2,1)S(1)} %fusion.1.refs_0_), channel_id=1, source_target_pairs={{0,16},{4,20},{8,24},{12,28},{16,0},{20,4},{24,8},{28,12},{1,17},{... | collective-permute-start | bytes 688136 | tf_op jit(solution)/shard_map/ppermute | solution.py:1120
  15.6 16.5 %collective-permute-start.2 = (bf16[128,896]{1,0:T(8,128)(2,1)S(1)}, bf16[128,896]{1,0:T(8,128)(2,1)}, u32[]{:S(2)}, u32[]{:S(2)}) collective-permute-start(bf16[128,896]{1,0:T(8,128)(2,1)S(1)} %fusion.1.refs_0_), channel_id=1, source_target_pairs={{0,24},{4,28},{8,0},{12,4},{16,8},{20,12},{24,16},{28,20},{1,25},{... | collective-permute-start | bytes 688136 | tf_op jit(solution)/shard_map/ppermute | solution.py:1120
  16.9 15.2 %collective-permute-start.1 = (bf16[128,896]{1,0:T(8,128)(2,1)S(1)}, bf16[128,896]{1,0:T(8,128)(2,1)}, u32[]{:S(2)}, u32[]{:S(2)}) collective-permute-start(bf16[128,896]{1,0:T(8,128)(2,1)S(1)} %fusion.1.refs_0_), channel_id=1, source_target_pairs={{0,8},{4,12},{8,16},{12,20},{16,24},{20,28},{24,0},{28,4},{1,9},{5... | collective-permute-start | bytes 688136 | tf_op jit(solution)/shard_map/ppermute | solution.py:1120
  17.7 10.8 %collective-permute-start.18 = (bf16[128,256]{1,0:T(8,128)(2,1)S(1)}, bf16[128,256]{1,0:T(8,128)(2,1)S(1)}, u32[]{:S(2)}, u32[]{:S(2)}) collective-permute-start(bf16[128,256]{1,0:T(8,128)(2,1)S(1)} %bitcast.46), channel_id=1, source_target_pairs={{0,2},{1,3},{2,0},{3,1},{4,6},{5,7},{6,4},{7,5},{8,10},{9,11},{10,... | collective-permute-start | bytes 196616 | tf_op jit(solution)/shard_map/ppermute | solution.py:1108
  32.2 390.9 %reduce-scatter.2.cloned.1.call-start = ((), (), s32[]{:S(2)}) async-start(), calls=%async_computation.2 | async-start | bytes 7077888 | tf_op jit(solution)/shard_map/reduce_scatter | solution.py:1244
  32.2 7.2 %collective-permute-start.4 = (bf16[128,896]{1,0:T(8,128)(2,1)S(1)}, bf16[128,896]{1,0:T(8,128)(2,1)S(1)}, u32[]{:S(2)}, u32[]{:S(2)}) collective-permute-start(bf16[128,896]{1,0:T(8,128)(2,1)S(1)} %fusion.1.refs_0_), channel_id=1, source_target_pairs={{0,4},{4,0},{8,12},{12,8},{16,20},{20,16},{24,28},{28,24},{1,5},{5... | collective-permute-start | bytes 688136 | tf_op jit(solution)/shard_map/ppermute | solution.py:1116
  33.8 45.0 %collective-permute-start = (bf16[640,1024]{1,0:T(8,128)(2,1)S(1)}, bf16[640,1024]{1,0:T(8,128)(2,1)}, u32[]{:S(2)}, u32[]{:S(2)}) collective-permute-start(bf16[640,1024]{1,0:T(8,128)(2,1)S(1)} %copy-done), channel_id=1, source_target_pairs={{0,1},{1,0},{2,3},{3,2},{4,5},{5,4},{6,7},{7,6},{8,9},{9,8},{10,11... | collective-permute-start | bytes 3932168 | tf_op jit(solution)/shard_map/ppermute | solution.py:1104
  33.8 42.4 %collective-permute-start.9 = (bf16[320,1024]{1,0:T(8,128)(2,1)}, bf16[320,1024]{1,0:T(8,128)(2,1)}, u32[]{:S(2)}, u32[]{:S(2)}) collective-permute-start(bf16[320,1024]{1,0:T(8,128)(2,1)} %get-tuple-element.221), channel_id=1, source_target_pairs={{0,2},{1,3},{2,0},{3,1},{4,6},{5,7},{6,4},{7,5},{8,10},{9,11},{10,... | collective-permute-start | bytes 1966088 | tf_op jit(solution)/shard_map/ppermute | solution.py:1108
  34.4 13.2 %collective-permute-start.7 = (bf16[128,896]{1,0:T(8,128)(2,1)}, bf16[128,896]{1,0:T(8,128)(2,1)}, u32[]{:S(2)}, u32[]{:S(2)}) collective-permute-start(bf16[128,896]{1,0:T(8,128)(2,1)} %collective-permute-done.3.refs_3_), channel_id=1, source_target_pairs={{0,4},{4,0},{8,12},{12,8},{16,20},{20,16},{24,28},{28,24},{1,5},{5... | collective-permute-start | bytes 688136 | tf_op jit(solution)/shard_map/ppermute | solution.py:1116
  34.9 19.6 %collective-permute-start.6 = (bf16[128,896]{1,0:T(8,128)(2,1)}, bf16[128,896]{1,0:T(8,128)(2,1)}, u32[]{:S(2)}, u32[]{:S(2)}) collective-permute-start(bf16[128,896]{1,0:T(8,128)(2,1)} %collective-permute-done.2.refs_2_), channel_id=1, source_target_pairs={{0,4},{4,0},{8,12},{12,8},{16,20},{20,16},{24,28},{28,24},{1,5},{5... | collective-permute-start | bytes 688136 | tf_op jit(solution)/shard_map/ppermute | solution.py:1116
  39.4 20.7 %collective-permute-start.5 = (bf16[128,896]{1,0:T(8,128)(2,1)}, bf16[128,896]{1,0:T(8,128)(2,1)S(1)}, u32[]{:S(2)}, u32[]{:S(2)}) collective-permute-start(bf16[128,896]{1,0:T(8,128)(2,1)} %collective-permute-done.1.refs_1_), channel_id=1, source_target_pairs={{0,4},{4,0},{8,12},{12,8},{16,20},{20,16},{24,28},{28,24},{1,5},{5... | collective-permute-start | bytes 688136 | tf_op jit(solution)/shard_map/ppermute | solution.py:1116
  60.1 46.3 %collective-permute-start.21 = (bf16[128,1024]{1,0:T(8,128)(2,1)S(1)}, bf16[128,1024]{1,0:T(8,128)(2,1)}, u32[]{:S(2)}, u32[]{:S(2)}) collective-permute-start(bf16[128,1024]{1,0:T(8,128)(2,1)S(1)} %bitcast.39), channel_id=1, source_target_pairs={{0,16},{4,20},{8,24},{12,28},{16,0},{20,4},{24,8},{28,12},{1,17},{... | collective-permute-start | bytes 786440 | tf_op jit(solution)/shard_map/ppermute | solution.py:1120
  67.9 38.5 %collective-permute-start.20 = (bf16[128,1024]{1,0:T(8,128)(2,1)S(1)}, bf16[128,1024]{1,0:T(8,128)(2,1)}, u32[]{:S(2)}, u32[]{:S(2)}) collective-permute-start(bf16[128,1024]{1,0:T(8,128)(2,1)S(1)} %bitcast.40), channel_id=1, source_target_pairs={{0,24},{4,28},{8,0},{12,4},{16,8},{20,12},{24,16},{28,20},{1,25},{... | collective-permute-start | bytes 786440 | tf_op jit(solution)/shard_map/ppermute | solution.py:1120
  68.2 38.2 %collective-permute-start.19 = (bf16[128,1024]{1,0:T(8,128)(2,1)S(1)}, bf16[128,1024]{1,0:T(8,128)(2,1)}, u32[]{:S(2)}, u32[]{:S(2)}) collective-permute-start(bf16[128,1024]{1,0:T(8,128)(2,1)S(1)} %bitcast.41), channel_id=1, source_target_pairs={{0,8},{4,12},{8,16},{12,20},{16,24},{20,28},{24,0},{28,4},{1,9},{5... | collective-permute-start | bytes 786440 | tf_op jit(solution)/shard_map/ppermute | solution.py:1120
  78.2 8.1 %collective-permute-start.10 = (bf16[640,1024]{1,0:T(8,128)(2,1)}, bf16[640,1024]{1,0:T(8,128)(2,1)}, u32[]{:S(2)}, u32[]{:S(2)}) collective-permute-start(bf16[640,1024]{1,0:T(8,128)(2,1)} %constant_dynamic-update-slice_fusion.x0_ref.refs_9_), channel_id=1, source_target_pairs={{0,1},{1,0},{2,3},{3,2},{4,5},{5,4},{6,7},{7,6},{8,9},{9,8},{10,11... | collective-permute-start | bytes 3932168 | tf_op jit(solution)/shard_map/ppermute | solution.py:1104
  78.8 31.2 %collective-permute-start.14 = (bf16[640,1024]{1,0:T(8,128)(2,1)S(1)}, bf16[640,1024]{1,0:T(8,128)(2,1)S(1)}, u32[]{:S(2)}, u32[]{:S(2)}) collective-permute-start(bf16[640,1024]{1,0:T(8,128)(2,1)S(1)} %convert_element_type.94.refs_11_.refs_5_), channel_id=1, source_target_pairs={{0,2},{1,3},{2,0},{3,1},{4,6},{5,7},{6,4},{7,5},{8,10},{9,11},{10,... | collective-permute-start | bytes 3932168 | tf_op jit(solution)/shard_map/ppermute | solution.py:1108
  110.0 24.9 %collective-permute-start.22 = (bf16[128,1024]{1,0:T(8,128)(2,1)S(1)}, bf16[128,1024]{1,0:T(8,128)(2,1)S(1)}, u32[]{:S(2)}, u32[]{:S(2)}) collective-permute-start(bf16[128,1024]{1,0:T(8,128)(2,1)S(1)} %bitcast.42), channel_id=1, source_target_pairs={{0,4},{4,0},{8,12},{12,8},{16,20},{20,16},{24,28},{28,24},{1,5},{5... | collective-permute-start | bytes 786440 | tf_op jit(solution)/shard_map/ppermute | solution.py:1116
  111.5 23.4 %collective-permute-start.23 = (bf16[128,1024]{1,0:T(8,128)(2,1)}, bf16[128,1024]{1,0:T(8,128)(2,1)S(1)}, u32[]{:S(2)}, u32[]{:S(2)}) collective-permute-start(bf16[128,1024]{1,0:T(8,128)(2,1)} %collective-permute-done.19.refs_1_), channel_id=1, source_target_pairs={{0,4},{4,0},{8,12},{12,8},{16,20},{20,16},{24,28},{28,24},{1,5},{5... | collective-permute-start | bytes 786440 | tf_op jit(solution)/shard_map/ppermute | solution.py:1116
  112.0 26.1 %collective-permute-start.24 = (bf16[128,1024]{1,0:T(8,128)(2,1)}, bf16[128,1024]{1,0:T(8,128)(2,1)S(1)}, u32[]{:S(2)}, u32[]{:S(2)}) collective-permute-start(bf16[128,1024]{1,0:T(8,128)(2,1)} %collective-permute-done.20.refs_2_), channel_id=1, source_target_pairs={{0,4},{4,0},{8,12},{12,8},{16,20},{20,16},{24,28},{28,24},{1,5},{5... | collective-permute-start | bytes 786440 | tf_op jit(solution)/shard_map/ppermute | solution.py:1116
  113.6 29.8 %collective-permute-start.25 = (bf16[128,1024]{1,0:T(8,128)(2,1)}, bf16[128,1024]{1,0:T(8,128)(2,1)S(1)}, u32[]{:S(2)}, u32[]{:S(2)}) collective-permute-start(bf16[128,1024]{1,0:T(8,128)(2,1)} %collective-permute-done.21.refs_3_), channel_id=1, source_target_pairs={{0,4},{4,0},{8,12},{12,8},{16,20},{20,16},{24,28},{28,24},{1,5},{5... | collective-permute-start | bytes 786440 | tf_op jit(solution)/shard_map/ppermute | solution.py:1116
  114.1 36.8 %collective-permute-start.15 = (bf16[2,640,256]{2,1,0:T(8,128)(2,1)}, bf16[2,640,256]{2,1,0:T(8,128)(2,1)}, u32[]{:S(2)}, u32[]{:S(2)}) collective-permute-start(bf16[2,640,256]{2,1,0:T(8,128)(2,1)} %get-tuple-element.114.refs_0_.refs_4_.a0), channel_id=1, source_target_pairs={{0,2},{1,3},{2,0},{3,1},{4,6},{5,7},{6,4},{7,5},{8,10},{9,11},{10,... | collective-permute-start | bytes 1966088 | tf_op jit(solution)/shard_map/ppermute | solution.py:1108
  134.9 20.2 %collective-permute-start.17 = (bf16[640,1024]{1,0:T(8,128)(2,1)S(1)}, bf16[640,1024]{1,0:T(8,128)(2,1)S(1)}, u32[]{:S(2)}, u32[]{:S(2)}) collective-permute-start(bf16[640,1024]{1,0:T(8,128)(2,1)S(1)} %collective-permute-done.14.refs_11_.refs_3_), channel_id=1, source_target_pairs={{0,1},{1,0},{2,3},{3,2},{4,5},{5,4},{6,7},{7,6},{8,9},{9,8},{10,11... | collective-permute-start | bytes 3932168 | tf_op jit(solution)/shard_map/ppermute | solution.py:1104
  151.0 37.2 %collective-permute-start.12 = (bf16[2,640,256]{2,1,0:T(8,128)(2,1)}, bf16[2,640,256]{2,1,0:T(8,128)(2,1)}, u32[]{:S(2)}, u32[]{:S(2)}) collective-permute-start(bf16[2,640,256]{2,1,0:T(8,128)(2,1)} %get-tuple-element.112.refs_0_.refs_4_.refs_5_), channel_id=1, source_target_pairs={{0,2},{1,3},{2,0},{3,1},{4,6},{5,7},{6,4},{7,5},{8,10},{9,11},{10,... | collective-permute-start | bytes 1966088 | tf_op jit(solution)/shard_map/ppermute | solution.py:1108
  188.4 6.4 %collective-permute-start.28 = (bf16[640,1024]{1,0:T(8,128)(2,1)S(1)}, bf16[640,1024]{1,0:T(8,128)(2,1)S(1)}, u32[]{:S(2)}, u32[]{:S(2)}) collective-permute-start(bf16[640,1024]{1,0:T(8,128)(2,1)S(1)} %copy-done.6), channel_id=1, source_target_pairs={{0,1},{1,0},{2,3},{3,2},{4,5},{5,4},{6,7},{7,6},{8,9},{9,8},{10,11... | collective-permute-start | bytes 3932168 | tf_op jit(solution)/shard_map/ppermute | solution.py:1104
  188.8 6.0 %collective-permute-start.11 = (bf16[2,640,256]{2,1,0:T(8,128)(2,1)}, bf16[2,640,256]{2,1,0:T(8,128)(2,1)}, u32[]{:S(2)}, u32[]{:S(2)}) collective-permute-start(bf16[2,640,256]{2,1,0:T(8,128)(2,1)} %get-tuple-element.114.refs_0_.refs_4_.a0), channel_id=1, source_target_pairs={{0,1},{1,0},{2,3},{3,2},{4,5},{5,4},{6,7},{7,6},{8,9},{9,8},{10,11... | collective-permute-start | bytes 1966088 | tf_op jit(solution)/shard_map/ppermute | solution.py:1104
  188.9 6.5 %collective-permute-start.27 = (bf16[2,640,256]{2,1,0:T(8,128)(2,1)}, bf16[2,640,256]{2,1,0:T(8,128)(2,1)}, u32[]{:S(2)}, u32[]{:S(2)}) collective-permute-start(bf16[2,640,256]{2,1,0:T(8,128)(2,1)} %collective-permute-done.12.refs_2_.refs_6_.a2), channel_id=1, source_target_pairs={{0,1},{1,0},{2,3},{3,2},{4,5},{5,4},{6,7},{7,6},{8,9},{9,8},{10,11... | collective-permute-start | bytes 1966088 | tf_op jit(solution)/shard_map/ppermute | solution.py:1104
  189.3 79.9 %collective-permute-start.31 = (bf16[640,1024]{1,0:T(8,128)(2,1)}, bf16[640,1024]{1,0:T(8,128)(2,1)}, u32[]{:S(2)}, u32[]{:S(2)}) collective-permute-start(bf16[640,1024]{1,0:T(8,128)(2,1)} %get-tuple-element.138), channel_id=1, source_target_pairs={{0,1},{1,0},{2,3},{3,2},{4,5},{5,4},{6,7},{7,6},{8,9},{9,8},{10,11... | collective-permute-start | bytes 3932168 | tf_op jit(solution)/shard_map/ppermute | solution.py:1104
  193.9 33.7 %collective-permute-start.32 = (bf16[640,1024]{1,0:T(8,128)(2,1)S(1)}, bf16[640,1024]{1,0:T(8,128)(2,1)}, u32[]{:S(2)}, u32[]{:S(2)}) collective-permute-start(bf16[640,1024]{1,0:T(8,128)(2,1)S(1)} %add_convert_fusion.1), channel_id=1, source_target_pairs={{0,2},{1,3},{2,0},{3,1},{4,6},{5,7},{6,4},{7,5},{8,10},{9,11},{10,... | collective-permute-start | bytes 3932168 | tf_op jit(solution)/shard_map/ppermute | solution.py:1108
  227.6 25.5 %collective-permute-start.33 = (bf16[640,1024]{1,0:T(8,128)(2,1)}, bf16[640,1024]{1,0:T(8,128)(2,1)S(1)}, u32[]{:S(2)}, u32[]{:S(2)}) collective-permute-start(bf16[640,1024]{1,0:T(8,128)(2,1)} %get-tuple-element.148), channel_id=1, source_target_pairs={{0,1},{1,0},{2,3},{3,2},{4,5},{5,4},{6,7},{7,6},{8,9},{9,8},{10,11... | collective-permute-start | bytes 3932168 | tf_op jit(solution)/shard_map/ppermute | solution.py:1104
  266.9 17.4 %collective-permute-start.38 = (bf16[1024,512]{1,0:T(8,128)(2,1)}, bf16[1024,512]{1,0:T(8,128)(2,1)}, u32[]{:S(2)}, u32[]{:S(2)}) collective-permute-start(bf16[1024,512]{1,0:T(8,128)(2,1)} %get-tuple-element.156), channel_id=1, source_target_pairs={{0,1},{1,0},{2,3},{3,2},{4,5},{5,4},{6,7},{7,6},{8,9},{9,8},{10,11... | collective-permute-start | bytes 3145736 | tf_op jit(solution)/shard_map/ppermute | solution.py:1104
  267.0 10.8 %collective-permute-start.34 = (bf16[640,256]{1,0:T(8,128)(2,1)}, bf16[640,256]{1,0:T(8,128)(2,1)S(1)}, u32[]{:S(2)}, u32[]{:S(2)}) collective-permute-start(bf16[640,256]{1,0:T(8,128)(2,1)} %get-tuple-element.149), channel_id=1, source_target_pairs={{0,2},{1,3},{2,0},{3,1},{4,6},{5,7},{6,4},{7,5},{8,10},{9,11},{10,... | collective-permute-start | bytes 983048 | tf_op jit(solution)/shard_map/ppermute | solution.py:1108
  268.2 15.6 %collective-permute-start.35 = (bf16[640,256]{1,0:T(8,128)(2,1)}, bf16[640,256]{1,0:T(8,128)(2,1)}, u32[]{:S(2)}, u32[]{:S(2)}) collective-permute-start(bf16[640,256]{1,0:T(8,128)(2,1)} %get-tuple-element.150), channel_id=1, source_target_pairs={{0,3},{1,2},{2,1},{3,0},{4,7},{5,6},{6,5},{7,4},{8,11},{9,10},{10,... | collective-permute-start | bytes 983048 | tf_op jit(solution)/shard_map/ppermute | solution.py:1112
  268.8 19.3 %collective-permute-start.37 = (bf16[640,256]{1,0:T(8,128)(2,1)S(1)}, bf16[640,256]{1,0:T(8,128)(2,1)}, u32[]{:S(2)}, u32[]{:S(2)}) collective-permute-start(bf16[640,256]{1,0:T(8,128)(2,1)S(1)} %copy-done.36), channel_id=1, source_target_pairs={{0,1},{1,0},{2,3},{3,2},{4,5},{5,4},{6,7},{7,6},{8,9},{9,8},{10,11... | collective-permute-start | bytes 983048 | tf_op jit(solution)/shard_map/ppermute | solution.py:1104
  283.8 48.2 %collective-permute-start.36 = (bf16[640,1024]{1,0:T(8,128)(2,1)S(1)}, bf16[640,1024]{1,0:T(8,128)(2,1)S(1)}, u32[]{:S(2)}, u32[]{:S(2)}) collective-permute-start(bf16[640,1024]{1,0:T(8,128)(2,1)S(1)} %add_convert_fusion), channel_id=1, source_target_pairs={{0,2},{1,3},{2,0},{3,1},{4,6},{5,7},{6,4},{7,5},{8,10},{9,11},{10,... | collective-permute-start | bytes 3932168 | tf_op jit(solution)/shard_map/ppermute | solution.py:1108
  288.0 44.0 %collective-permute-start.39 = (bf16[4,128,512]{2,1,0:T(8,128)(2,1)}, bf16[4,128,512]{2,1,0:T(8,128)(2,1)S(1)}, u32[]{:S(2)}, u32[]{:S(2)}) collective-permute-start(bf16[4,128,512]{2,1,0:T(8,128)(2,1)} %get-tuple-element.158), channel_id=1, source_target_pairs={{0,4},{4,0},{8,12},{12,8},{16,20},{20,16},{24,28},{28,24},{1,5},{5... | collective-permute-start | bytes 1572872 | tf_op jit(solution)/shard_map/ppermute | solution.py:1116
  349.6 5.2 %collective-permute-start.40 = (bf16[640,1024]{1,0:T(8,128)(2,1)}, bf16[640,1024]{1,0:T(8,128)(2,1)S(1)}, u32[]{:S(2)}, u32[]{:S(2)}) collective-permute-start(bf16[640,1024]{1,0:T(8,128)(2,1)} %project_back.4), channel_id=1, source_target_pairs={{0,1},{1,0},{2,3},{3,2},{4,5},{5,4},{6,7},{7,6},{8,9},{9,8},{10,11... | collective-permute-start | bytes 3932168 | tf_op jit(solution)/shard_map/ppermute | solution.py:1104
  350.3 31.1 %collective-permute-start.44 = (bf16[4,128,896]{2,1,0:T(8,128)(2,1)}, bf16[4,128,896]{2,1,0:T(8,128)(2,1)}, u32[]{:S(2)}, u32[]{:S(2)}) collective-permute-start(bf16[4,128,896]{2,1,0:T(8,128)(2,1)} %get-tuple-element.181), channel_id=1, source_target_pairs={{0,4},{4,0},{8,12},{12,8},{16,20},{20,16},{24,28},{28,24},{1,5},{5... | collective-permute-start | bytes 2752520 | tf_op jit(solution)/shard_map/ppermute | solution.py:1116
  352.0 33.4 %collective-permute-start.30 = (bf16[640,1024]{1,0:T(8,128)(2,1)}, bf16[640,1024]{1,0:T(8,128)(2,1)}, u32[]{:S(2)}, u32[]{:S(2)}) collective-permute-start(bf16[640,1024]{1,0:T(8,128)(2,1)} %get-tuple-element.136), channel_id=1, source_target_pairs={{0,1},{1,0},{2,3},{3,2},{4,5},{5,4},{6,7},{7,6},{8,9},{9,8},{10,11... | collective-permute-start | bytes 3932168 | tf_op jit(solution)/shard_map/ppermute | solution.py:1104
  352.0 17.7 %collective-permute-start.41 = (bf16[128,512]{1,0:T(8,128)(2,1)S(1)}, bf16[128,512]{1,0:T(8,128)(2,1)S(1)}, u32[]{:S(2)}, u32[]{:S(2)}) collective-permute-start(bf16[128,512]{1,0:T(8,128)(2,1)S(1)} %copy-done.40), channel_id=1, source_target_pairs={{0,16},{4,20},{8,24},{12,28},{16,0},{20,4},{24,8},{28,12},{1,17},{... | collective-permute-start | bytes 393224 | tf_op jit(solution)/shard_map/ppermute | solution.py:1120
  353.3 16.3 %collective-permute-start.43 = (bf16[128,512]{1,0:T(8,128)(2,1)S(1)}, bf16[128,512]{1,0:T(8,128)(2,1)S(1)}, u32[]{:S(2)}, u32[]{:S(2)}) collective-permute-start(bf16[128,512]{1,0:T(8,128)(2,1)S(1)} %copy-done.39), channel_id=1, source_target_pairs={{0,24},{4,28},{8,0},{12,4},{16,8},{20,12},{24,16},{28,20},{1,25},{... | collective-permute-start | bytes 393224 | tf_op jit(solution)/shard_map/ppermute | solution.py:1120
  354.8 14.9 %collective-permute-start.42 = (bf16[128,512]{1,0:T(8,128)(2,1)S(1)}, bf16[128,512]{1,0:T(8,128)(2,1)S(1)}, u32[]{:S(2)}, u32[]{:S(2)}) collective-permute-start(bf16[128,512]{1,0:T(8,128)(2,1)S(1)} %copy-done.38), channel_id=1, source_target_pairs={{0,8},{4,12},{8,16},{12,20},{16,24},{20,28},{24,0},{28,4},{1,9},{5... | collective-permute-start | bytes 393224 | tf_op jit(solution)/shard_map/ppermute | solution.py:1120
  369.7 31.0 %collective-permute-start.46 = (bf16[640,1024]{1,0:T(8,128)(2,1)}, bf16[640,1024]{1,0:T(8,128)(2,1)}, u32[]{:S(2)}, u32[]{:S(2)}) collective-permute-start(bf16[640,1024]{1,0:T(8,128)(2,1)} %project_back.5), channel_id=1, source_target_pairs={{0,2},{1,3},{2,0},{3,1},{4,6},{5,7},{6,4},{7,5},{8,10},{9,11},{10,... | collective-permute-start | bytes 3932168 | tf_op jit(solution)/shard_map/ppermute | solution.py:1108
  381.5 19.2 %collective-permute-start.45 = (bf16[640,1024]{1,0:T(8,128)(2,1)}, bf16[640,1024]{1,0:T(8,128)(2,1)}, u32[]{:S(2)}, u32[]{:S(2)}) collective-permute-start(bf16[640,1024]{1,0:T(8,128)(2,1)} %project_back.6), channel_id=1, source_target_pairs={{0,1},{1,0},{2,3},{3,2},{4,5},{5,4},{6,7},{7,6},{8,9},{9,8},{10,11... | collective-permute-start | bytes 3932168 | tf_op jit(solution)/shard_map/ppermute | solution.py:1104
  392.0 17.3 %collective-permute-start.47 = (bf16[128,896]{1,0:T(8,128)(2,1)}, bf16[128,896]{1,0:T(8,128)(2,1)S(1)}, u32[]{:S(2)}, u32[]{:S(2)}) collective-permute-start(bf16[128,896]{1,0:T(8,128)(2,1)} %get-tuple-element.196), channel_id=1, source_target_pairs={{0,16},{4,20},{8,24},{12,28},{16,0},{20,4},{24,8},{28,12},{1,17},{... | collective-permute-start | bytes 688136 | tf_op jit(solution)/shard_map/ppermute | solution.py:1120
  397.6 17.7 %collective-permute-start.49 = (bf16[128,896]{1,0:T(8,128)(2,1)}, bf16[128,896]{1,0:T(8,128)(2,1)S(1)}, u32[]{:S(2)}, u32[]{:S(2)}) collective-permute-start(bf16[128,896]{1,0:T(8,128)(2,1)} %get-tuple-element.197), channel_id=1, source_target_pairs={{0,24},{4,28},{8,0},{12,4},{16,8},{20,12},{24,16},{28,20},{1,25},{... | collective-permute-start | bytes 688136 | tf_op jit(solution)/shard_map/ppermute | solution.py:1120
  397.7 17.5 %collective-permute-start.48 = (bf16[128,896]{1,0:T(8,128)(2,1)}, bf16[128,896]{1,0:T(8,128)(2,1)S(1)}, u32[]{:S(2)}, u32[]{:S(2)}) collective-permute-start(bf16[128,896]{1,0:T(8,128)(2,1)} %get-tuple-element.192), channel_id=1, source_target_pairs={{0,8},{4,12},{8,16},{12,20},{16,24},{20,28},{24,0},{28,4},{1,9},{5... | collective-permute-start | bytes 688136 | tf_op jit(solution)/shard_map/ppermute | solution.py:1120
  (48 other events, 438.8 us)
Sparse Core Ops, SparseCore 0:
  32.3 116.6 all-gather.1
  269.4 124.0 reduce-scatter.1
